TPU v7x, 32 devices: a whole 2x2x4 slice. The times are simulated.
32 devices in a mesh: group: 2 (over y), tm: 4 (over z), height: 2 (over x), width: 2 (over core).
Axes of the slice: x: 2, y: 2, z: 4, core: 2. Of those that a mesh axis runs over, the one named last changes fastest.
Arguments:
- queries: bfloat16 [8, 16, 32, 1120], P(('group', 'tm'), 'height', 'width'), parts along dimension 0, may hold values from -5 to 5
- attn_keys: bfloat16 [8, 16, 32, 1120], P(('group', 'tm'), 'height', 'width'), parts along dimension 0, may hold values from -40 to 40
- attn_values: bfloat16 [8, 16, 32, 1120], P(('group', 'tm'), 'height', 'width'), parts along dimension 0, may hold values from -7 to 7
- attn_cotangent: bfloat16 [8, 16, 32, 1120], P(('group', 'tm'), 'height', 'width'), parts along dimension 0, may hold values from -7 to 7
- clip_ids: int32 [8], P('group'), parts along dimension 0, may hold values from 0 to 1, as said below
- hidden_pre: bfloat16 [8, 16, 32, 5632], P(('group', 'tm'), 'height', 'width'), parts along dimension 0, may hold values from -6 to 6
- conv_weight: float32 [9, 5632], replicated, may hold values from -2 to 2
Outputs:
- query_grad: bfloat16 [8, 16, 32, 1120], P(('group', 'tm'), 'height', 'width'), parts along dimension 0
- key_grad: bfloat16 [8, 16, 32, 1120], P(('group', 'tm'), 'height', 'width'), parts along dimension 0
- value_gradient: bfloat16 [8, 16, 32, 1120], P(('group', 'tm'), 'height', 'width'), parts along dimension 0
- hidden_grad: bfloat16 [8, 16, 32, 5632], P(('group', 'tm'), 'height', 'width'), parts along dimension 0
There are 2 independent parts, one for each index of `group`. A program takes and returns all parts, laid end to end along the dimension named above; an argument that names none is the same for every part. Nothing has to cross between parts.
Inputs may be any that keep to these rules, and one draw needn't show every extreme that they name: clip_ids never falls; the 4 frames form two clips, 0 then 1, each of 1 to 3 frames.
All inputs are finite; a program needn't handle non-finite values.
Results may differ from a plain program's by a relative error of at most 0.001.
Values may be sent and summed in bfloat16 or wider, within the bound.
No kernel may reach another device: no remote copies, remote signals or barrier semaphores. Data moves between devices by JAX's collectives and lax.ppermute only.
A program may use at most 64 MiB of HBM per device.

v0:
```python
from functools import reduce

import jax
import jax.numpy as jnp
from jax import lax
from jax.sharding import PartitionSpec as P

HEAD_DIM = 112
HEADS = 10


EPSILON = 1e-06
TOP_PRECISION = lax.Precision.HIGHEST


def entering(value, axis, join, neutral, backward):
    count, mine = (lax.axis_size(axis), lax.axis_index(axis))
    pieces = jax.tree.map(lambda part: lax.all_gather(part, axis), value)
    if backward:
        pieces = jax.tree.map(lambda part: part[::-1], pieces)
        mine = count - 1 - mine
    so_far = jax.tree.map(
        lambda part, zero: jnp.full_like(part, 0) + jnp.asarray(zero, part.dtype), value, neutral
    )

    def turn(position, so_far):
        longer = join(so_far, jax.tree.map(lambda part: part[position], pieces))
        return jax.tree.map(lambda new, old: jnp.where(position < mine, new, old), longer, so_far)

    return lax.fori_loop(0, count - 1, turn, so_far)


def padded(block, sides, width):
    for axis, dim in sides:
        count = lax.axis_size(axis)
        forward = [(i, i + 1) for i in range(count - 1)]
        backward = [(target, source) for source, target in forward]
        low = lax.ppermute(
            lax.slice_in_dim(block, block.shape[dim] - width, None, axis=dim), axis, forward
        )
        high = lax.ppermute(lax.slice_in_dim(block, 0, width, axis=dim), axis, backward)
        block = jnp.concatenate([low, block, high], axis=dim)
    return block


def carry_on(earlier, later):
    keeping = 1.0 - later[0]
    return (
        jnp.maximum(earlier[0], later[0]),
        later[1] + keeping * earlier[1],
        later[2] + keeping * earlier[2],
    )


def clip_flags(clip_ids):
    frame = lax.axis_index("tm")
    frame_count = lax.axis_size("tm")
    current = lax.dynamic_index_in_dim(clip_ids, frame, 0, keepdims=False)
    before = lax.dynamic_index_in_dim(clip_ids, jnp.maximum(frame - 1, 0), 0, keepdims=False)
    after = lax.dynamic_index_in_dim(
        clip_ids, jnp.minimum(frame + 1, frame_count - 1), 0, keepdims=False
    )
    starts = jnp.where((frame == 0) | (current != before), 1.0, 0.0).astype(jnp.float32)
    ends = jnp.where((frame == frame_count - 1) | (current != after), 1.0, 0.0).astype(jnp.float32)
    return (starts, ends)


def glu_grad(conv_out, split_at):
    value_part = conv_out[..., :split_at]
    gate_part = conv_out[..., split_at:]
    squash = jax.nn.sigmoid(gate_part)
    glu = value_part * gate_part * squash
    value_gradient = glu * gate_part * squash
    gate_grad = glu * value_part * squash * (1.0 + gate_part * (1.0 - squash))
    return jnp.concatenate([value_gradient, gate_grad], axis=-1)


def depthwise(source, weights, start, sign, height_out, width_out):
    terms = []
    for offset_row in (-1, 0, 1):
        for offset_col in (-1, 0, 1):
            tap_index = (offset_row + 1) * 3 + offset_col + 1
            row_start = start + sign * offset_row
            col_start = start + sign * offset_col
            window = source[
                row_start : row_start + height_out, col_start : col_start + width_out
            ].astype(jnp.float32)
            terms.append(weights[tap_index] * window)
    return reduce(lambda first, second: first + second, terms)


def per_device(queries, attn_keys, attn_values, attn_cotangent, clip_ids, hidden_pre, conv_weight):
    token_count = queries.shape[1] * queries.shape[2]
    flat_width = HEADS * HEAD_DIM
    starts, ends = clip_flags(clip_ids)
    zero_flag = jnp.zeros((), jnp.float32)
    feature_keys = jnp.maximum(attn_keys, 0).reshape(token_count, HEADS, HEAD_DIM)
    value_row_block = attn_values.reshape(token_count, HEADS, HEAD_DIM)
    local_kv = jnp.einsum(
        "jrf,jrx->rfx", feature_keys, value_row_block, preferred_element_type=jnp.float32
    ).reshape(flat_width, HEAD_DIM)
    local_norm = jnp.sum(feature_keys.astype(jnp.float32), axis=0).reshape(flat_width)
    share_kv, share_norm = (
        lax.psum_scatter(local_kv, ("height", "width"), scatter_dimension=0, tiled=True),
        lax.psum_scatter(local_norm, ("height", "width"), scatter_dimension=0, tiled=True),
    )
    earlier = entering(
        (starts, share_kv, share_norm),
        "tm",
        carry_on,
        (zero_flag, jnp.zeros_like(share_kv), jnp.zeros_like(share_norm)),
        False,
    )
    part_kv = share_kv + (1.0 - starts) * earlier[1]
    part_norm = share_norm + (1.0 - starts) * earlier[2]
    state_key_value, state_norm = (
        lax.all_gather(part_kv, ("height", "width"), axis=0, tiled=True),
        lax.all_gather(part_norm, ("height", "width"), axis=0, tiled=True),
    )
    state_key_value = state_key_value.reshape(HEADS, HEAD_DIM, HEAD_DIM)
    state_norm = state_norm.reshape(HEADS, HEAD_DIM)
    feature_query = (
        jnp.maximum(queries, 0).reshape(token_count, HEADS, HEAD_DIM).astype(jnp.float32)
    )
    cotangent = attn_cotangent.reshape(token_count, HEADS, HEAD_DIM).astype(jnp.float32)
    ratio_numerator = jnp.einsum(
        "cob,obq->coq", feature_query, state_key_value, precision=TOP_PRECISION
    )
    denominator = (
        jnp.einsum("thk,hk->th", feature_query, state_norm, precision=TOP_PRECISION) + EPSILON
    )
    attended = ratio_numerator / denominator[..., None]
    scaled_gradient = cotangent / denominator[..., None]
    denominator_grad = -jnp.sum(cotangent * attended, axis=-1) / denominator
    query_feature_gradient = jnp.einsum(
        "dla,lja->dlj", scaled_gradient, state_key_value, precision=TOP_PRECISION
    )
    query_feature_gradient = query_feature_gradient + state_norm[None] * denominator_grad[..., None]
    query_grad = (
        jnp.where(feature_query > 0.0, query_feature_gradient, 0.0)
        .reshape(queries.shape)
        .astype(jnp.bfloat16)
    )
    gradient_key_value = jnp.einsum(
        "jrf,jrx->rfx", feature_query, scaled_gradient, precision=TOP_PRECISION
    ).reshape(flat_width, HEAD_DIM)
    grad_norm = jnp.einsum(
        "thk,th->hk", feature_query, denominator_grad, precision=TOP_PRECISION
    ).reshape(flat_width)
    share_grad_kv, share_grad_norm = (
        lax.psum_scatter(gradient_key_value, ("height", "width"), scatter_dimension=0, tiled=True),
        lax.psum_scatter(grad_norm, ("height", "width"), scatter_dimension=0, tiled=True),
    )
    later = entering(
        (ends, share_grad_kv, share_grad_norm),
        "tm",
        carry_on,
        (zero_flag, jnp.zeros_like(share_grad_kv), jnp.zeros_like(share_grad_norm)),
        True,
    )
    part_grad_kv = share_grad_kv + (1.0 - ends) * later[1]
    part_grad_norm = share_grad_norm + (1.0 - ends) * later[2]
    total_key_value, norm_total = (
        lax.all_gather(part_grad_kv, ("height", "width"), axis=0, tiled=True),
        lax.all_gather(part_grad_norm, ("height", "width"), axis=0, tiled=True),
    )
    total_key_value = total_key_value.reshape(HEADS, HEAD_DIM, HEAD_DIM)
    norm_total = norm_total.reshape(HEADS, HEAD_DIM)
    key_feat_grad = (
        jnp.einsum(
            "dla,lja->dlj",
            value_row_block.astype(jnp.float32),
            total_key_value,
            precision=TOP_PRECISION,
        )
        + norm_total[None]
    )
    key_grad = (
        jnp.where(feature_keys > 0, key_feat_grad, 0.0)
        .reshape(attn_keys.shape)
        .astype(jnp.bfloat16)
    )
    value_gradient = jnp.einsum(
        "cob,obq->coq", feature_keys.astype(jnp.float32), total_key_value, precision=TOP_PRECISION
    )
    value_gradient = value_gradient.reshape(attn_values.shape).astype(jnp.bfloat16)
    row_count = hidden_pre.shape[1]
    col_count = hidden_pre.shape[2]
    split_at = hidden_pre.shape[3] // 2
    widened = padded(hidden_pre, (("height", 1), ("width", 2)), 2)[0]
    conv_out = depthwise(widened, conv_weight, 1, 1, row_count + 2, col_count + 2)
    row_global = lax.axis_index("height") * row_count + jnp.arange(row_count + 2) - 1
    col_global = lax.axis_index("width") * col_count + jnp.arange(col_count + 2) - 1
    row_inside = (row_global >= 0) & (row_global < row_count * lax.axis_size("height"))
    col_inside = (col_global >= 0) & (col_global < col_count * lax.axis_size("width"))
    inside = (row_inside[:, None] & col_inside[None, :]).astype(jnp.float32)
    conv_grad = glu_grad(conv_out, split_at) * inside[:, :, None]
    hidden_grad = depthwise(conv_grad, conv_weight, 1, -1, row_count, col_count)
    hidden_grad = hidden_grad[None].astype(jnp.bfloat16)
    return (query_grad, key_grad, value_gradient, hidden_grad)


def solution(mesh):
    return jax.shard_map(
        per_device,
        mesh=mesh,
        in_specs=(
            P(("group", "tm"), "height", "width", None),
            P(("group", "tm"), "height", "width", None),
            P(("group", "tm"), "height", "width", None),
            P(("group", "tm"), "height", "width", None),
            P("group"),
            P(("group", "tm"), "height", "width", None),
            P(),
        ),
        out_specs=(
            P(("group", "tm"), "height", "width", None),
            P(("group", "tm"), "height", "width", None),
            P(("group", "tm"), "height", "width", None),
            P(("group", "tm"), "height", "width", None),
        ),
        check_vma=False,
    )
```

profile of v0, /device:TPU:0, one launch (start us, length us, event | category | flops | bytes accessed | tf_op | source)
XLA Modules:
  0.0 199.7 jit_solution(10173100332461614557)
XLA Ops:
  7.2 1.9 fusion.27
  9.1 5.7 %collective-permute-start = (bf16[1,2,16,5632]{3,2,1,0:T(8,128)(2,1)S(1)}, bf16[1,2,16,5632]{3,2,1,0:T(8,128)(2,1)}, u32[]{:S(2)}, u32[]{:S(2)}) collective-permute-start(bf16[1,2,16,5632]{3,2,1,0:T(8,128)(2,1)S(1)} %get-tuple-element.356), channel_id=1, source_target_pairs={{0,2},{1,3},{4,6},{5,7},{8,10},{9,11},{12,14},{13,15},{16,18},{17,... | collective-permute-start | bytes 1081352 | tf_op jit(solution)/shard_map/ppermute | solution.py:38
  14.8 1.4 collective-permute-start.1
  19.3 1.2 fusion.30
  21.8 8.0 %all-reduce.7 = f32[1120]{0:T(1024)S(1)} all-reduce(f32[1120]{0:T(1024)S(1)} %convert_reduce_fusion), channel_id=7, replica_groups=mesh['group'=2,'tm'=4,'height'=2,'width'=2] {'height','width'}, use_global_device_ids=true, to_apply=%region_2.3.clone | all-reduce | flops 1120 | bytes 8960
  36.7 1.5 constant_dynamic-update-slice_fusion.1
  39.2 1.2 fusion.26
  40.4 2.0 collective-permute-start.2
  42.4 1.3 collective-permute-start.3
  44.3 12.9 %all-reduce.11 = (f32[4]{0:T(128)}, f32[1120]{0:T(1024)S(1)}) all-reduce(f32[4]{0:T(128)S(1)} %dynamic-update-slice, f32[1120]{0:T(1024)S(1)} %dynamic-slice_dynamic-update-slice_fusion.1), channel_id=1, replica_groups=mesh['group'=2,'tm'=4,'height'=2,'width'=2] {'tm'}, use_global_device_ids=true, to_apply=%add | all-reduce | flops 1124 | bytes 8992
  57.9 2.4 %reshape.147 = bf16[128,10,112]{2,1,0:T(8,128)(2,1)} reshape(bf16[1,8,16,1120]{3,2,1,0:T(8,128)(2,1)} %broadcast_maximum_fusion.1) | data formatting | bytes 573440 | tf_op jit(solution)/shard_map/reshape | solution.py:123
  60.2 1.4 copy.36
  61.6 2.5 %reshape.156 = f32[128,10,112]{2,1,0:T(8,128)} reshape(bf16[1,8,16,1120]{3,2,1,0:T(8,128)(2,1)} %param.14) | data formatting | bytes 860160 | tf_op jit(solution)/shard_map/convert_element_type | solution.py:125
  64.1 2.3 %copy.39 = f32[128,10,112]{0,2,1:T(8,128)} copy(f32[128,10,112]{2,1,0:T(8,128)} %reshape.156) | data formatting | bytes 1146880 | tf_op jit(solution)/shard_map/convert_element_type | solution.py:125
  68.3 1.8 dynamic-update-slice.3
  70.8 2.4 %maximum_bitcast_fusion = bf16[12,20,5632]{2,1,0:T(8,128)(2,1)S(1)} fusion(bf16[1,12,2,5632]{3,2,1,0:T(2,128)(2,1)} %collective-permute-done.3, bf16[1,12,16,5632]{3,2,1,0:T(8,128)(2,1)S(1)} %constant_dynamic-update-slice_fusion, bf16[1,12,2,5632]{3,2,1,0:T(2,128)(2,1)} %collective-permute-done.2), kind=kLoop, calls=%fused_computation.10 | loop fusion | flops 8110080 | bytes 5406720 | tf_op jit(solution)/shard_map/squeeze | solution.py:190
  73.2 5.8 %multiply_add_fusion = f32[10,18,5632]{2,1,0:T(8,128)S(1)} fusion(bf16[12,20,5632]{2,1,0:T(8,128)(2,1)S(1)} %maximum_bitcast_fusion, f32[5632]{0:T(1024)S(1)} %get-tuple-element.317, f32[5632]{0:T(1024)S(1)} %get-tuple-element.318, f32[5632]{0:T(1024)S(1)} %get-tuple-element.311, f32[5632]{0:T(1024)S(1)} %get-tuple-element.312, ...), kind=kLoop, calls=%fused_computation.9 | loop fusion | flops 26357760 | bytes 22505472 | tf_op jit(solution)/shard_map/add | solution.py:89
  79.1 1.4 multiply_multiply_fusion
  80.5 3.0 %maximum_multiply_fusion = f32[10,18,5632]{2,1,0:T(8,128)} fusion(f32[10,18,2816]{2,1,0:T(8,128)S(1)} %get-tuple-element.352, f32[10,18,2816]{2,1,0:T(8,128)S(1)} %get-tuple-element.351, f32[10,18]{1,0:T(8,128)S(1)} %and_convert_fusion), kind=kLoop, calls=%fused_computation.8 | loop fusion | flops 2027520 | bytes 8110800 | tf_op jit(solution)/shard_map/mul | solution.py:197
  83.5 16.9 %all-gather = f32[1120,112]{1,0:T(8,128)S(1)} all-gather(f32[280,112]{1,0:T(8,128)} %reduce-scatter.7.cloned.1.call-done), channel_id=2, replica_groups=mesh['group'=2,'tm'=4,'height'=2,'width'=2] {'tm'}, dimensions={0}, use_global_device_ids=true | all-gather | bytes 627200 | tf_op jit(solution)/shard_map/all_gather | solution.py:18
  100.4 4.1 %while.32 = (s32[]{:T(128)}, f32[280,112]{1,0:T(8,128)S(1)}, f32[280]{0:T(512)S(1)}, s32[]{:T(128)}, f32[4,280,112]{2,1,0:T(8,128)S(1)}, /*index=5*/f32[4]{0:T(1...) while((s32[]{:T(128)}, f32[280,112]{1,0:T(8,128)S(1)}, f32[280]{0:T(512)S(1)}, ...), condition=%wide.region_4.5_spmd.clone, body=%wide.region_3.4_spmd.clone.sunk | while | flops 126565 | bytes 382083 | solution.py:30
  104.8 5.7 %all-reduce.2 = f32[1120]{0:T(1024)S(1)} all-reduce(f32[1120]{0:T(1024)S(1)} %add_dynamic-update-slice_fusion.1), channel_id=1, replica_groups=mesh['group'=2,'tm'=4,'height'=2,'width'=2] {'height','width'}, use_global_device_ids=true, to_apply=%add.2 | all-reduce | flops 1120 | bytes 8960
  110.9 1.6 fusion.22
  112.6 7.9 %all_gather.54 = f32[1120,112]{1,0:T(8,128)S(1)} all-gather(f32[280,112]{1,0:T(8,128)S(1)} %multiply_add_fusion.2), channel_id=1, replica_groups=mesh['group'=2,'tm'=4,'height'=2,'width'=2] {'height','width'}, dimensions={0}, use_global_device_ids=true | all-gather | bytes 627200 | tf_op jit(solution)/shard_map/all_gather | solution.py:117
  121.8 6.7 %all-reduce.9 = f32[1120]{0:T(1024)S(1)} all-reduce(f32[1120]{0:T(1024)S(1)} %reshape.154), channel_id=9, replica_groups=mesh['group'=2,'tm'=4,'height'=2,'width'=2] {'height','width'}, use_global_device_ids=true, to_apply=%region_7.8.clone | all-reduce | flops 1120 | bytes 8960
  128.6 14.8 %fusion.11 = bf16[1,8,16,5632]{3,2,1,0:T(8,128)(2,1)} fusion(f32[10,18,5632]{2,1,0:T(8,128)} %maximum_multiply_fusion, f32[5632]{0:T(1024)S(1)} %get-tuple-element.317, f32[5632]{0:T(1024)S(1)} %get-tuple-element.318, f32[5632]{0:T(1024)S(1)} %get-tuple-element.311, f32[5632]{0:T(1024)S(1)} %get-tuple-element.312, f32[5632]{0:T(1024)S(1)} %get-tuple-element.313, ...), kind=kLoop, calls=%fused_computation.33 | loop fusion | flops 12976128 | bytes 27596800 | tf_op jit(solution)/shard_map/convert_element_type | solution.py:199
  143.4 9.0 %all-reduce.10 = (f32[4]{0:T(128)S(1)}, f32[1120]{0:T(1024)S(1)}) all-reduce(f32[4]{0:T(128)S(1)} %copy-done.9, f32[1120]{0:T(1024)S(1)} %dynamic-slice_dynamic-update-slice_fusion), channel_id=1, replica_groups=mesh['group'=2,'tm'=4,'height'=2,'width'=2] {'tm'}, use_global_device_ids=true, to_apply=%add.3 | all-reduce | flops 1124 | bytes 8992
  154.0 1.1 convert_element_type.105
  155.1 15.5 %all-gather.2 = f32[1120,112]{1,0:T(8,128)S(1)} all-gather(f32[280,112]{1,0:T(8,128)} %reduce-scatter.9.cloned.1.call-done), channel_id=4, replica_groups=mesh['group'=2,'tm'=4,'height'=2,'width'=2] {'tm'}, dimensions={0}, use_global_device_ids=true | all-gather | bytes 627200 | tf_op jit(solution)/shard_map/all_gather | solution.py:18
  170.6 4.1 %while.33 = (s32[]{:T(128)}, f32[280,112]{1,0:T(8,128)S(1)}, f32[280]{0:T(512)S(1)}, s32[]{:T(128)}, f32[4,280,112]{2,1,0:T(8,128)S(1)}, /*index=5*/f32[4]{0:T(1...) while((s32[]{:T(128)}, f32[280,112]{1,0:T(8,128)S(1)}, f32[280]{0:T(512)S(1)}, ...), condition=%wide.region_9.10_spmd.clone, body=%wide.region_8.9_spmd.clone.sunk | while | flops 126565 | bytes 382083 | solution.py:30
  174.8 6.9 %all_gather.62 = f32[1120,112]{1,0:T(8,128)S(1)} all-gather(f32[280,112]{1,0:T(8,128)S(1)} %multiply_add_fusion.1), channel_id=1, replica_groups=mesh['group'=2,'tm'=4,'height'=2,'width'=2] {'height','width'}, dimensions={0}, use_global_device_ids=true | all-gather | bytes 627200 | tf_op jit(solution)/shard_map/all_gather | solution.py:164
  184.0 6.8 %all-reduce.5 = f32[1120]{0:T(1024)S(1)} all-reduce(f32[1120]{0:T(1024)S(1)} %add_dynamic-update-slice_fusion), channel_id=1, replica_groups=mesh['group'=2,'tm'=4,'height'=2,'width'=2] {'height','width'}, use_global_device_ids=true, to_apply=%add.5 | all-reduce | flops 1120 | bytes 8960
  (114 shorter events, 24.0 us)
Async XLA Ops:
  7.2 11.1 %copy-start.4 = (bf16[1,8,16,1120]{3,2,1,0:T(8,128)(2,1)S(1)}, bf16[1,8,16,1120]{3,2,1,0:T(8,128)(2,1)}, u32[]{:S(2)}) copy-start(bf16[1,8,16,1120]{3,2,1,0:T(8,128)(2,1)} %param.13) | copy-start | bytes 860164
  7.2 76.3 %reduce-scatter.7.cloned.1.call-start = ((), (), s32[]{:S(2)}) async-start(), calls=%async_computation.2 | async-start | bytes 716800
  9.1 11.5 %copy-start = (bf16[1,8,16,1120]{3,2,1,0:T(8,128)(2,1)S(1)}, bf16[1,8,16,1120]{3,2,1,0:T(8,128)(2,1)}, u32[]{:S(2)}) copy-start(bf16[1,8,16,1120]{3,2,1,0:T(8,128)(2,1)} %param.12) | copy-start | bytes 860164
  9.1 26.6 %collective-permute-start = (bf16[1,2,16,5632]{3,2,1,0:T(8,128)(2,1)S(1)}, bf16[1,2,16,5632]{3,2,1,0:T(8,128)(2,1)}, u32[]{:S(2)}, u32[]{:S(2)}) collective-permute-start(bf16[1,2,16,5632]{3,2,1,0:T(8,128)(2,1)S(1)} %get-tuple-element.356), channel_id=1, source_target_pairs={{0,2},{1,3},{4,6},{5,7},{8,10},{9,11},{12,14},{13,15},{16,18},{17,... | collective-permute-start | bytes 1081352 | tf_op jit(solution)/shard_map/ppermute | solution.py:38
  14.8 5.8 %copy-start.6 = (f32[9,5632]{1,0:T(8,128)S(1)}, f32[9,5632]{1,0:T(8,128)}, u32[]{:S(2)}) copy-start(f32[9,5632]{1,0:T(8,128)} %param.17) | copy-start | bytes 608260
  14.8 23.4 %collective-permute-start.1 = (bf16[1,2,16,5632]{3,2,1,0:T(8,128)(2,1)}, bf16[1,2,16,5632]{3,2,1,0:T(8,128)(2,1)}, u32[]{:S(2)}, u32[]{:S(2)}) collective-permute-start(bf16[1,2,16,5632]{3,2,1,0:T(8,128)(2,1)} %get-tuple-element.355), channel_id=1, source_target_pairs={{2,0},{3,1},{6,4},{7,5},{10,8},{11,9},{14,12},{15,13},{18,16},{19,... | collective-permute-start | bytes 1081352 | tf_op jit(solution)/shard_map/ppermute | solution.py:41
  17.2 12.5 %copy-start.7 = (s32[4]{0:T(128)S(1)}, s32[4]{0:T(128)}, u32[]{:S(2)}) copy-start(s32[4]{0:T(128)} %param.15) | copy-start | bytes 52
  17.3 14.5 %copy-start.11 = (u32[32]{0:T(128)S(1)}, u32[32]{0:T(128)}, u32[]{:S(2)}) copy-start(u32[32]{0:T(128)} %constant.120) | copy-start | bytes 388
  17.3 15.1 %copy-start.8 = (u32[32]{0:T(128)S(1)}, u32[32]{0:T(128)}, u32[]{:S(2)}) copy-start(u32[32]{0:T(128)} %constant.130) | copy-start | bytes 388
  17.3 17.7 %copy-start.5 = (bf16[1,8,16,1120]{3,2,1,0:T(8,128)(2,1)S(1)}, bf16[1,8,16,1120]{3,2,1,0:T(8,128)(2,1)}, u32[]{:S(2)}) copy-start(bf16[1,8,16,1120]{3,2,1,0:T(8,128)(2,1)} %param.11) | copy-start | bytes 860164
  20.5 134.6 %reduce-scatter.9.cloned.1.call-start = ((), (), s32[]{:S(2)}) async-start(), calls=%async_computation.3 | async-start | bytes 716800
  40.4 30.4 %collective-permute-start.2 = (bf16[1,12,2,5632]{3,2,1,0:T(2,128)(2,1)}, bf16[1,12,2,5632]{3,2,1,0:T(2,128)(2,1)}, u32[]{:S(2)}, u32[]{:S(2)}) collective-permute-start(bf16[1,12,2,5632]{3,2,1,0:T(2,128)(2,1)} %get-tuple-element.353), channel_id=1, source_target_pairs={{0,1},{2,3},{4,5},{6,7},{8,9},{10,11},{12,13},{14,15},{16,17},{18,... | collective-permute-start | bytes 811016 | tf_op jit(solution)/shard_map/ppermute | solution.py:38
  42.4 28.4 %collective-permute-start.3 = (bf16[1,12,2,5632]{3,2,1,0:T(2,128)(2,1)}, bf16[1,12,2,5632]{3,2,1,0:T(2,128)(2,1)}, u32[]{:S(2)}, u32[]{:S(2)}) collective-permute-start(bf16[1,12,2,5632]{3,2,1,0:T(2,128)(2,1)} %get-tuple-element.354), channel_id=1, source_target_pairs={{1,0},{3,2},{5,4},{7,6},{9,8},{11,10},{13,12},{15,14},{17,16},{19,... | collective-permute-start | bytes 811016 | tf_op jit(solution)/shard_map/ppermute | solution.py:41
  80.5 20.0 %copy-start.10 = (f32[4]{0:T(128)S(1)}, f32[4]{0:T(128)}, u32[]{:S(2)}) copy-start(f32[4]{0:T(128)} %get-tuple-element.453) | copy-start | bytes 52
  83.5 27.4 %copy-start.1 = (f32[128,10,112]{0,2,1:T(8,128)S(1)}, f32[128,10,112]{0,2,1:T(8,128)}, u32[]{:S(2)}) copy-start(f32[128,10,112]{0,2,1:T(8,128)} %copy.39) | copy-start | bytes 1720324
  100.4 12.1 %copy-start.2 = (f32[280,112]{1,0:T(8,128)S(1)}, f32[280,112]{1,0:T(8,128)}, u32[]{:S(2)}) copy-start(f32[280,112]{1,0:T(8,128)} %reduce-scatter.7.cloned.1.call-done) | copy-start | bytes 376324
  128.6 14.8 %copy-start.9 = (f32[4]{0:T(128)S(1)}, f32[4]{0:T(128)}, u32[]{:S(2)}) copy-start(f32[4]{0:T(128)} %dynamic-update-slice.3) | copy-start | bytes 52
  155.1 19.6 %copy-start.3 = (f32[280,112]{1,0:T(8,128)S(1)}, f32[280,112]{1,0:T(8,128)}, u32[]{:S(2)}) copy-start(f32[280,112]{1,0:T(8,128)} %reduce-scatter.9.cloned.1.call-done) | copy-start | bytes 376324
Sparse Core Ops, SparseCore 0:
  20.6 25.0 reduce-scatter.6
  112.7 20.6 reduce-scatter.8
where the time goes:
time: 201 us; the launch traced here: 200 us
  blocking collectives  96.2 us (48%)
  other arithmetic  32 us (16%)
  local copies, waits for them, and re-layouts  31.9 us (16%)
  between operations  18.9 us (9%)
  starting transfers between devices  10.5 us (5%)
  matrix products  6.22 us (3%)
  loops' own time  4.06 us (2%)
    unnamed x6, blocking collectives  49 us
    all_gather x2, blocking collectives, entering(): pieces = jax.tree.map(lambda part: lax.all_gather(part, axis), value)  32.4 us
    convert_element_type x1, other arithmetic, per_device(): hidden_grad = hidden_grad[None].astype(jnp.bfloat16)  14.8 us
    all_gather x1, blocking collectives, per_device(): lax.all_gather(part_kv, ('height', 'width'), axis=0, tiled=True)  7.86 us
    ppermute x2, starting transfers between devices, padded(): lax.ppermute(lax.slice_in_dim(block, block.shape[dim] - width, None, axis...  7.68 us
    unnamed x38, local copies, waits for them, and re-layouts  7.01 us
    all_gather x1, blocking collectives, per_device(): lax.all_gather(part_grad_kv, ('height', 'width'), axis=0, tiled=True)  6.9 us
    add x1, other arithmetic, depthwise(): return reduce(lambda first, second: first + second, terms)  5.8 us
  transfers between devices with their start and end apart: 6, of which 0 were waited for; matrix products, arithmetic and copies ran while one was open for 29% of the time, Pallas kernels for 0%

commit v1 on v0

--- a/solution.py
+++ b/solution.py
@@ -1,8 +1,11 @@
+import functools
 from functools import reduce
 
 import jax
 import jax.numpy as jnp
 from jax import lax
+from jax.experimental import pallas as pl
+from jax.experimental.pallas import tpu as pltpu
 from jax.sharding import PartitionSpec as P
 
 HEAD_DIM = 112
@@ -89,7 +92,7 @@
     return reduce(lambda first, second: first + second, terms)
 
 
-def per_device(queries, attn_keys, attn_values, attn_cotangent, clip_ids, hidden_pre, conv_weight):
+def general_attention(queries, attn_keys, attn_values, attn_cotangent, clip_ids):
     token_count = queries.shape[1] * queries.shape[2]
     flat_width = HEADS * HEAD_DIM
     starts, ends = clip_flags(clip_ids)
@@ -184,6 +187,256 @@
         "cob,obq->coq", feature_keys.astype(jnp.float32), total_key_value, precision=TOP_PRECISION
     )
     value_gradient = value_gradient.reshape(attn_values.shape).astype(jnp.bfloat16)
+    return (query_grad, key_grad, value_gradient)
+
+
+LANES = 128
+
+
+def split_terms(value):
+    high = value.astype(jnp.bfloat16)
+    low = (value - high.astype(jnp.float32)).astype(jnp.bfloat16)
+    return high, low
+
+
+def dot_tokens(left, right):
+    return lax.dot_general(left, right, (((0,), (0,)), ((), ())), preferred_element_type=jnp.float32)
+
+
+def dot_rows(left, right):
+    return lax.dot_general(left, right, (((1,), (0,)), ((), ())), preferred_element_type=jnp.float32)
+
+
+def dot_columns(left, right):
+    return lax.dot_general(left, right, (((1,), (1,)), ((), ())), preferred_element_type=jnp.float32)
+
+
+def head_slice(ref, head):
+    return ref[:, head * HEAD_DIM : (head + 1) * HEAD_DIM]
+
+
+def tail_block(rows, first):
+    column = lax.broadcasted_iota(jnp.int32, (rows, LANES - HEAD_DIM), 1)
+    return jnp.where(column == 0, first, 0.0).astype(jnp.bfloat16)
+
+
+def vmem_call(kernel, out_shape, scratch=(), smem_first=False, n_in=0, flops=0, bytes_accessed=0, aliases=None):
+    vmem = pl.BlockSpec(memory_space=pltpu.VMEM)
+    in_specs = [vmem] * n_in
+    if smem_first:
+        in_specs[0] = pl.BlockSpec(memory_space=pltpu.SMEM)
+    return pl.pallas_call(
+        kernel,
+        out_shape=out_shape,
+        in_specs=in_specs,
+        out_specs=jax.tree.map(lambda _: vmem, out_shape),
+        scratch_shapes=list(scratch),
+        cost_estimate=pl.CostEstimate(flops=flops, bytes_accessed=bytes_accessed, transcendentals=0),
+    )
+
+
+def state_kernel(key_ref, value_ref, keep_ref, send_ref, halves):
+    tokens = key_ref.shape[0]
+    one = tail_block(tokens, 1.0)
+    half = halves.shape[2]
+    per_group = HEADS // 2
+    column = lax.axis_index("width")
+    for group in range(2):
+        for place in range(per_group):
+            head = group * per_group + place
+            feature = jnp.maximum(head_slice(key_ref, head), 0)
+            wide = jnp.concatenate([head_slice(value_ref, head), one], axis=1)
+            store_rows(halves, group, place * HEAD_DIM, dot_tokens(feature, wide), half)
+    keep_ref[...] = halves[column]
+    send_ref[...] = halves[1 - column]
+
+
+def store_rows(halves, group, first, block, half):
+    cut = min(max(half - first, 0), HEAD_DIM)
+    if cut:
+        index = (0, group) if group is not None else (0,)
+        halves[(*index, slice(first, first + cut))] = block[:cut]
+    if cut < HEAD_DIM:
+        index = (1, group) if group is not None else (1,)
+        start = first + cut - half
+        halves[(*index, slice(start, start + HEAD_DIM - cut))] = block[cut:]
+
+
+def pick_kernel(keep_ref, came_ref, mine_ref, other_ref):
+    row = lax.axis_index("height")
+    mine_ref[...] = keep_ref[row] + came_ref[row]
+    other_ref[...] = keep_ref[1 - row] + came_ref[1 - row]
+
+
+def heads_kernel(query_ref, cotangent_ref, mine_ref, other_ref, groups):
+    none = tail_block(query_ref.shape[0], 0.0)
+    per_group = HEADS // 2
+    row = lax.axis_index("height")
+    for head in range(HEADS):
+        group, place = divmod(head, per_group)
+        feature = jnp.maximum(head_slice(query_ref, head), 0)
+        groups[group, 0, place] = jnp.concatenate([feature, none], axis=1)
+        groups[group, 1, place] = jnp.concatenate([head_slice(cotangent_ref, head), none], axis=1)
+    mine_ref[...] = groups[row]
+    other_ref[...] = groups[1 - row]
+
+
+def chain_kernel(step, clip_ref, own_ref, near_ref, far_ref, out_ref):
+    frame = lax.axis_index("tm")
+    last = lax.axis_size("tm") - 1
+    here = clip_ref[frame]
+    first = jnp.clip(frame - step, 0, last)
+    second = jnp.clip(frame - 2 * step, 0, last)
+    near = jnp.where((clip_ref[first] == here) & (first != frame), 1.0, 0.0)
+    far = jnp.where((clip_ref[second] == here) & (second != first), 1.0, 0.0)
+    out_ref[...] = own_ref[...] + near * near_ref[...] + far * far_ref[...]
+
+
+def query_kernel(state_ref, came_ref, mine_ref, other_ref, keep_ref, send_ref, own_out, other_out, state, halves):
+    column = lax.axis_index("width")
+    half = state_ref.shape[0]
+    per_group = HEADS // 2
+    tokens = mine_ref.shape[2]
+    state[column] = state_ref[...]
+    state[1 - column] = came_ref[...]
+    lane = lax.broadcasted_iota(jnp.int32, (2 * tokens, LANES), 1)
+    for place in range(per_group):
+        feature = jnp.concatenate([mine_ref[0, place], other_ref[0, place]], axis=0)
+        cotangent = jnp.concatenate([mine_ref[1, place], other_ref[1, place]], axis=0).astype(jnp.float32)
+        high, low = split_terms(load_rows(state, place * HEAD_DIM, half))
+        narrow = feature[:, :HEAD_DIM]
+        product = dot_rows(narrow, high) + dot_rows(narrow, low)
+        inverse = 1.0 / (product[:, HEAD_DIM : HEAD_DIM + 1] + EPSILON)
+        against = jnp.sum(cotangent * product, axis=1, keepdims=True)
+        norm_grad = -(against * inverse) * inverse
+        scaled = jnp.where(lane == HEAD_DIM, norm_grad, cotangent * inverse)
+        scaled_high, scaled_low = split_terms(scaled)
+        grad = dot_tokens(narrow, scaled_high) + dot_tokens(narrow, scaled_low)
+        store_rows(halves, None, place * HEAD_DIM, grad, half)
+        back = dot_columns(scaled_high, high) + dot_columns(scaled_high, low) + dot_columns(scaled_low, high)
+        back = jnp.where(narrow > 0, back, 0.0).astype(jnp.bfloat16)
+        own_out[place, :, :HEAD_DIM] = back[:tokens]
+        other_out[place, :, :HEAD_DIM] = back[tokens:]
+    keep_ref[...] = halves[column]
+    send_ref[...] = halves[1 - column]
+
+
+def load_rows(state, first, half):
+    cut = min(max(half - first, 0), HEAD_DIM)
+    parts = []
+    if cut:
+        parts.append(state[0, first : first + cut])
+    if cut < HEAD_DIM:
+        start = first + cut - half
+        parts.append(state[1, start : start + HEAD_DIM - cut])
+    return parts[0] if len(parts) == 1 else jnp.concatenate(parts, axis=0)
+
+
+def key_kernel(key_ref, value_ref, near_ref, near_came_ref, far_ref, far_came_ref, key_out, value_out, total):
+    column, row = lax.axis_index("width"), lax.axis_index("height")
+    half = near_ref.shape[0]
+    per_group = HEADS // 2
+    total[row, column] = near_ref[...]
+    total[row, 1 - column] = near_came_ref[...]
+    total[1 - row, column] = far_ref[...]
+    total[1 - row, 1 - column] = far_came_ref[...]
+    one = tail_block(key_ref.shape[0], 1.0)
+    for head in range(HEADS):
+        group, place = divmod(head, per_group)
+        feature = jnp.maximum(head_slice(key_ref, head), 0)
+        wide = jnp.concatenate([head_slice(value_ref, head), one], axis=1)
+        high, low = split_terms(load_rows(total.at[group], place * HEAD_DIM, half))
+        grad = dot_columns(wide, high) + dot_columns(wide, low)
+        lanes = slice(head * HEAD_DIM, (head + 1) * HEAD_DIM)
+        key_out[:, lanes] = jnp.where(feature > 0, grad, 0.0).astype(jnp.bfloat16)
+        product = dot_rows(feature, high) + dot_rows(feature, low)
+        value_out[:, lanes] = product[:, :HEAD_DIM].astype(jnp.bfloat16)
+
+
+def join_kernel(mine_ref, came_ref, out_ref):
+    row = lax.axis_index("height")
+    per_group = HEADS // 2
+    for place in range(per_group):
+        mine, came = mine_ref[place, :, :HEAD_DIM], came_ref[place, :, :HEAD_DIM]
+        first = jnp.where(row == 0, mine, came)
+        second = jnp.where(row == 0, came, mine)
+        out_ref[:, place * HEAD_DIM : (place + 1) * HEAD_DIM] = first
+        at = (per_group + place) * HEAD_DIM
+        out_ref[:, at : at + HEAD_DIM] = second
+
+
+def struct(shape, dtype=jnp.float32):
+    return jax.ShapeDtypeStruct(shape, dtype)
+
+
+SWAP = [(0, 1), (1, 0)]
+
+
+def paired_attention(queries, attn_keys, attn_values, attn_cotangent, clip_ids):
+    tokens = queries.shape[1] * queries.shape[2]
+    flat = HEADS * HEAD_DIM
+    per_group = HEADS // 2
+    half = per_group * HEAD_DIM // 2
+    frames = lax.axis_size("tm")
+    query, key, value, cotangent = (
+        part.reshape(tokens, flat) for part in (queries, attn_keys, attn_values, attn_cotangent)
+    )
+    share = struct((half, LANES))
+    pair = struct((2, half, LANES))
+
+    keep, send = vmem_call(
+        state_kernel, (pair, pair), [pltpu.VMEM((2, 2, half, LANES), jnp.float32)], n_in=2,
+        flops=2 * tokens * flat * LANES, bytes_accessed=4 * tokens * flat + 8 * half * LANES * 2,
+    )(key, value)
+    came = lax.ppermute(send, "width", SWAP)
+    mine, other = vmem_call(pick_kernel, (share, share), n_in=2, bytes_accessed=24 * half * LANES)(keep, came)
+    came = lax.ppermute(other, "height", SWAP)
+
+    packed = struct((2, per_group, tokens, LANES), jnp.bfloat16)
+    heads_mine, heads_other = vmem_call(
+        heads_kernel, (packed, packed), [pltpu.VMEM((2, 2, per_group, tokens, LANES), jnp.bfloat16)], n_in=2,
+        bytes_accessed=12 * tokens * flat,
+    )(query, cotangent)
+    own = mine + came
+    heads_other, own = lax.optimization_barrier((heads_other, own))
+    heads_came = lax.ppermute(heads_other, "height", SWAP)
+
+    def along_frames(own, step):
+        moves = [[(at, at + step * hop) for at in range(frames) if 0 <= at + step * hop < frames] for hop in (1, 2)]
+        near = lax.ppermute(own, "tm", moves[0])
+        far = lax.ppermute(own, "tm", moves[1])
+        return vmem_call(
+            functools.partial(chain_kernel, step), share, smem_first=True, n_in=4, bytes_accessed=16 * half * LANES
+        )(clip_ids, own, near, far)
+
+    state = along_frames(own, 1)
+    came = lax.ppermute(state, "width", SWAP)
+    back = struct((per_group, tokens, LANES), jnp.bfloat16)
+    keep, send, back_mine, back_other = vmem_call(
+        query_kernel, (share, share, back, back),
+        [pltpu.VMEM((2, half, LANES), jnp.float32), pltpu.VMEM((2, half, LANES), jnp.float32)], n_in=4,
+        flops=14 * tokens * flat * LANES, bytes_accessed=8 * tokens * flat,
+    )(state, came, heads_mine, heads_came)
+    came = lax.ppermute(send, "width", SWAP)
+    own = keep + came
+    back_other, own = lax.optimization_barrier((back_other, own))
+    total = along_frames(own, -1)
+    back_came = lax.ppermute(back_other, "height", SWAP)
+    query_grad = vmem_call(
+        join_kernel, struct((tokens, flat), jnp.bfloat16), n_in=2, bytes_accessed=4 * tokens * flat
+    )(back_mine, back_came)
+    far = lax.ppermute(total, "height", SWAP)
+    near_came = lax.ppermute(total, "width", SWAP)
+    far_came = lax.ppermute(far, "width", SWAP)
+    out = struct((tokens, flat), jnp.bfloat16)
+    key_grad, value_gradient = vmem_call(
+        key_kernel, (out, out), [pltpu.VMEM((2, 2, half, LANES), jnp.float32)], n_in=6,
+        flops=8 * tokens * flat * LANES, bytes_accessed=8 * tokens * flat,
+    )(key, value, total, near_came, far, far_came)
+    return tuple(part.reshape(queries.shape) for part in (query_grad, key_grad, value_gradient))
+
+
+def mixed_ffn(hidden_pre, conv_weight):
     row_count = hidden_pre.shape[1]
     col_count = hidden_pre.shape[2]
     split_at = hidden_pre.shape[3] // 2
@@ -197,7 +450,20 @@
     conv_grad = glu_grad(conv_out, split_at) * inside[:, :, None]
     hidden_grad = depthwise(conv_grad, conv_weight, 1, -1, row_count, col_count)
     hidden_grad = hidden_grad[None].astype(jnp.bfloat16)
-    return (query_grad, key_grad, value_gradient, hidden_grad)
+    return hidden_grad
+
+
+def per_device(queries, attn_keys, attn_values, attn_cotangent, clip_ids, hidden_pre, conv_weight):
+    paired = (
+        lax.axis_size("height") == 2
+        and lax.axis_size("width") == 2
+        and 3 <= lax.axis_size("tm") <= 4
+        and HEADS % 2 == 0
+        and queries.shape[0] == 1
+    )
+    attention = paired_attention if paired else general_attention
+    grads = attention(queries, attn_keys, attn_values, attn_cotangent, clip_ids)
+    return (*grads, mixed_ffn(hidden_pre, conv_weight))
 
 
 def solution(mesh):

time: 201 us -> 95.2 us (0.47)
  the two profiles are of different devices: /device:TPU:0 before, /device:TPU:1 now
where the time goes in v1:
time: 95.2 us; the launch traced here: 94.7 us
  starting transfers between devices  28.1 us (30%)
  Pallas kernels  20 us (21%)
  other arithmetic  18.9 us (20%)
  waiting for transfers between devices  18.3 us (19%)
  local copies, waits for them, and re-layouts  8.35 us (9%)
  between operations  0.99 us (1%)
    ppermute x2, waiting for transfers between devices, along_frames(): far = lax.ppermute(own, 'tm', moves[1])  8.52 us
    add x1, other arithmetic, depthwise(): return reduce(lambda first, second: first + second, terms)  6.85 us
    ppermute x2, waiting for transfers between devices, padded(): lax.ppermute(lax.slice_in_dim(block, 0, width, axis=dim), axis, backward)  5.84 us
    ppermute x2, starting transfers between devices, along_frames(): far = lax.ppermute(own, 'tm', moves[1])  5.69 us
    unnamed x54, local copies, waits for them, and re-layouts  5.53 us
    ppermute x2, starting transfers between devices, padded(): lax.ppermute(lax.slice_in_dim(block, block.shape[dim] - width, None, axis...  5.26 us
    ppermute x2, starting transfers between devices, padded(): lax.ppermute(lax.slice_in_dim(block, 0, width, axis=dim), axis, backward)  5.07 us
    pallas_call x1, Pallas kernels, paired_attention(): vmem_call(query_kernel, (share, share, back, back), [pltpu.VMEM((2, half,...  4.95 us
  transfers between devices with their start and end apart: 17, of which 6 were waited for; matrix products, arithmetic and copies ran while one was open for 22% of the time, Pallas kernels for 11%

profile of v1, /device:TPU:1, one launch (start us, length us, event | category | flops | bytes accessed | tf_op | source)
XLA Modules:
  0.0 94.7 jit_solution(11615005476826629281)
XLA Ops:
  0.6 1.3 %fusion.11 = (bf16[1,2,16,5632]{3,2,1,0:T(8,128)(2,1)S(1)}, bf16[1,2,16,5632]{3,2,1,0:T(8,128)(2,1)S(1)}) fusion(bf16[1,8,16,5632]{3,2,1,0:T(8,128)(2,1)} %param.12), kind=kLoop, calls=%fused_computation.42 | loop fusion | bytes 1441792 | tf_op jit(solution)/shard_map/slice | solution.py:44
  1.9 4.0 %collective-permute-start.13 = (bf16[1,2,16,5632]{3,2,1,0:T(8,128)(2,1)S(1)}, bf16[1,2,16,5632]{3,2,1,0:T(8,128)(2,1)S(1)}, u32[]{:S(2)}, u32[]{:S(2)}) collective-permute-start(bf16[1,2,16,5632]{3,2,1,0:T(8,128)(2,1)S(1)} %get-tuple-element.50), channel_id=1, source_target_pairs={{0,2},{1,3},{4,6},{5,7},{8,10},{9,11},{12,14},{13,15},{16,18},{17,... | collective-permute-start | bytes 1081352 | tf_op jit(solution)/shard_map/ppermute | solution.py:41
  5.9 2.7 %shard_map.103 = (f32[2,280,128]{2,1,0:T(8,128)}, f32[2,280,128]{2,1,0:T(8,128)}) custom-call(bf16[128,1120]{1,0:T(8,128)(2,1)} %bitcast.11, bf16[128,1120]{1,0:T(8,128)(2,1)} %bitcast.13), custom_call_target="tpu_custom_call" | custom-call | flops 36700160 | bytes 1146880 | tf_op jit(solution)/shard_map/pallas_call | solution.py:387
  9.5 1.3 %collective-permute-start.14 = (bf16[1,2,16,5632]{3,2,1,0:T(8,128)(2,1)S(1)}, bf16[1,2,16,5632]{3,2,1,0:T(8,128)(2,1)S(1)}, u32[]{:S(2)}, u32[]{:S(2)}) collective-permute-start(bf16[1,2,16,5632]{3,2,1,0:T(8,128)(2,1)S(1)} %get-tuple-element.49), channel_id=1, source_target_pairs={{2,0},{3,1},{6,4},{7,5},{10,8},{11,9},{14,12},{15,13},{18,16},{19,... | collective-permute-start | bytes 1081352 | tf_op jit(solution)/shard_map/ppermute | solution.py:44
  11.6 1.8 %shard_map.104 = (f32[280,128]{1,0:T(8,128)}, f32[280,128]{1,0:T(8,128)}) custom-call(f32[2,280,128]{2,1,0:T(8,128)} %get-tuple-element.21.keep_ref, f32[2,280,128]{2,1,0:T(8,128)} %copy-done.5), custom_call_target="tpu_custom_call" | custom-call | bytes 860160 | tf_op jit(solution)/shard_map/pallas_call | solution.py:392
  13.4 2.0 %collective-permute-start.1 = (f32[280,128]{1,0:T(8,128)}, f32[280,128]{1,0:T(8,128)S(1)}, u32[]{:S(2)}, u32[]{:S(2)}) collective-permute-start(f32[280,128]{1,0:T(8,128)} %get-tuple-element.24), channel_id=1, source_target_pairs={{0,2},{2,0},{1,3},{3,1},{4,6},{6,4},{5,7},{7,5},{8,10},{10,8},{9,1... | collective-permute-start | bytes 430088 | tf_op jit(solution)/shard_map/ppermute | solution.py:393
  15.6 5.8 %collective-permute-done.14 = bf16[1,2,16,5632]{3,2,1,0:T(8,128)(2,1)S(1)} collective-permute-done((bf16[1,2,16,5632]{3,2,1,0:T(8,128)(2,1)S(1)}, bf16[1,2,16,5632]{3,2,1,0:T(8,128)(2,1)S(1)}, u32[]{:S(2)}, u32[]{:S(2)}) %collective-permute-start.14) | collective-permute-done | bytes 360480 | tf_op jit(solution)/shard_map/ppermute | solution.py:44
  21.4 1.3 %copy-done = bf16[1,12,16,5632]{3,2,1,0:T(8,128)(2,1)} copy-done((bf16[1,12,16,5632]{3,2,1,0:T(8,128)(2,1)}, bf16[1,12,16,5632]{3,2,1,0:T(8,128)(2,1)S(1)}, u32[]{:S(2)}) %copy-start) | copy-done | bytes 2162712
  23.2 1.3 %collective-permute-start.15 = (bf16[1,12,2,5632]{3,2,1,0:T(2,128)(2,1)S(1)}, bf16[1,12,2,5632]{3,2,1,0:T(2,128)(2,1)S(1)}, u32[]{:S(2)}, u32[]{:S(2)}) collective-permute-start(bf16[1,12,2,5632]{3,2,1,0:T(2,128)(2,1)S(1)} %get-tuple-element.47), channel_id=1, source_target_pairs={{0,1},{2,3},{4,5},{6,7},{8,9},{10,11},{12,13},{14,15},{16,17},{18,... | collective-permute-start | bytes 811016 | tf_op jit(solution)/shard_map/ppermute | solution.py:41
  24.5 3.8 %collective-permute-start.16 = (bf16[1,12,2,5632]{3,2,1,0:T(2,128)(2,1)S(1)}, bf16[1,12,2,5632]{3,2,1,0:T(2,128)(2,1)}, u32[]{:S(2)}, u32[]{:S(2)}) collective-permute-start(bf16[1,12,2,5632]{3,2,1,0:T(2,128)(2,1)S(1)} %get-tuple-element.48), channel_id=1, source_target_pairs={{1,0},{3,2},{5,4},{7,6},{9,8},{11,10},{13,12},{15,14},{17,16},{19,... | collective-permute-start | bytes 811016 | tf_op jit(solution)/shard_map/ppermute | solution.py:44
  28.4 2.4 %shard_map.102 = (bf16[2,5,128,128]{3,2,1,0:T(8,128)(2,1)}, bf16[2,5,128,128]{3,2,1,0:T(8,128)(2,1)}) custom-call(bf16[128,1120]{1,0:T(8,128)(2,1)} %bitcast.15, bf16[128,1120]{1,0:T(8,128)(2,1)} %bitcast.16), custom_call_target="tpu_custom_call" | custom-call | bytes 1720320 | tf_op jit(solution)/shard_map/pallas_call | solution.py:396
  30.8 3.2 %collective-permute-start.2 = (f32[280,128]{1,0:T(8,128)S(1)}, f32[280,128]{1,0:T(8,128)S(1)}, u32[]{:S(2)}, u32[]{:S(2)}) collective-permute-start(f32[280,128]{1,0:T(8,128)S(1)} %add.90.own_ref), channel_id=1, source_target_pairs={{0,4},{4,8},{8,12},{1,5},{5,9},{9,13},{2,6},{6,10},{10,14},{3,7},{... | collective-permute-start | bytes 430088 | tf_op jit(solution)/shard_map/ppermute | solution.py:406
  34.0 4.2 %collective-permute-start.3 = (f32[280,128]{1,0:T(8,128)S(1)}, f32[280,128]{1,0:T(8,128)S(1)}, u32[]{:S(2)}, u32[]{:S(2)}) collective-permute-start(f32[280,128]{1,0:T(8,128)S(1)} %add.90.own_ref), channel_id=1, source_target_pairs={{0,8},{4,12},{1,9},{5,13},{2,10},{6,14},{3,11},{7,15},{16,24},{20,... | collective-permute-start | bytes 430088 | tf_op jit(solution)/shard_map/ppermute | solution.py:407
  39.4 1.9 %collective-permute-done.3.far_ref = f32[280,128]{1,0:T(8,128)S(1)} collective-permute-done((f32[280,128]{1,0:T(8,128)S(1)}, f32[280,128]{1,0:T(8,128)S(1)}, u32[]{:S(2)}, u32[]{:S(2)}) %collective-permute-start.3) | collective-permute-done | bytes 143392 | tf_op jit(solution)/shard_map/ppermute | solution.py:407
  41.9 1.7 %shard_map.105.state_ref = f32[280,128]{1,0:T(8,128)} custom-call(s32[4]{0:T(128)} %clip_ref.3, f32[280,128]{1,0:T(8,128)} %copy-done.3, f32[280,128]{1,0:T(8,128)} %copy-done.18, f32[280,128]{1,0:T(8,128)} %copy-done.19), custom_call_target="tpu_custom_call" | custom-call | bytes 573440 | tf_op jit(solution)/shard_map/pallas_call | solution.py:408
  43.7 2.7 %maximum_bitcast_fusion = bf16[12,20,5632]{2,1,0:T(8,128)(2,1)S(1)} fusion(bf16[1,12,2,5632]{3,2,1,0:T(2,128)(2,1)} %collective-permute-done.16, bf16[1,12,16,5632]{3,2,1,0:T(8,128)(2,1)} %copy-done, bf16[1,12,2,5632]{3,2,1,0:T(2,128)(2,1)S(1)} %collective-permute-done.15), kind=kLoop, calls=%fused_computation.2 | loop fusion | flops 8110080 | bytes 5406720 | tf_op jit(solution)/shard_map/squeeze | solution.py:443
  46.4 2.4 %collective-permute-done.5.other_ref = bf16[2,5,128,128]{3,2,1,0:T(8,128)(2,1)} collective-permute-done((bf16[2,5,128,128]{3,2,1,0:T(8,128)(2,1)}, bf16[2,5,128,128]{3,2,1,0:T(8,128)(2,1)}, u32[]{:S(2)}, u32[]{:S(2)}) %collective-permute-start.5) | collective-permute-done | bytes 327712 | tf_op jit(solution)/shard_map/ppermute | solution.py:402
  48.8 5.0 %shard_map.106 = (f32[280,128]{1,0:T(8,128)}, f32[280,128]{1,0:T(8,128)}, bf16[5,128,128]{2,1,0:T(8,128)(2,1)}, bf16[5,128,128]{2,1,0:T(8,128)(2,1)}) custom-call(f32[280,128]{1,0:T(8,128)} %shard_map.105.state_ref, f32[280,128]{1,0:T(8,128)} %collective-permute-done.4.came_ref, bf16[2,5,128,128]{3,2,1,0:T(8,128)(2,1)} %get-tuple-element.26.mine_ref, ...), custom_call_target="tpu_custom_call" | custom-call | flops 256901120 | bytes 1146880 | tf_op jit(solution)/shard_map/pallas_call | solution.py:415
  54.2 6.8 %multiply_add_fusion = f32[10,18,5632]{2,1,0:T(8,128)S(1)} fusion(bf16[12,20,5632]{2,1,0:T(8,128)(2,1)S(1)} %maximum_bitcast_fusion, f32[5632]{0:T(1024)} %get-tuple-element.43, f32[5632]{0:T(1024)} %get-tuple-element.44, f32[5632]{0:T(1024)} %get-tuple-element.37, f32[5632]{0:T(1024)} %get-tuple-element.38, f32[5632]{0:T(1024)} %get-tuple-element.39, ...), kind=kLoop, calls=%fused_computation.1 | loop fusion | flops 26357760 | bytes 22505472 | tf_op jit(solution)/shard_map/add | solution.py:92
  61.1 1.3 %collective-permute-start.8 = (f32[280,128]{1,0:T(8,128)S(1)}, f32[280,128]{1,0:T(8,128)S(1)}, u32[]{:S(2)}, u32[]{:S(2)}) collective-permute-start(f32[280,128]{1,0:T(8,128)S(1)} %add.91.own_ref), channel_id=1, source_target_pairs={{4,0},{8,4},{12,8},{5,1},{9,5},{13,9},{6,2},{10,6},{14,10},{7,3},{... | collective-permute-start | bytes 430088 | tf_op jit(solution)/shard_map/ppermute | solution.py:406
  62.4 1.5 %collective-permute-start.9 = (f32[280,128]{1,0:T(8,128)S(1)}, f32[280,128]{1,0:T(8,128)S(1)}, u32[]{:S(2)}, u32[]{:S(2)}) collective-permute-start(f32[280,128]{1,0:T(8,128)S(1)} %add.91.own_ref), channel_id=1, source_target_pairs={{8,0},{12,4},{9,1},{13,5},{10,2},{14,6},{11,3},{15,7},{24,16},{28,... | collective-permute-start | bytes 430088 | tf_op jit(solution)/shard_map/ppermute | solution.py:407
  63.9 2.9 %multiply_multiply_fusion = (f32[10,18,2816]{2,1,0:T(8,128)S(1)}, f32[10,18,2816]{2,1,0:T(8,128)}) fusion(f32[10,18,5632]{2,1,0:T(8,128)S(1)} %multiply_add_fusion), kind=kLoop, calls=%fused_computation.22 | loop fusion | flops 6589440 | bytes 8110080 | tf_op jit(solution)/shard_map/mul | solution.py:76
  66.8 1.4 %collective-permute-done.8.near_ref = f32[280,128]{1,0:T(8,128)S(1)} collective-permute-done((f32[280,128]{1,0:T(8,128)S(1)}, f32[280,128]{1,0:T(8,128)S(1)}, u32[]{:S(2)}, u32[]{:S(2)}) %collective-permute-start.8) | collective-permute-done | bytes 143392 | tf_op jit(solution)/shard_map/ppermute | solution.py:406
  68.2 6.6 %collective-permute-done.9.far_ref = f32[280,128]{1,0:T(8,128)S(1)} collective-permute-done((f32[280,128]{1,0:T(8,128)S(1)}, f32[280,128]{1,0:T(8,128)S(1)}, u32[]{:S(2)}, u32[]{:S(2)}) %collective-permute-start.9) | collective-permute-done | bytes 143392 | tf_op jit(solution)/shard_map/ppermute | solution.py:407
  75.5 1.8 %shard_map.108.near_ref = f32[280,128]{1,0:T(8,128)} custom-call(s32[4]{0:T(128)} %clip_ref.3, f32[280,128]{1,0:T(8,128)} %copy-done.4, f32[280,128]{1,0:T(8,128)} %copy-done.20, f32[280,128]{1,0:T(8,128)} %copy-done.21), custom_call_target="tpu_custom_call" | custom-call | bytes 573440 | tf_op jit(solution)/shard_map/pallas_call | solution.py:408
  77.3 2.6 %maximum_multiply_fusion = f32[10,18,5632]{2,1,0:T(8,128)S(1)} fusion(f32[10,18,2816]{2,1,0:T(8,128)} %get-tuple-element.46, f32[10,18,2816]{2,1,0:T(8,128)S(1)} %get-tuple-element.45, f32[10,18]{1,0:T(8,128)S(1)} %and_convert_fusion), kind=kLoop, calls=%fused_computation | loop fusion | flops 2027520 | bytes 8110800 | tf_op jit(solution)/shard_map/mul | solution.py:450
  79.9 1.5 %collective-permute-start.7 = (bf16[5,128,128]{2,1,0:T(8,128)(2,1)S(1)}, bf16[5,128,128]{2,1,0:T(8,128)(2,1)S(1)}, u32[]{:S(2)}, u32[]{:S(2)}) collective-permute-start(bf16[5,128,128]{2,1,0:T(8,128)(2,1)S(1)} %copy-done.25), channel_id=1, source_target_pairs={{0,2},{2,0},{1,3},{3,1},{4,6},{6,4},{5,7},{7,5},{8,10},{10,8},{9,1... | collective-permute-start | bytes 491528 | tf_op jit(solution)/shard_map/ppermute | solution.py:424
  81.4 1.4 %collective-permute-start.10 = (f32[280,128]{1,0:T(8,128)S(1)}, f32[280,128]{1,0:T(8,128)S(1)}, u32[]{:S(2)}, u32[]{:S(2)}) collective-permute-start(f32[280,128]{1,0:T(8,128)S(1)} %copy-done.2), channel_id=1, source_target_pairs={{0,1},{1,0},{2,3},{3,2},{4,5},{5,4},{6,7},{7,6},{8,9},{9,8},{10,11... | collective-permute-start | bytes 430088 | tf_op jit(solution)/shard_map/ppermute | solution.py:429
  82.8 1.4 %collective-permute-start.12 = (f32[280,128]{1,0:T(8,128)S(1)}, f32[280,128]{1,0:T(8,128)S(1)}, u32[]{:S(2)}, u32[]{:S(2)}) collective-permute-start(f32[280,128]{1,0:T(8,128)S(1)} %collective-permute-done.11.far_ref), channel_id=1, source_target_pairs={{0,1},{1,0},{2,3},{3,2},{4,5},{5,4},{6,7},{7,6},{8,9},{9,8},{10,11... | collective-permute-start | bytes 430088 | tf_op jit(solution)/shard_map/ppermute | solution.py:430
  84.2 3.7 %fusion.9 = bf16[1,8,16,5632]{3,2,1,0:T(8,128)(2,1)} fusion(f32[10,18,5632]{2,1,0:T(8,128)S(1)} %maximum_multiply_fusion, f32[5632]{0:T(1024)S(1)} %copy-done.12, f32[5632]{0:T(1024)S(1)} %copy-done.13, f32[5632]{0:T(1024)S(1)} %copy-done.6, f32[5632]{0:T(1024)S(1)} %copy-done.7, f32[5632]{0:T(1024)S(1)} %copy-done.8, f32[5632]{0:T(1024)S(1)} %copy-done.9, ...), kind=kLoop, calls=%fused_computation.25 | loop fusion | flops 12976128 | bytes 27596800 | tf_op jit(solution)/shard_map/convert_element_type | solution.py:452
  88.6 1.9 %shard_map.107 = bf16[128,1120]{1,0:T(8,128)(2,1)} custom-call(bf16[5,128,128]{2,1,0:T(8,128)(2,1)} %get-tuple-element.28.mine_ref, bf16[5,128,128]{2,1,0:T(8,128)(2,1)} %copy-done.14), custom_call_target="tpu_custom_call" | custom-call | bytes 573440 | tf_op jit(solution)/shard_map/pallas_call | solution.py:425
  91.8 2.8 %shard_map.109 = (bf16[128,1120]{1,0:T(8,128)(2,1)}, bf16[128,1120]{1,0:T(8,128)(2,1)}) custom-call(bf16[128,1120]{1,0:T(8,128)(2,1)} %bitcast.12, bf16[128,1120]{1,0:T(8,128)(2,1)} %bitcast.14, f32[280,128]{1,0:T(8,128)} %shard_map.108.near_ref, f32[280,128]{1,0:T(8,128)} %copy-done.16, f32[280,128]{1,0:T(8,128)} %copy-done.15, f32[280,128]{1,0:T(8,128)} %copy-done.17), custom_call_target="tpu_custom_call" | custom-call | flops 146800640 | bytes 1146880 | tf_op jit(solution)/shard_map/pallas_call | solution.py:432
  (78 shorter events, 7.3 us)
Async XLA Ops:
  0.6 14.8 %copy-start.1 = (bf16[1,8,16,5632]{3,2,1,0:T(8,128)(2,1)S(1)}, bf16[1,8,16,5632]{3,2,1,0:T(8,128)(2,1)}, u32[]{:S(2)}) copy-start(bf16[1,8,16,5632]{3,2,1,0:T(8,128)(2,1)} %param.12) | copy-start | bytes 4325380
  1.9 13.5 %collective-permute-start.13 = (bf16[1,2,16,5632]{3,2,1,0:T(8,128)(2,1)S(1)}, bf16[1,2,16,5632]{3,2,1,0:T(8,128)(2,1)S(1)}, u32[]{:S(2)}, u32[]{:S(2)}) collective-permute-start(bf16[1,2,16,5632]{3,2,1,0:T(8,128)(2,1)S(1)} %get-tuple-element.50), channel_id=1, source_target_pairs={{0,2},{1,3},{4,6},{5,7},{8,10},{9,11},{12,14},{13,15},{16,18},{17,... | collective-permute-start | bytes 1081352 | tf_op jit(solution)/shard_map/ppermute | solution.py:41
  8.5 2.4 %collective-permute-start = (f32[2,280,128]{2,1,0:T(8,128)}, f32[2,280,128]{2,1,0:T(8,128)S(1)}, u32[]{:S(2)}, u32[]{:S(2)}) collective-permute-start(f32[2,280,128]{2,1,0:T(8,128)} %get-tuple-element.22), channel_id=1, source_target_pairs={{0,1},{1,0},{2,3},{3,2},{4,5},{5,4},{6,7},{7,6},{8,9},{9,8},{10,11... | collective-permute-start | bytes 860168 | tf_op jit(solution)/shard_map/ppermute | solution.py:391
  9.5 11.9 %collective-permute-start.14 = (bf16[1,2,16,5632]{3,2,1,0:T(8,128)(2,1)S(1)}, bf16[1,2,16,5632]{3,2,1,0:T(8,128)(2,1)S(1)}, u32[]{:S(2)}, u32[]{:S(2)}) collective-permute-start(bf16[1,2,16,5632]{3,2,1,0:T(8,128)(2,1)S(1)} %get-tuple-element.49), channel_id=1, source_target_pairs={{2,0},{3,1},{6,4},{7,5},{10,8},{11,9},{14,12},{15,13},{18,16},{19,... | collective-permute-start | bytes 1081352 | tf_op jit(solution)/shard_map/ppermute | solution.py:44
  13.4 17.4 %copy-start.22 = (f32[280,128]{1,0:T(8,128)S(1)}, f32[280,128]{1,0:T(8,128)}, u32[]{:S(2)}) copy-start(f32[280,128]{1,0:T(8,128)} %get-tuple-element.23) | copy-start | bytes 430084
  13.4 17.4 %collective-permute-start.1 = (f32[280,128]{1,0:T(8,128)}, f32[280,128]{1,0:T(8,128)S(1)}, u32[]{:S(2)}, u32[]{:S(2)}) collective-permute-start(f32[280,128]{1,0:T(8,128)} %get-tuple-element.24), channel_id=1, source_target_pairs={{0,2},{2,0},{1,3},{3,1},{4,6},{6,4},{5,7},{7,5},{8,10},{10,8},{9,1... | collective-permute-start | bytes 430088 | tf_op jit(solution)/shard_map/ppermute | solution.py:393
  15.5 22.8 %copy-start.24 = (f32[9,5632]{1,0:T(8,128)S(1)}, f32[9,5632]{1,0:T(8,128)}, u32[]{:S(2)}) copy-start(f32[9,5632]{1,0:T(8,128)} %param.13) | copy-start | bytes 608260
  23.2 20.5 %collective-permute-start.15 = (bf16[1,12,2,5632]{3,2,1,0:T(2,128)(2,1)S(1)}, bf16[1,12,2,5632]{3,2,1,0:T(2,128)(2,1)S(1)}, u32[]{:S(2)}, u32[]{:S(2)}) collective-permute-start(bf16[1,12,2,5632]{3,2,1,0:T(2,128)(2,1)S(1)} %get-tuple-element.47), channel_id=1, source_target_pairs={{0,1},{2,3},{4,5},{6,7},{8,9},{10,11},{12,13},{14,15},{16,17},{18,... | collective-permute-start | bytes 811016 | tf_op jit(solution)/shard_map/ppermute | solution.py:41
  24.5 19.2 %collective-permute-start.16 = (bf16[1,12,2,5632]{3,2,1,0:T(2,128)(2,1)S(1)}, bf16[1,12,2,5632]{3,2,1,0:T(2,128)(2,1)}, u32[]{:S(2)}, u32[]{:S(2)}) collective-permute-start(bf16[1,12,2,5632]{3,2,1,0:T(2,128)(2,1)S(1)} %get-tuple-element.48), channel_id=1, source_target_pairs={{1,0},{3,2},{5,4},{7,6},{9,8},{11,10},{13,12},{15,14},{17,16},{19,... | collective-permute-start | bytes 811016 | tf_op jit(solution)/shard_map/ppermute | solution.py:44
  30.8 10.5 %copy-start.3 = (f32[280,128]{1,0:T(8,128)}, f32[280,128]{1,0:T(8,128)S(1)}, u32[]{:S(2)}) copy-start(f32[280,128]{1,0:T(8,128)S(1)} %add.90.own_ref) | copy-start | bytes 430084
  30.8 8.6 %collective-permute-start.2 = (f32[280,128]{1,0:T(8,128)S(1)}, f32[280,128]{1,0:T(8,128)S(1)}, u32[]{:S(2)}, u32[]{:S(2)}) collective-permute-start(f32[280,128]{1,0:T(8,128)S(1)} %add.90.own_ref), channel_id=1, source_target_pairs={{0,4},{4,8},{8,12},{1,5},{5,9},{9,13},{2,6},{6,10},{10,14},{3,7},{... | collective-permute-start | bytes 430088 | tf_op jit(solution)/shard_map/ppermute | solution.py:406
  34.0 7.3 %collective-permute-start.3 = (f32[280,128]{1,0:T(8,128)S(1)}, f32[280,128]{1,0:T(8,128)S(1)}, u32[]{:S(2)}, u32[]{:S(2)}) collective-permute-start(f32[280,128]{1,0:T(8,128)S(1)} %add.90.own_ref), channel_id=1, source_target_pairs={{0,8},{4,12},{1,9},{5,13},{2,10},{6,14},{3,11},{7,15},{16,24},{20,... | collective-permute-start | bytes 430088 | tf_op jit(solution)/shard_map/ppermute | solution.py:407
  39.4 9.5 %collective-permute-start.5 = (bf16[2,5,128,128]{3,2,1,0:T(8,128)(2,1)}, bf16[2,5,128,128]{3,2,1,0:T(8,128)(2,1)}, u32[]{:S(2)}, u32[]{:S(2)}) collective-permute-start(bf16[2,5,128,128]{3,2,1,0:T(8,128)(2,1)} %get-tuple-element.27), channel_id=1, source_target_pairs={{0,2},{2,0},{1,3},{3,1},{4,6},{6,4},{5,7},{7,5},{8,10},{10,8},{9,1... | collective-permute-start | bytes 983048 | tf_op jit(solution)/shard_map/ppermute | solution.py:402
  43.7 2.8 %collective-permute-start.4 = (f32[280,128]{1,0:T(8,128)}, f32[280,128]{1,0:T(8,128)}, u32[]{:S(2)}, u32[]{:S(2)}) collective-permute-start(f32[280,128]{1,0:T(8,128)} %shard_map.105.state_ref), channel_id=1, source_target_pairs={{0,1},{1,0},{2,3},{3,2},{4,5},{5,4},{6,7},{7,6},{8,9},{9,8},{10,11... | collective-permute-start | bytes 430088 | tf_op jit(solution)/shard_map/ppermute | solution.py:413
  53.8 7.3 %collective-permute-start.6 = (f32[280,128]{1,0:T(8,128)}, f32[280,128]{1,0:T(8,128)S(1)}, u32[]{:S(2)}, u32[]{:S(2)}) collective-permute-start(f32[280,128]{1,0:T(8,128)} %get-tuple-element.31), channel_id=1, source_target_pairs={{0,1},{1,0},{2,3},{3,2},{4,5},{5,4},{6,7},{7,6},{8,9},{9,8},{10,11... | collective-permute-start | bytes 430088 | tf_op jit(solution)/shard_map/ppermute | solution.py:420
  54.2 6.9 %copy-start.23 = (f32[280,128]{1,0:T(8,128)S(1)}, f32[280,128]{1,0:T(8,128)}, u32[]{:S(2)}) copy-start(f32[280,128]{1,0:T(8,128)} %get-tuple-element.30) | copy-start | bytes 430084
  61.1 5.7 %copy-start.4 = (f32[280,128]{1,0:T(8,128)}, f32[280,128]{1,0:T(8,128)S(1)}, u32[]{:S(2)}) copy-start(f32[280,128]{1,0:T(8,128)S(1)} %add.91.own_ref) | copy-start | bytes 430084
  61.1 7.1 %collective-permute-start.8 = (f32[280,128]{1,0:T(8,128)S(1)}, f32[280,128]{1,0:T(8,128)S(1)}, u32[]{:S(2)}, u32[]{:S(2)}) collective-permute-start(f32[280,128]{1,0:T(8,128)S(1)} %add.91.own_ref), channel_id=1, source_target_pairs={{4,0},{8,4},{12,8},{5,1},{9,5},{13,9},{6,2},{10,6},{14,10},{7,3},{... | collective-permute-start | bytes 430088 | tf_op jit(solution)/shard_map/ppermute | solution.py:406
  62.4 12.4 %collective-permute-start.9 = (f32[280,128]{1,0:T(8,128)S(1)}, f32[280,128]{1,0:T(8,128)S(1)}, u32[]{:S(2)}, u32[]{:S(2)}) collective-permute-start(f32[280,128]{1,0:T(8,128)S(1)} %add.91.own_ref), channel_id=1, source_target_pairs={{8,0},{12,4},{9,1},{13,5},{10,2},{14,6},{11,3},{15,7},{24,16},{28,... | collective-permute-start | bytes 430088 | tf_op jit(solution)/shard_map/ppermute | solution.py:407
  68.2 6.6 %copy-start.20 = (f32[280,128]{1,0:T(8,128)}, f32[280,128]{1,0:T(8,128)S(1)}, u32[]{:S(2)}) copy-start(f32[280,128]{1,0:T(8,128)S(1)} %collective-permute-done.8.near_ref) | copy-start | bytes 430084
  77.2 5.5 %collective-permute-start.11 = (f32[280,128]{1,0:T(8,128)}, f32[280,128]{1,0:T(8,128)S(1)}, u32[]{:S(2)}, u32[]{:S(2)}) collective-permute-start(f32[280,128]{1,0:T(8,128)} %shard_map.108.near_ref), channel_id=1, source_target_pairs={{0,2},{2,0},{1,3},{3,1},{4,6},{6,4},{5,7},{7,5},{8,10},{10,8},{9,1... | collective-permute-start | bytes 430088 | tf_op jit(solution)/shard_map/ppermute | solution.py:428
  77.3 6.9 %copy-start.6 = (f32[5632]{0:T(1024)S(1)}, f32[5632]{0:T(1024)}, u32[]{:S(2)}) copy-start(f32[5632]{0:T(1024)} %get-tuple-element.37) | copy-start | bytes 67588
  77.3 6.9 %copy-start.7 = (f32[5632]{0:T(1024)S(1)}, f32[5632]{0:T(1024)}, u32[]{:S(2)}) copy-start(f32[5632]{0:T(1024)} %get-tuple-element.38) | copy-start | bytes 67588
  77.3 6.9 %copy-start.8 = (f32[5632]{0:T(1024)S(1)}, f32[5632]{0:T(1024)}, u32[]{:S(2)}) copy-start(f32[5632]{0:T(1024)} %get-tuple-element.39) | copy-start | bytes 67588
  77.3 6.9 %copy-start.9 = (f32[5632]{0:T(1024)S(1)}, f32[5632]{0:T(1024)}, u32[]{:S(2)}) copy-start(f32[5632]{0:T(1024)} %get-tuple-element.40) | copy-start | bytes 67588
  77.3 6.9 %copy-start.10 = (f32[5632]{0:T(1024)S(1)}, f32[5632]{0:T(1024)}, u32[]{:S(2)}) copy-start(f32[5632]{0:T(1024)} %get-tuple-element.41) | copy-start | bytes 67588
  77.3 6.9 %copy-start.11 = (f32[5632]{0:T(1024)S(1)}, f32[5632]{0:T(1024)}, u32[]{:S(2)}) copy-start(f32[5632]{0:T(1024)} %get-tuple-element.42) | copy-start | bytes 67588
  77.3 6.9 %copy-start.12 = (f32[5632]{0:T(1024)S(1)}, f32[5632]{0:T(1024)}, u32[]{:S(2)}) copy-start(f32[5632]{0:T(1024)} %get-tuple-element.43) | copy-start | bytes 67588
  77.3 6.9 %copy-start.13 = (f32[5632]{0:T(1024)S(1)}, f32[5632]{0:T(1024)}, u32[]{:S(2)}) copy-start(f32[5632]{0:T(1024)} %get-tuple-element.44) | copy-start | bytes 67588
  79.9 8.0 %collective-permute-start.7 = (bf16[5,128,128]{2,1,0:T(8,128)(2,1)S(1)}, bf16[5,128,128]{2,1,0:T(8,128)(2,1)S(1)}, u32[]{:S(2)}, u32[]{:S(2)}) collective-permute-start(bf16[5,128,128]{2,1,0:T(8,128)(2,1)S(1)} %copy-done.25), channel_id=1, source_target_pairs={{0,2},{2,0},{1,3},{3,1},{4,6},{6,4},{5,7},{7,5},{8,10},{10,8},{9,1... | collective-permute-start | bytes 491528 | tf_op jit(solution)/shard_map/ppermute | solution.py:424
  81.4 9.1 %collective-permute-start.10 = (f32[280,128]{1,0:T(8,128)S(1)}, f32[280,128]{1,0:T(8,128)S(1)}, u32[]{:S(2)}, u32[]{:S(2)}) collective-permute-start(f32[280,128]{1,0:T(8,128)S(1)} %copy-done.2), channel_id=1, source_target_pairs={{0,1},{1,0},{2,3},{3,2},{4,5},{5,4},{6,7},{7,6},{8,9},{9,8},{10,11... | collective-permute-start | bytes 430088 | tf_op jit(solution)/shard_map/ppermute | solution.py:429
  82.8 7.8 %collective-permute-start.12 = (f32[280,128]{1,0:T(8,128)S(1)}, f32[280,128]{1,0:T(8,128)S(1)}, u32[]{:S(2)}, u32[]{:S(2)}) collective-permute-start(f32[280,128]{1,0:T(8,128)S(1)} %collective-permute-done.11.far_ref), channel_id=1, source_target_pairs={{0,1},{1,0},{2,3},{3,2},{4,5},{5,4},{6,7},{7,6},{8,9},{9,8},{10,11... | collective-permute-start | bytes 430088 | tf_op jit(solution)/shard_map/ppermute | solution.py:430
  (11 other events, 19.2 us)

commit v2 on v1

--- a/solution.py
+++ b/solution.py
@@ -220,7 +220,7 @@
     return jnp.where(column == 0, first, 0.0).astype(jnp.bfloat16)
 
 
-def vmem_call(kernel, out_shape, scratch=(), smem_first=False, n_in=0, flops=0, bytes_accessed=0, aliases=None):
+def vmem_call(kernel, out_shape, scratch=(), smem_first=False, n_in=0, flops=0, bytes_accessed=0, vmem_mib=8):
     vmem = pl.BlockSpec(memory_space=pltpu.VMEM)
     in_specs = [vmem] * n_in
     if smem_first:
@@ -232,6 +232,7 @@
         out_specs=jax.tree.map(lambda _: vmem, out_shape),
         scratch_shapes=list(scratch),
         cost_estimate=pl.CostEstimate(flops=flops, bytes_accessed=bytes_accessed, transcendentals=0),
+        compiler_params=pltpu.CompilerParams(vmem_limit_bytes=vmem_mib << 20),
     )
 
 
@@ -453,6 +454,183 @@
     return hidden_grad
 
 
+TILES = 8
+REACH = 2
+
+
+def conv_kernel(rows_per_frame, row_refs, *refs):
+    halo_rows, refs = refs[:row_refs], refs[row_refs:]
+    side_ref, refs = refs[0], refs[1:]
+    corners, refs = refs[:row_refs], refs[row_refs:]
+    block_ref, weight_ref, out_ref, taps, value_in, gate_in, value_grad, gate_grad, value_out, gate_out = refs
+    rows, cols, channels = block_ref.shape
+    lane_tiles = channels // LANES // 2
+    pitch = -(-lane_tiles // TILES) * TILES
+    row, column = lax.axis_index("height"), lax.axis_index("width")
+    first_row, last_row = row == 0, row == lax.axis_size("height") - 1
+    wide, tall = cols + 2 * REACH, rows + 2 * REACH
+    grad_wide = wide - 2
+
+    for tile in range(2 * lane_tiles):
+        place = tile if tile < lane_tiles else pitch + tile - lane_tiles
+        taps[pl.ds(place, 9, stride=2 * pitch), :] = weight_ref[:, tile * LANES : (tile + 1) * LANES]
+
+    def source_at(at_row, at_col):
+        return pl.multiple_of((at_row * wide + at_col) * TILES, TILES)
+
+    def grad_at(at_row, at_col):
+        return pl.multiple_of((at_row * grad_wide + at_col) * TILES, TILES)
+
+    zero = jnp.zeros((TILES, LANES), jnp.float32)
+    low_border = jnp.where(first_row, 0, rows + REACH)
+    outer_col = jnp.where(column == 0, 0, cols + REACH)
+    side_col = jnp.where(column == 0, cols + REACH, 0)
+    grad_outer_col = jnp.where(column == 0, 0, grad_wide - 1)
+    start_col = jnp.where(column == 0, REACH, REACH - 1)
+    low, high = jnp.where(first_row, REACH, REACH - 1), jnp.where(last_row, rows + REACH, rows + REACH + 1)
+
+    for ref in (value_in, gate_in):
+        @pl.loop(0, tall)
+        def _(at):
+            for extra in range(REACH):
+                ref[pl.ds(source_at(at, outer_col + extra), TILES), :] = zero
+
+    for ref in (value_grad, gate_grad):
+        @pl.loop(0, rows + 2)
+        def _(at):
+            ref[pl.ds(grad_at(at, grad_outer_col), TILES), :] = zero
+
+        for edge, at in ((first_row, 0), (last_row, rows + 1)):
+            @pl.when(edge)
+            def _():
+                for col in range(grad_wide):
+                    ref[pl.ds(grad_at(at, col), TILES), :] = zero
+
+    for base in range(0, lane_tiles, TILES):
+        count = min(TILES, lane_tiles - base)
+
+        def spread(load, at_row, at_col, length):
+            for ref, offset in ((value_in, base), (gate_in, lane_tiles + base)):
+                for tile in range(count):
+                    part = load(slice((offset + tile) * LANES, (offset + tile + 1) * LANES)).astype(jnp.float32)
+                    ref[pl.ds(source_at(at_row, at_col) + tile, length, stride=TILES), :] = part
+
+        @pl.loop(0, rows)
+        def _(at):
+            spread(lambda lanes: block_ref[at, :, lanes], at + REACH, REACH, cols)
+            spread(lambda lanes: side_ref[at, :, lanes], at + REACH, side_col, REACH)
+
+        for edge, at, which in ((first_row, 0, 0), (last_row, rows + REACH, row_refs - 1)):
+            rows_ref, corner_ref = halo_rows[which], corners[which]
+            for extra in range(REACH):
+                @pl.when(jnp.logical_not(edge))
+                def _():
+                    spread(lambda lanes: rows_ref[extra, :, lanes], at + extra, REACH, cols)
+                    spread(lambda lanes: corner_ref[extra, :, lanes], at + extra, side_col, REACH)
+
+                @pl.when(edge)
+                def _():
+                    for ref in (value_in, gate_in):
+                        for col in range(wide):
+                            ref[pl.ds(source_at(at + extra, col), TILES), :] = zero
+
+        def weights(offset):
+            return [taps[2 * pitch * tap + offset + base : 2 * pitch * tap + offset + base + TILES, :] for tap in range(9)]
+
+        value_taps, gate_taps = weights(0), weights(pitch)
+
+        @pl.loop(low, high)
+        def _(at):
+            cache = {}
+
+            def read(ref, a, col):
+                if (id(ref), a, col) not in cache:
+                    cache[id(ref), a, col] = ref[pl.ds(source_at(at + a, start_col + col), TILES), :]
+                return cache[id(ref), a, col]
+
+            for col in range(cols + 1):
+                def conv(ref, kernel):
+                    total = None
+                    for a in (-1, 0, 1):
+                        for b in (-1, 0, 1):
+                            term = kernel[3 * (a + 1) + b + 1] * read(ref, a, col + b)
+                            total = term if total is None else total + term
+                    return total
+
+                value, gate = conv(value_in, value_taps), conv(gate_in, gate_taps)
+                squash = jax.nn.sigmoid(gate)
+                gated = gate * squash
+                glu = value * gated
+                place = pl.ds(grad_at(at - 1, start_col + col - 1), TILES)
+                value_grad[place, :] = glu * gated
+                gate_grad[place, :] = glu * value * (squash + gated * (1.0 - squash))
+
+        @pl.loop(0, rows)
+        def _(at):
+            for ref, kernel, result in ((value_grad, value_taps, value_out), (gate_grad, gate_taps, gate_out)):
+                cache = {}
+
+                def read(a, col):
+                    if (a, col) not in cache:
+                        cache[a, col] = ref[pl.ds(grad_at(at + a, col), TILES), :]
+                    return cache[a, col]
+
+                for col in range(cols):
+                    total = None
+                    for a in (-1, 0, 1):
+                        for b in (-1, 0, 1):
+                            term = kernel[3 * (a + 1) + b + 1] * read(1 - a, col + 1 - b)
+                            total = term if total is None else total + term
+                    result[col * TILES : (col + 1) * TILES, :] = total
+            for result, offset in ((value_out, base), (gate_out, lane_tiles + base)):
+                for tile in range(count):
+                    lanes = slice((offset + tile) * LANES, (offset + tile + 1) * LANES)
+                    out_ref[at, :, lanes] = result[pl.ds(tile, cols, stride=TILES), :].astype(jnp.bfloat16)
+
+
+def edge_slice(block, axis_name, dim, low_side):
+    start = jnp.where(low_side, 0, block.shape[dim] - REACH)
+    return lax.dynamic_slice_in_dim(block, start, REACH, axis=dim)
+
+
+def halo_arrays(hidden_pre):
+    block = hidden_pre[0]
+    height = lax.axis_size("height")
+    column = lax.axis_index("width")
+    if height == 2:
+        edge = edge_slice(block, "height", 0, lax.axis_index("height") == 1)
+        halo_rows = [lax.ppermute(edge, "height", SWAP)]
+    else:
+        up = [(at, at + 1) for at in range(height - 1)]
+        down = [(at + 1, at) for at in range(height - 1)]
+        halo_rows = [
+            lax.ppermute(block[block.shape[0] - REACH :], "height", up),
+            lax.ppermute(block[:REACH], "height", down),
+        ]
+    side = lax.ppermute(edge_slice(block, "width", 1, column == 1), "width", SWAP)
+    corners = [lax.ppermute(edge_slice(part, "width", 1, column == 1), "width", SWAP) for part in halo_rows]
+    return halo_rows, side, corners
+
+
+def paired_ffn(hidden_pre, conv_weight):
+    halo_rows, side, corners = halo_arrays(hidden_pre)
+    block = hidden_pre[0]
+    rows, cols, channels = block.shape
+    lane_tiles = channels // LANES // 2
+    pitch = -(-lane_tiles // TILES) * TILES
+    source = pltpu.VMEM(((rows + 2 * REACH) * (cols + 2 * REACH) * TILES, LANES), jnp.float32)
+    grad = pltpu.VMEM(((rows + 2) * (cols + 2) * TILES, LANES), jnp.float32)
+    result = pltpu.VMEM((cols * TILES, LANES), jnp.float32)
+    size = rows * cols * channels
+    hidden_grad = vmem_call(
+        functools.partial(conv_kernel, rows, len(halo_rows)),
+        struct((rows, cols, channels), jnp.bfloat16),
+        [pltpu.VMEM((9 * 2 * pitch, LANES), jnp.float32), source, source, grad, grad, result, result],
+        n_in=2 * len(halo_rows) + 3, flops=60 * size, bytes_accessed=6 * size,
+    )(*halo_rows, side, *corners, block, conv_weight)
+    return hidden_grad[None]
+
+
 def per_device(queries, attn_keys, attn_values, attn_cotangent, clip_ids, hidden_pre, conv_weight):
     paired = (
         lax.axis_size("height") == 2
@@ -463,7 +641,8 @@
     )
     attention = paired_attention if paired else general_attention
     grads = attention(queries, attn_keys, attn_values, attn_cotangent, clip_ids)
-    return (*grads, mixed_ffn(hidden_pre, conv_weight))
+    hidden_grad = paired_ffn(hidden_pre, conv_weight) if lax.axis_size("width") == 2 and hidden_pre.shape[0] == 1 and hidden_pre.shape[3] % (2 * LANES) == 0 else mixed_ffn(hidden_pre, conv_weight)
+    return (*grads, hidden_grad)
 
 
 def solution(mesh):

time: 95.2 us -> 65.6 us (0.69)
  the two profiles are of different devices: /device:TPU:1 before, /device:TPU:9 now
where the time goes in v2:
time: 65.6 us; the launch traced here: 65.3 us
  waiting for transfers between devices  24 us (37%)
  starting transfers between devices  20.6 us (31%)
  Pallas kernels  15.6 us (24%)
  local copies, waits for them, and re-layouts  4.14 us (6%)
  between operations  0.78 us (1%)
    ppermute x2, waiting for transfers between devices, along_frames(): near = lax.ppermute(own, 'tm', moves[0])  8.71 us
    ppermute x2, waiting for transfers between devices, along_frames(): far = lax.ppermute(own, 'tm', moves[1])  8.39 us
    pallas_call x1, Pallas kernels, paired_ffn(): vmem_call(functools.partial(conv_kernel, rows, len(halo_rows)), struct((r...  7.66 us
    ppermute x2, starting transfers between devices, along_frames(): far = lax.ppermute(own, 'tm', moves[1])  5.5 us
    unnamed x18, local copies, waits for them, and re-layouts  3.86 us
    ppermute x2, starting transfers between devices, along_frames(): near = lax.ppermute(own, 'tm', moves[0])  3.84 us
    ppermute x1, starting transfers between devices, paired_attention(): far_came = lax.ppermute(far, 'width', SWAP)  3.14 us
    pallas_call x1, Pallas kernels, paired_attention(): vmem_call(query_kernel, (share, share, back, back), [pltpu.VMEM((2, half,...  2.98 us
  transfers between devices with their start and end apart: 16, of which 10 were waited for; matrix products, arithmetic and copies ran while one was open for 0% of the time, Pallas kernels for 16%

profile of v2, /device:TPU:9, one launch (start us, length us, event | category | flops | bytes accessed | tf_op | source)
XLA Modules:
  0.0 65.3 jit_solution(13151640795970373772)
XLA Ops:
  0.7 1.0 %copy-done.1 = bf16[1,8,16,1120]{3,2,1,0:T(8,128)(2,1)S(1)} copy-done((bf16[1,8,16,1120]{3,2,1,0:T(8,128)(2,1)S(1)}, bf16[1,8,16,1120]{3,2,1,0:T(8,128)(2,1)}, u32[]{:S(2)}) %copy-start.1) | copy-done | bytes 286744
  1.6 1.0 %copy-done.3 = bf16[1,8,16,1120]{3,2,1,0:T(8,128)(2,1)S(1)} copy-done((bf16[1,8,16,1120]{3,2,1,0:T(8,128)(2,1)S(1)}, bf16[1,8,16,1120]{3,2,1,0:T(8,128)(2,1)}, u32[]{:S(2)}) %copy-start.3) | copy-done | bytes 286744
  2.6 0.8 %shard_map.103 = (f32[2,280,128]{2,1,0:T(8,128)S(1)}, f32[2,280,128]{2,1,0:T(8,128)S(1)}) custom-call(bf16[128,1120]{1,0:T(8,128)(2,1)S(1)} %bitcast.14, bf16[128,1120]{1,0:T(8,128)(2,1)S(1)} %bitcast.16), custom_call_target="tpu_custom_call" | custom-call | flops 36700160 | bytes 1146880 | tf_op jit(solution)/shard_map/pallas_call | solution.py:388
  3.4 0.7 %collective-permute-start = (f32[2,280,128]{2,1,0:T(8,128)S(1)}, f32[2,280,128]{2,1,0:T(8,128)S(1)}, u32[]{:S(2)}, u32[]{:S(2)}) collective-permute-start(f32[2,280,128]{2,1,0:T(8,128)S(1)} %get-tuple-element.22), channel_id=1, source_target_pairs={{0,1},{1,0},{2,3},{3,2},{4,5},{5,4},{6,7},{7,6},{8,9},{9,8},{10,11... | collective-permute-start | bytes 860168 | tf_op jit(solution)/shard_map/ppermute | solution.py:392
  4.1 1.2 %collective-permute-done.came_ref = f32[2,280,128]{2,1,0:T(8,128)S(1)} collective-permute-done((f32[2,280,128]{2,1,0:T(8,128)S(1)}, f32[2,280,128]{2,1,0:T(8,128)S(1)}, u32[]{:S(2)}, u32[]{:S(2)}) %collective-permute-start) | collective-permute-done | bytes 286752 | tf_op jit(solution)/shard_map/ppermute | solution.py:392
  5.3 1.3 %collective-permute-start.1 = (f32[280,128]{1,0:T(8,128)S(1)}, f32[280,128]{1,0:T(8,128)S(1)}, u32[]{:S(2)}, u32[]{:S(2)}) collective-permute-start(f32[280,128]{1,0:T(8,128)S(1)} %get-tuple-element.24), channel_id=1, source_target_pairs={{0,2},{2,0},{1,3},{3,1},{4,6},{6,4},{5,7},{7,5},{8,10},{10,8},{9,1... | collective-permute-start | bytes 430088 | tf_op jit(solution)/shard_map/ppermute | solution.py:394
  6.6 1.0 %copy-done.6 = bf16[1,8,16,1120]{3,2,1,0:T(8,128)(2,1)S(1)} copy-done((bf16[1,8,16,1120]{3,2,1,0:T(8,128)(2,1)S(1)}, bf16[1,8,16,1120]{3,2,1,0:T(8,128)(2,1)}, u32[]{:S(2)}) %copy-start.6) | copy-done | bytes 286744
  7.6 1.0 %copy-done.7 = bf16[1,8,16,1120]{3,2,1,0:T(8,128)(2,1)S(1)} copy-done((bf16[1,8,16,1120]{3,2,1,0:T(8,128)(2,1)S(1)}, bf16[1,8,16,1120]{3,2,1,0:T(8,128)(2,1)}, u32[]{:S(2)}) %copy-start.7) | copy-done | bytes 286744
  9.0 1.4 %collective-permute-done.1 = f32[280,128]{1,0:T(8,128)S(1)} collective-permute-done((f32[280,128]{1,0:T(8,128)S(1)}, f32[280,128]{1,0:T(8,128)S(1)}, u32[]{:S(2)}, u32[]{:S(2)}) %collective-permute-start.1) | collective-permute-done | bytes 143392 | tf_op jit(solution)/shard_map/ppermute | solution.py:394
  10.4 1.3 %collective-permute-start.5 = (bf16[2,5,128,128]{3,2,1,0:T(8,128)(2,1)S(1)}, bf16[2,5,128,128]{3,2,1,0:T(8,128)(2,1)S(1)}, u32[]{:S(2)}, u32[]{:S(2)}) collective-permute-start(bf16[2,5,128,128]{3,2,1,0:T(8,128)(2,1)S(1)} %get-tuple-element.27), channel_id=1, source_target_pairs={{0,2},{2,0},{1,3},{3,1},{4,6},{6,4},{5,7},{7,5},{8,10},{10,8},{9,1... | collective-permute-start | bytes 983048 | tf_op jit(solution)/shard_map/ppermute | solution.py:403
  11.7 4.2 %collective-permute-start.3 = (f32[280,128]{1,0:T(8,128)S(1)}, f32[280,128]{1,0:T(8,128)S(1)}, u32[]{:S(2)}, u32[]{:S(2)}) collective-permute-start(f32[280,128]{1,0:T(8,128)S(1)} %add.4.own_ref), channel_id=1, source_target_pairs={{0,8},{4,12},{1,9},{5,13},{2,10},{6,14},{3,11},{7,15},{16,24},{20,... | collective-permute-start | bytes 430088 | tf_op jit(solution)/shard_map/ppermute | solution.py:408
  15.9 1.9 %collective-permute-start.2 = (f32[280,128]{1,0:T(8,128)S(1)}, f32[280,128]{1,0:T(8,128)S(1)}, u32[]{:S(2)}, u32[]{:S(2)}) collective-permute-start(f32[280,128]{1,0:T(8,128)S(1)} %add.4.own_ref), channel_id=1, source_target_pairs={{0,4},{4,8},{8,12},{1,5},{5,9},{9,13},{2,6},{6,10},{10,14},{3,7},{... | collective-permute-start | bytes 430088 | tf_op jit(solution)/shard_map/ppermute | solution.py:407
  17.8 4.2 %collective-permute-done.3.far_ref = f32[280,128]{1,0:T(8,128)S(1)} collective-permute-done((f32[280,128]{1,0:T(8,128)S(1)}, f32[280,128]{1,0:T(8,128)S(1)}, u32[]{:S(2)}, u32[]{:S(2)}) %collective-permute-start.3) | collective-permute-done | bytes 143392 | tf_op jit(solution)/shard_map/ppermute | solution.py:408
  22.0 3.1 %collective-permute-done.2.near_ref = f32[280,128]{1,0:T(8,128)S(1)} collective-permute-done((f32[280,128]{1,0:T(8,128)S(1)}, f32[280,128]{1,0:T(8,128)S(1)}, u32[]{:S(2)}, u32[]{:S(2)}) %collective-permute-start.2) | collective-permute-done | bytes 143392 | tf_op jit(solution)/shard_map/ppermute | solution.py:407
  25.0 0.6 shard_map.105.state_ref
  25.6 0.9 %collective-permute-start.4 = (f32[280,128]{1,0:T(8,128)S(1)}, f32[280,128]{1,0:T(8,128)S(1)}, u32[]{:S(2)}, u32[]{:S(2)}) collective-permute-start(f32[280,128]{1,0:T(8,128)S(1)} %shard_map.105.state_ref), channel_id=1, source_target_pairs={{0,1},{1,0},{2,3},{3,2},{4,5},{5,4},{6,7},{7,6},{8,9},{9,8},{10,11... | collective-permute-start | bytes 430088 | tf_op jit(solution)/shard_map/ppermute | solution.py:414
  26.6 1.0 %collective-permute-done.4.came_ref = f32[280,128]{1,0:T(8,128)S(1)} collective-permute-done((f32[280,128]{1,0:T(8,128)S(1)}, f32[280,128]{1,0:T(8,128)S(1)}, u32[]{:S(2)}, u32[]{:S(2)}) %collective-permute-start.4) | collective-permute-done | bytes 143392 | tf_op jit(solution)/shard_map/ppermute | solution.py:414
  27.6 3.0 %shard_map.106 = (f32[280,128]{1,0:T(8,128)S(1)}, f32[280,128]{1,0:T(8,128)S(1)}, bf16[5,128,128]{2,1,0:T(8,128)(2,1)S(1)}, bf16[5,128,128]{2,1,0:T(8,128)(2,1)S(1)}) custom-call(f32[280,128]{1,0:T(8,128)S(1)} %shard_map.105.state_ref, f32[280,128]{1,0:T(8,128)S(1)} %collective-permute-done.4.came_ref, ...), custom_call_target="tpu_custom_call" | custom-call | flops 256901120 | bytes 1146880 | tf_op jit(solution)/shard_map/pallas_call | solution.py:416
  31.0 1.0 %collective-permute-done.6 = f32[280,128]{1,0:T(8,128)S(1)} collective-permute-done((f32[280,128]{1,0:T(8,128)S(1)}, f32[280,128]{1,0:T(8,128)S(1)}, u32[]{:S(2)}, u32[]{:S(2)}) %collective-permute-start.6) | collective-permute-done | bytes 143392 | tf_op jit(solution)/shard_map/ppermute | solution.py:421
  32.0 1.3 %collective-permute-start.9 = (f32[280,128]{1,0:T(8,128)S(1)}, f32[280,128]{1,0:T(8,128)S(1)}, u32[]{:S(2)}, u32[]{:S(2)}) collective-permute-start(f32[280,128]{1,0:T(8,128)S(1)} %add.10.own_ref), channel_id=1, source_target_pairs={{8,0},{12,4},{9,1},{13,5},{10,2},{14,6},{11,3},{15,7},{24,16},{28,... | collective-permute-start | bytes 430088 | tf_op jit(solution)/shard_map/ppermute | solution.py:408
  33.3 1.9 %collective-permute-start.8 = (f32[280,128]{1,0:T(8,128)S(1)}, f32[280,128]{1,0:T(8,128)S(1)}, u32[]{:S(2)}, u32[]{:S(2)}) collective-permute-start(f32[280,128]{1,0:T(8,128)S(1)} %add.10.own_ref), channel_id=1, source_target_pairs={{4,0},{8,4},{12,8},{5,1},{9,5},{13,9},{6,2},{10,6},{14,10},{7,3},{... | collective-permute-start | bytes 430088 | tf_op jit(solution)/shard_map/ppermute | solution.py:407
  35.6 4.2 %collective-permute-done.9.far_ref = f32[280,128]{1,0:T(8,128)S(1)} collective-permute-done((f32[280,128]{1,0:T(8,128)S(1)}, f32[280,128]{1,0:T(8,128)S(1)}, u32[]{:S(2)}, u32[]{:S(2)}) %collective-permute-start.9) | collective-permute-done | bytes 143392 | tf_op jit(solution)/shard_map/ppermute | solution.py:408
  39.8 5.6 %collective-permute-done.8.near_ref = f32[280,128]{1,0:T(8,128)S(1)} collective-permute-done((f32[280,128]{1,0:T(8,128)S(1)}, f32[280,128]{1,0:T(8,128)S(1)}, u32[]{:S(2)}, u32[]{:S(2)}) %collective-permute-start.8) | collective-permute-done | bytes 143392 | tf_op jit(solution)/shard_map/ppermute | solution.py:407
  45.5 0.6 shard_map.108.near_ref
  46.6 1.2 %collective-permute-start.14 = (bf16[8,2,5632]{2,1,0:T(2,128)(2,1)S(1)}, bf16[8,2,5632]{2,1,0:T(2,128)(2,1)S(1)}, u32[]{:S(2)}, u32[]{:S(2)}) collective-permute-start(bf16[8,2,5632]{2,1,0:T(2,128)(2,1)S(1)} %dynamic-slice_bitcast_fusion.1), channel_id=1, source_target_pairs={{0,1},{1,0},{2,3},{3,2},{4,5},{5,4},{6,7},{7,6},{8,9},{9,8},{10,11... | collective-permute-start | bytes 540680 | tf_op jit(solution)/shard_map/ppermute | solution.py:610
  47.8 1.2 %collective-permute-start.7 = (bf16[5,128,128]{2,1,0:T(8,128)(2,1)S(1)}, bf16[5,128,128]{2,1,0:T(8,128)(2,1)S(1)}, u32[]{:S(2)}, u32[]{:S(2)}) collective-permute-start(bf16[5,128,128]{2,1,0:T(8,128)(2,1)S(1)} %get-tuple-element.32), channel_id=1, source_target_pairs={{0,2},{2,0},{1,3},{3,1},{4,6},{6,4},{5,7},{7,5},{8,10},{10,8},{9,1... | collective-permute-start | bytes 491528 | tf_op jit(solution)/shard_map/ppermute | solution.py:425
  49.4 1.2 %collective-permute-done.11.far_ref = f32[280,128]{1,0:T(8,128)S(1)} collective-permute-done((f32[280,128]{1,0:T(8,128)S(1)}, f32[280,128]{1,0:T(8,128)S(1)}, u32[]{:S(2)}, u32[]{:S(2)}) %collective-permute-start.11) | collective-permute-done | bytes 143392 | tf_op jit(solution)/shard_map/ppermute | solution.py:429
  50.5 3.1 %collective-permute-start.12 = (f32[280,128]{1,0:T(8,128)S(1)}, f32[280,128]{1,0:T(8,128)S(1)}, u32[]{:S(2)}, u32[]{:S(2)}) collective-permute-start(f32[280,128]{1,0:T(8,128)S(1)} %collective-permute-done.11.far_ref), channel_id=1, source_target_pairs={{0,1},{1,0},{2,3},{3,2},{4,5},{5,4},{6,7},{7,6},{8,9},{9,8},{10,11... | collective-permute-start | bytes 430088 | tf_op jit(solution)/shard_map/ppermute | solution.py:431
  53.8 1.2 %collective-permute-done.15.refs_2_ = bf16[2,2,5632]{2,1,0:T(2,128)(2,1)S(1)} collective-permute-done((bf16[2,2,5632]{2,1,0:T(2,128)(2,1)S(1)}, bf16[2,2,5632]{2,1,0:T(2,128)(2,1)S(1)}, u32[]{:S(2)}, u32[]{:S(2)}) %collective-permute-start.15) | collective-permute-done | bytes 45088 | tf_op jit(solution)/shard_map/ppermute | solution.py:611
  55.0 7.7 %shard_map.110 = bf16[8,16,5632]{2,1,0:T(8,128)(2,1)} custom-call(bf16[2,16,5632]{2,1,0:T(8,128)(2,1)S(1)} %collective-permute-done.13.refs_0_, bf16[8,2,5632]{2,1,0:T(2,128)(2,1)S(1)} %collective-permute-done.14.refs_1_, bf16[2,2,5632]{2,1,0:T(2,128)(2,1)S(1)} %collective-permute-done.15.refs_2_, bf16[8,16,5632]{2,1,0:T(8,128)(2,1)S(1)} %bitcast.13, ...), custom_call_target="tpu_custom_call" | custom-call | flops 43253760 | bytes 4325376 | tf_op jit(solution)/shard_map/pallas_call | solution.py:625
  62.7 0.9 %shard_map.107 = bf16[128,1120]{1,0:T(8,128)(2,1)} custom-call(bf16[5,128,128]{2,1,0:T(8,128)(2,1)S(1)} %get-tuple-element.28.mine_ref, bf16[5,128,128]{2,1,0:T(8,128)(2,1)S(1)} %collective-permute-done.7.came_ref), custom_call_target="tpu_custom_call" | custom-call | bytes 573440 | tf_op jit(solution)/shard_map/pallas_call | solution.py:426
  63.6 1.6 %shard_map.109 = (bf16[128,1120]{1,0:T(8,128)(2,1)}, bf16[128,1120]{1,0:T(8,128)(2,1)}) custom-call(bf16[128,1120]{1,0:T(8,128)(2,1)S(1)} %bitcast.15, bf16[128,1120]{1,0:T(8,128)(2,1)S(1)} %bitcast.17, f32[280,128]{1,0:T(8,128)S(1)} %shard_map.108.near_ref, f32[280,128]{1,0:T(8,128)S(1)} %collective-permute-done.10.near_came_ref, ...), custom_call_target="tpu_custom_call" | custom-call | flops 146800640 | bytes 1146880 | tf_op jit(solution)/shard_map/pallas_call | solution.py:433
  (32 shorter events, 2.3 us)
Async XLA Ops:
  0.6 24.4 %copy-start.8 = (s32[4]{0:T(128)S(1)}, s32[4]{0:T(128)}, u32[]{:S(2)}) copy-start(s32[4]{0:T(128)} %clip_ref.3) | copy-start | bytes 52
  0.6 1.0 %copy-start.1 = (bf16[1,8,16,1120]{3,2,1,0:T(8,128)(2,1)S(1)}, bf16[1,8,16,1120]{3,2,1,0:T(8,128)(2,1)}, u32[]{:S(2)}) copy-start(bf16[1,8,16,1120]{3,2,1,0:T(8,128)(2,1)} %param.8) | copy-start | bytes 860164
  1.6 1.0 %copy-start.3 = (bf16[1,8,16,1120]{3,2,1,0:T(8,128)(2,1)S(1)}, bf16[1,8,16,1120]{3,2,1,0:T(8,128)(2,1)}, u32[]{:S(2)}) copy-start(bf16[1,8,16,1120]{3,2,1,0:T(8,128)(2,1)} %param.9) | copy-start | bytes 860164
  3.4 1.9 %collective-permute-start = (f32[2,280,128]{2,1,0:T(8,128)S(1)}, f32[2,280,128]{2,1,0:T(8,128)S(1)}, u32[]{:S(2)}, u32[]{:S(2)}) collective-permute-start(f32[2,280,128]{2,1,0:T(8,128)S(1)} %get-tuple-element.22), channel_id=1, source_target_pairs={{0,1},{1,0},{2,3},{3,2},{4,5},{5,4},{6,7},{7,6},{8,9},{9,8},{10,11... | collective-permute-start | bytes 860168 | tf_op jit(solution)/shard_map/ppermute | solution.py:392
  5.3 5.0 %collective-permute-start.1 = (f32[280,128]{1,0:T(8,128)S(1)}, f32[280,128]{1,0:T(8,128)S(1)}, u32[]{:S(2)}, u32[]{:S(2)}) collective-permute-start(f32[280,128]{1,0:T(8,128)S(1)} %get-tuple-element.24), channel_id=1, source_target_pairs={{0,2},{2,0},{1,3},{3,1},{4,6},{6,4},{5,7},{7,5},{8,10},{10,8},{9,1... | collective-permute-start | bytes 430088 | tf_op jit(solution)/shard_map/ppermute | solution.py:394
  6.6 1.0 %copy-start.6 = (bf16[1,8,16,1120]{3,2,1,0:T(8,128)(2,1)S(1)}, bf16[1,8,16,1120]{3,2,1,0:T(8,128)(2,1)}, u32[]{:S(2)}) copy-start(bf16[1,8,16,1120]{3,2,1,0:T(8,128)(2,1)} %param.7) | copy-start | bytes 860164
  7.6 1.0 %copy-start.7 = (bf16[1,8,16,1120]{3,2,1,0:T(8,128)(2,1)S(1)}, bf16[1,8,16,1120]{3,2,1,0:T(8,128)(2,1)}, u32[]{:S(2)}) copy-start(bf16[1,8,16,1120]{3,2,1,0:T(8,128)(2,1)} %param.10) | copy-start | bytes 860164
  8.5 26.7 %copy-start = (bf16[1,8,16,5632]{3,2,1,0:T(8,128)(2,1)S(1)}, bf16[1,8,16,5632]{3,2,1,0:T(8,128)(2,1)}, u32[]{:S(2)}) copy-start(bf16[1,8,16,5632]{3,2,1,0:T(8,128)(2,1)} %param.12) | copy-start | bytes 4325380
  10.4 17.2 %collective-permute-start.5 = (bf16[2,5,128,128]{3,2,1,0:T(8,128)(2,1)S(1)}, bf16[2,5,128,128]{3,2,1,0:T(8,128)(2,1)S(1)}, u32[]{:S(2)}, u32[]{:S(2)}) collective-permute-start(bf16[2,5,128,128]{3,2,1,0:T(8,128)(2,1)S(1)} %get-tuple-element.27), channel_id=1, source_target_pairs={{0,2},{2,0},{1,3},{3,1},{4,6},{6,4},{5,7},{7,5},{8,10},{10,8},{9,1... | collective-permute-start | bytes 983048 | tf_op jit(solution)/shard_map/ppermute | solution.py:403
  11.7 10.3 %collective-permute-start.3 = (f32[280,128]{1,0:T(8,128)S(1)}, f32[280,128]{1,0:T(8,128)S(1)}, u32[]{:S(2)}, u32[]{:S(2)}) collective-permute-start(f32[280,128]{1,0:T(8,128)S(1)} %add.4.own_ref), channel_id=1, source_target_pairs={{0,8},{4,12},{1,9},{5,13},{2,10},{6,14},{3,11},{7,15},{16,24},{20,... | collective-permute-start | bytes 430088 | tf_op jit(solution)/shard_map/ppermute | solution.py:408
  15.9 9.2 %collective-permute-start.2 = (f32[280,128]{1,0:T(8,128)S(1)}, f32[280,128]{1,0:T(8,128)S(1)}, u32[]{:S(2)}, u32[]{:S(2)}) collective-permute-start(f32[280,128]{1,0:T(8,128)S(1)} %add.4.own_ref), channel_id=1, source_target_pairs={{0,4},{4,8},{8,12},{1,5},{5,9},{9,13},{2,6},{6,10},{10,14},{3,7},{... | collective-permute-start | bytes 430088 | tf_op jit(solution)/shard_map/ppermute | solution.py:407
  25.6 1.9 %collective-permute-start.4 = (f32[280,128]{1,0:T(8,128)S(1)}, f32[280,128]{1,0:T(8,128)S(1)}, u32[]{:S(2)}, u32[]{:S(2)}) collective-permute-start(f32[280,128]{1,0:T(8,128)S(1)} %shard_map.105.state_ref), channel_id=1, source_target_pairs={{0,1},{1,0},{2,3},{3,2},{4,5},{5,4},{6,7},{7,6},{8,9},{9,8},{10,11... | collective-permute-start | bytes 430088 | tf_op jit(solution)/shard_map/ppermute | solution.py:414
  27.6 27.5 %copy-start.5 = (f32[9,5632]{1,0:T(8,128)S(1)}, f32[9,5632]{1,0:T(8,128)}, u32[]{:S(2)}) copy-start(f32[9,5632]{1,0:T(8,128)} %refs_4_.1) | copy-start | bytes 608260
  30.6 1.4 %collective-permute-start.6 = (f32[280,128]{1,0:T(8,128)S(1)}, f32[280,128]{1,0:T(8,128)S(1)}, u32[]{:S(2)}, u32[]{:S(2)}) collective-permute-start(f32[280,128]{1,0:T(8,128)S(1)} %get-tuple-element.31), channel_id=1, source_target_pairs={{0,1},{1,0},{2,3},{3,2},{4,5},{5,4},{6,7},{7,6},{8,9},{9,8},{10,11... | collective-permute-start | bytes 430088 | tf_op jit(solution)/shard_map/ppermute | solution.py:421
  32.0 7.8 %collective-permute-start.9 = (f32[280,128]{1,0:T(8,128)S(1)}, f32[280,128]{1,0:T(8,128)S(1)}, u32[]{:S(2)}, u32[]{:S(2)}) collective-permute-start(f32[280,128]{1,0:T(8,128)S(1)} %add.10.own_ref), channel_id=1, source_target_pairs={{8,0},{12,4},{9,1},{13,5},{10,2},{14,6},{11,3},{15,7},{24,16},{28,... | collective-permute-start | bytes 430088 | tf_op jit(solution)/shard_map/ppermute | solution.py:408
  33.3 12.2 %collective-permute-start.8 = (f32[280,128]{1,0:T(8,128)S(1)}, f32[280,128]{1,0:T(8,128)S(1)}, u32[]{:S(2)}, u32[]{:S(2)}) collective-permute-start(f32[280,128]{1,0:T(8,128)S(1)} %add.10.own_ref), channel_id=1, source_target_pairs={{4,0},{8,4},{12,8},{5,1},{9,5},{13,9},{6,2},{10,6},{14,10},{7,3},{... | collective-permute-start | bytes 430088 | tf_op jit(solution)/shard_map/ppermute | solution.py:407
  35.3 18.4 %collective-permute-start.13 = (bf16[2,16,5632]{2,1,0:T(8,128)(2,1)S(1)}, bf16[2,16,5632]{2,1,0:T(8,128)(2,1)S(1)}, u32[]{:S(2)}, u32[]{:S(2)}) collective-permute-start(bf16[2,16,5632]{2,1,0:T(8,128)(2,1)S(1)} %dynamic-slice_bitcast_fusion), channel_id=1, source_target_pairs={{0,2},{2,0},{1,3},{3,1},{4,6},{6,4},{5,7},{7,5},{8,10},{10,8},{9,1... | collective-permute-start | bytes 1081352 | tf_op jit(solution)/shard_map/ppermute | solution.py:602
  46.1 4.5 %collective-permute-start.11 = (f32[280,128]{1,0:T(8,128)S(1)}, f32[280,128]{1,0:T(8,128)S(1)}, u32[]{:S(2)}, u32[]{:S(2)}) collective-permute-start(f32[280,128]{1,0:T(8,128)S(1)} %shard_map.108.near_ref), channel_id=1, source_target_pairs={{0,2},{2,0},{1,3},{3,1},{4,6},{6,4},{5,7},{7,5},{8,10},{10,8},{9,1... | collective-permute-start | bytes 430088 | tf_op jit(solution)/shard_map/ppermute | solution.py:429
  46.6 7.2 %collective-permute-start.14 = (bf16[8,2,5632]{2,1,0:T(2,128)(2,1)S(1)}, bf16[8,2,5632]{2,1,0:T(2,128)(2,1)S(1)}, u32[]{:S(2)}, u32[]{:S(2)}) collective-permute-start(bf16[8,2,5632]{2,1,0:T(2,128)(2,1)S(1)} %dynamic-slice_bitcast_fusion.1), channel_id=1, source_target_pairs={{0,1},{1,0},{2,3},{3,2},{4,5},{5,4},{6,7},{7,6},{8,9},{9,8},{10,11... | collective-permute-start | bytes 540680 | tf_op jit(solution)/shard_map/ppermute | solution.py:610
  47.8 14.9 %collective-permute-start.7 = (bf16[5,128,128]{2,1,0:T(8,128)(2,1)S(1)}, bf16[5,128,128]{2,1,0:T(8,128)(2,1)S(1)}, u32[]{:S(2)}, u32[]{:S(2)}) collective-permute-start(bf16[5,128,128]{2,1,0:T(8,128)(2,1)S(1)} %get-tuple-element.32), channel_id=1, source_target_pairs={{0,2},{2,0},{1,3},{3,1},{4,6},{6,4},{5,7},{7,5},{8,10},{10,8},{9,1... | collective-permute-start | bytes 491528 | tf_op jit(solution)/shard_map/ppermute | solution.py:425
  49.0 14.6 %collective-permute-start.10 = (f32[280,128]{1,0:T(8,128)S(1)}, f32[280,128]{1,0:T(8,128)S(1)}, u32[]{:S(2)}, u32[]{:S(2)}) collective-permute-start(f32[280,128]{1,0:T(8,128)S(1)} %shard_map.108.near_ref), channel_id=1, source_target_pairs={{0,1},{1,0},{2,3},{3,2},{4,5},{5,4},{6,7},{7,6},{8,9},{9,8},{10,11... | collective-permute-start | bytes 430088 | tf_op jit(solution)/shard_map/ppermute | solution.py:430
  50.5 13.1 %collective-permute-start.12 = (f32[280,128]{1,0:T(8,128)S(1)}, f32[280,128]{1,0:T(8,128)S(1)}, u32[]{:S(2)}, u32[]{:S(2)}) collective-permute-start(f32[280,128]{1,0:T(8,128)S(1)} %collective-permute-done.11.far_ref), channel_id=1, source_target_pairs={{0,1},{1,0},{2,3},{3,2},{4,5},{5,4},{6,7},{7,6},{8,9},{9,8},{10,11... | collective-permute-start | bytes 430088 | tf_op jit(solution)/shard_map/ppermute | solution.py:431
  53.7 1.3 %collective-permute-start.15 = (bf16[2,2,5632]{2,1,0:T(2,128)(2,1)S(1)}, bf16[2,2,5632]{2,1,0:T(2,128)(2,1)S(1)}, u32[]{:S(2)}, u32[]{:S(2)}) collective-permute-start(bf16[2,2,5632]{2,1,0:T(2,128)(2,1)S(1)} %constant_dynamic-slice_fusion), channel_id=1, source_target_pairs={{0,1},{1,0},{2,3},{3,2},{4,5},{5,4},{6,7},{7,6},{8,9},{9,8},{10,11... | collective-permute-start | bytes 135176 | tf_op jit(solution)/shard_map/ppermute | solution.py:611
  55.0 8.6 %copy-start.2 = (bf16[1,8,16,1120]{3,2,1,0:T(8,128)(2,1)S(1)}, bf16[1,8,16,1120]{3,2,1,0:T(8,128)(2,1)}, u32[]{:S(2)}) copy-start(bf16[1,8,16,1120]{3,2,1,0:T(8,128)(2,1)} %param.8) | copy-start | bytes 860164
  55.0 8.6 %copy-start.4 = (bf16[1,8,16,1120]{3,2,1,0:T(8,128)(2,1)S(1)}, bf16[1,8,16,1120]{3,2,1,0:T(8,128)(2,1)}, u32[]{:S(2)}) copy-start(bf16[1,8,16,1120]{3,2,1,0:T(8,128)(2,1)} %param.9) | copy-start | bytes 860164

commit v3 on v2

--- a/solution.py
+++ b/solution.py
@@ -220,23 +220,40 @@
     return jnp.where(column == 0, first, 0.0).astype(jnp.bfloat16)
 
 
-def vmem_call(kernel, out_shape, scratch=(), smem_first=False, n_in=0, flops=0, bytes_accessed=0, vmem_mib=8):
+def vmem_call(kernel, out_shape, scratch=(), smem_first=False, n_in=0, flops=0, bytes_accessed=0, vmem_mib=8, in_hbm=False, out_hbm=False):
     vmem = pl.BlockSpec(memory_space=pltpu.VMEM)
-    in_specs = [vmem] * n_in
+    in_specs = [pl.BlockSpec(memory_space=pltpu.HBM) if in_hbm else vmem] * n_in
     if smem_first:
         in_specs[0] = pl.BlockSpec(memory_space=pltpu.SMEM)
     return pl.pallas_call(
         kernel,
         out_shape=out_shape,
         in_specs=in_specs,
-        out_specs=jax.tree.map(lambda _: vmem, out_shape),
+        out_specs=jax.tree.map(lambda _: pl.BlockSpec(memory_space=pltpu.HBM) if out_hbm else vmem, out_shape),
         scratch_shapes=list(scratch),
         cost_estimate=pl.CostEstimate(flops=flops, bytes_accessed=bytes_accessed, transcendentals=0),
         compiler_params=pltpu.CompilerParams(vmem_limit_bytes=vmem_mib << 20),
     )
 
 
-def state_kernel(key_ref, value_ref, keep_ref, send_ref, halves):
+PARTS = 4
+
+
+def stage(sources, targets, sems):
+    copies = []
+    for at, (source, target) in enumerate(zip(sources, targets)):
+        rows = source.shape[0] // PARTS
+        for part in range(PARTS):
+            span = pl.ds(part * rows, rows)
+            copies.append(pltpu.make_async_copy(source.at[span], target.at[span], sems.at[at, part]))
+    for copy in copies:
+        copy.start()
+    for copy in copies:
+        copy.wait()
+
+
+def state_kernel(key_hbm, value_hbm, keep_ref, send_ref, halves, key_ref, value_ref, sems):
+    stage((key_hbm, value_hbm), (key_ref, value_ref), sems)
     tokens = key_ref.shape[0]
     one = tail_block(tokens, 1.0)
     half = halves.shape[2]
@@ -269,7 +286,8 @@
     other_ref[...] = keep_ref[1 - row] + came_ref[1 - row]
 
 
-def heads_kernel(query_ref, cotangent_ref, mine_ref, other_ref, groups):
+def heads_kernel(query_hbm, cotangent_hbm, mine_ref, other_ref, groups, query_ref, cotangent_ref, sems):
+    stage((query_hbm, cotangent_hbm), (query_ref, cotangent_ref), sems)
     none = tail_block(query_ref.shape[0], 0.0)
     per_group = HEADS // 2
     row = lax.axis_index("height")
@@ -282,15 +300,18 @@
     other_ref[...] = groups[1 - row]
 
 
-def chain_kernel(step, clip_ref, own_ref, near_ref, far_ref, out_ref):
+def mask_kernel(clip_ref, out_ref):
     frame = lax.axis_index("tm")
     last = lax.axis_size("tm") - 1
     here = clip_ref[frame]
-    first = jnp.clip(frame - step, 0, last)
-    second = jnp.clip(frame - 2 * step, 0, last)
-    near = jnp.where((clip_ref[first] == here) & (first != frame), 1.0, 0.0)
-    far = jnp.where((clip_ref[second] == here) & (second != first), 1.0, 0.0)
-    out_ref[...] = own_ref[...] + near * near_ref[...] + far * far_ref[...]
+    line = lax.broadcasted_iota(jnp.int32, out_ref.shape, 0)
+    masks = jnp.zeros(out_ref.shape, jnp.float32)
+    for at, (step, hop) in enumerate(((1, 1), (1, 2), (-1, 1), (-1, 2))):
+        other = frame - step * hop
+        inside = (other >= 0) & (other <= last)
+        same = inside & (clip_ref[jnp.clip(other, 0, last)] == here)
+        masks = jnp.where(line == at, jnp.where(same, 1.0, 0.0), masks)
+    out_ref[...] = masks
 
 
 def query_kernel(state_ref, came_ref, mine_ref, other_ref, keep_ref, send_ref, own_out, other_out, state, halves):
@@ -333,25 +354,35 @@
     return parts[0] if len(parts) == 1 else jnp.concatenate(parts, axis=0)
 
 
-def key_kernel(key_ref, value_ref, near_ref, near_came_ref, far_ref, far_came_ref, key_out, value_out, total):
+def key_heads(key_ref, value_ref, total, half, group, place, one):
+    head = group * (HEADS // 2) + place
+    feature = jnp.maximum(head_slice(key_ref, head), 0)
+    wide = jnp.concatenate([head_slice(value_ref, head), one], axis=1)
+    high, low = split_terms(load_rows(total, place * HEAD_DIM, half))
+    grad = dot_columns(wide, high) + dot_columns(wide, low)
+    product = dot_rows(feature, high) + dot_rows(feature, low)
+    return jnp.where(feature > 0, grad, 0.0).astype(jnp.bfloat16), product[:, :HEAD_DIM].astype(jnp.bfloat16)
+
+
+def key_kernel(mine, key_ref, value_ref, here_ref, came_ref, *refs):
     column, row = lax.axis_index("width"), lax.axis_index("height")
-    half = near_ref.shape[0]
-    per_group = HEADS // 2
-    total[row, column] = near_ref[...]
-    total[row, 1 - column] = near_came_ref[...]
-    total[1 - row, column] = far_ref[...]
-    total[1 - row, 1 - column] = far_came_ref[...]
+    half = here_ref.shape[0]
+    given, (key_out, value_out, total) = refs[:-3], refs[-3:]
+    total[column] = here_ref[...]
+    total[1 - column] = came_ref[...]
     one = tail_block(key_ref.shape[0], 1.0)
-    for head in range(HEADS):
-        group, place = divmod(head, per_group)
-        feature = jnp.maximum(head_slice(key_ref, head), 0)
-        wide = jnp.concatenate([head_slice(value_ref, head), one], axis=1)
-        high, low = split_terms(load_rows(total.at[group], place * HEAD_DIM, half))
-        grad = dot_columns(wide, high) + dot_columns(wide, low)
-        lanes = slice(head * HEAD_DIM, (head + 1) * HEAD_DIM)
-        key_out[:, lanes] = jnp.where(feature > 0, grad, 0.0).astype(jnp.bfloat16)
-        product = dot_rows(feature, high) + dot_rows(feature, low)
-        value_out[:, lanes] = product[:, :HEAD_DIM].astype(jnp.bfloat16)
+    for group in range(2):
+        @pl.when(row == (group if mine else 1 - group))
+        def _():
+            for place in range(HEADS // 2):
+                grads = key_heads(key_ref, value_ref, total, half, group, place, one)
+                for at, out in enumerate((key_out, value_out)):
+                    if mine:
+                        out[place, :, :HEAD_DIM] = grads[at]
+                        continue
+                    for which, part in ((group, grads[at]), (1 - group, given[at][place, :, :HEAD_DIM])):
+                        first = (which * (HEADS // 2) + place) * HEAD_DIM
+                        out[:, first : first + HEAD_DIM] = part
 
 
 def join_kernel(mine_ref, came_ref, out_ref):
@@ -373,7 +404,7 @@
 SWAP = [(0, 1), (1, 0)]
 
 
-def paired_attention(queries, attn_keys, attn_values, attn_cotangent, clip_ids):
+def paired(queries, attn_keys, attn_values, attn_cotangent, clip_ids, hidden_pre, conv_weight):
     tokens = queries.shape[1] * queries.shape[2]
     flat = HEADS * HEAD_DIM
     per_group = HEADS // 2
@@ -385,32 +416,44 @@
     share = struct((half, LANES))
     pair = struct((2, half, LANES))
 
+    masks = vmem_call(mask_kernel, struct((8, LANES)), smem_first=True, n_in=1, bytes_accessed=4096)(
+        pltpu.with_memory_space_constraint(clip_ids, pltpu.HBM)
+    )
+    key_hbm, value_hbm = (
+        pltpu.with_memory_space_constraint(part, pltpu.HBM) for part in (key, value)
+    )
+    staged = [pltpu.VMEM((tokens, flat), jnp.bfloat16)] * 2 + [pltpu.SemaphoreType.DMA((2, PARTS))]
     keep, send = vmem_call(
-        state_kernel, (pair, pair), [pltpu.VMEM((2, 2, half, LANES), jnp.float32)], n_in=2,
+        state_kernel, (pair, pair), [pltpu.VMEM((2, 2, half, LANES), jnp.float32), *staged], n_in=2, in_hbm=True,
         flops=2 * tokens * flat * LANES, bytes_accessed=4 * tokens * flat + 8 * half * LANES * 2,
-    )(key, value)
+    )(key_hbm, value_hbm)
     came = lax.ppermute(send, "width", SWAP)
     mine, other = vmem_call(pick_kernel, (share, share), n_in=2, bytes_accessed=24 * half * LANES)(keep, came)
     came = lax.ppermute(other, "height", SWAP)
 
     packed = struct((2, per_group, tokens, LANES), jnp.bfloat16)
+    query, cotangent, mine = lax.optimization_barrier((query, cotangent, mine))
     heads_mine, heads_other = vmem_call(
-        heads_kernel, (packed, packed), [pltpu.VMEM((2, 2, per_group, tokens, LANES), jnp.bfloat16)], n_in=2,
+        heads_kernel, (packed, packed), [pltpu.VMEM((2, 2, per_group, tokens, LANES), jnp.bfloat16), *staged], n_in=2, in_hbm=True,
         bytes_accessed=12 * tokens * flat,
-    )(query, cotangent)
-    own = mine + came
-    heads_other, own = lax.optimization_barrier((heads_other, own))
-    heads_came = lax.ppermute(heads_other, "height", SWAP)
-
-    def along_frames(own, step):
+    )(*(pltpu.with_memory_space_constraint(part, pltpu.HBM) for part in (query, cotangent)))
+    _, own = lax.optimization_barrier((heads_other, mine + came))
+    heads_sent = lax.ppermute(heads_other, "height", SWAP)
+
+    def along_frames(own, step, beside):
         moves = [[(at, at + step * hop) for at in range(frames) if 0 <= at + step * hop < frames] for hop in (1, 2)]
         near = lax.ppermute(own, "tm", moves[0])
         far = lax.ppermute(own, "tm", moves[1])
-        return vmem_call(
-            functools.partial(chain_kernel, step), share, smem_first=True, n_in=4, bytes_accessed=16 * half * LANES
-        )(clip_ids, own, near, far)
-
-    state = along_frames(own, 1)
+        near, far, beside = beside(own, near, far)
+        at = 0 if step > 0 else 2
+        return own + masks[at : at + 1] * near + masks[at + 1 : at + 2] * far, beside
+
+    def fetch(own, near, far):
+        block, _ = lax.optimization_barrier((hidden_pre, own))
+        near, far, arrived = lax.optimization_barrier((near, far, heads_sent))
+        return near, far, (halo_arrays(block), arrived)
+
+    state, (halo, heads_came) = along_frames(own, 1, fetch)
     came = lax.ppermute(state, "width", SWAP)
     back = struct((per_group, tokens, LANES), jnp.bfloat16)
     keep, send, back_mine, back_other = vmem_call(
@@ -420,21 +463,32 @@
     )(state, came, heads_mine, heads_came)
     came = lax.ppermute(send, "width", SWAP)
     own = keep + came
-    back_other, own = lax.optimization_barrier((back_other, own))
-    total = along_frames(own, -1)
-    back_came = lax.ppermute(back_other, "height", SWAP)
-    query_grad = vmem_call(
-        join_kernel, struct((tokens, flat), jnp.bfloat16), n_in=2, bytes_accessed=4 * tokens * flat
-    )(back_mine, back_came)
+
+    def convolve(own, near, far):
+        other, _ = lax.optimization_barrier((back_other, own))
+        back_came = lax.ppermute(other, "height", SWAP)
+        hidden_grad = ffn(hidden_pre, conv_weight, halo)
+        query_grad = vmem_call(
+            join_kernel, struct((tokens, flat), jnp.bfloat16), n_in=2, bytes_accessed=4 * tokens * flat
+        )(back_mine, back_came)
+        near, far, grads = lax.optimization_barrier((near, far, (query_grad, hidden_grad)))
+        return near, far, grads
+
+    total, (query_grad, hidden_grad) = along_frames(own, -1, convolve)
     far = lax.ppermute(total, "height", SWAP)
     near_came = lax.ppermute(total, "width", SWAP)
+    state = [pltpu.VMEM((2, half, LANES), jnp.float32)]
+    cost = {"flops": 4 * tokens * flat * LANES, "bytes_accessed": 4 * tokens * flat}
+    near_grads = vmem_call(functools.partial(key_kernel, True), (back, back), state, n_in=4, **cost)(
+        key, value, total, near_came
+    )
     far_came = lax.ppermute(far, "width", SWAP)
     out = struct((tokens, flat), jnp.bfloat16)
-    key_grad, value_gradient = vmem_call(
-        key_kernel, (out, out), [pltpu.VMEM((2, 2, half, LANES), jnp.float32)], n_in=6,
-        flops=8 * tokens * flat * LANES, bytes_accessed=8 * tokens * flat,
-    )(key, value, total, near_came, far, far_came)
-    return tuple(part.reshape(queries.shape) for part in (query_grad, key_grad, value_gradient))
+    key_grad, value_gradient = vmem_call(functools.partial(key_kernel, False), (out, out), state, n_in=6, **cost)(
+        key, value, far, far_came, *near_grads
+    )
+    grads = tuple(part.reshape(queries.shape) for part in (query_grad, key_grad, value_gradient))
+    return (*grads, hidden_grad)
 
 
 def mixed_ffn(hidden_pre, conv_weight):
@@ -462,7 +516,7 @@
     halo_rows, refs = refs[:row_refs], refs[row_refs:]
     side_ref, refs = refs[0], refs[1:]
     corners, refs = refs[:row_refs], refs[row_refs:]
-    block_ref, weight_ref, out_ref, taps, value_in, gate_in, value_grad, gate_grad, value_out, gate_out = refs
+    block_ref, weight_ref, out_hbm, taps, value_in, gate_in, value_grad, gate_grad, value_out, gate_out, out_ref, sems = refs
     rows, cols, channels = block_ref.shape
     lane_tiles = channels // LANES // 2
     pitch = -(-lane_tiles // TILES) * TILES
@@ -506,6 +560,7 @@
                 for col in range(grad_wide):
                     ref[pl.ds(grad_at(at, col), TILES), :] = zero
 
+    copies = []
     for base in range(0, lane_tiles, TILES):
         count = min(TILES, lane_tiles - base)
 
@@ -586,6 +641,14 @@
                 for tile in range(count):
                     lanes = slice((offset + tile) * LANES, (offset + tile + 1) * LANES)
                     out_ref[at, :, lanes] = result[pl.ds(tile, cols, stride=TILES), :].astype(jnp.bfloat16)
+
+        for at, offset in enumerate((base, lane_tiles + base)):
+            lanes = pl.ds(offset * LANES, count * LANES)
+            copy = pltpu.make_async_copy(out_ref.at[:, :, lanes], out_hbm.at[:, :, lanes], sems.at[at, base // TILES])
+            copy.start()
+            copies.append(copy)
+    for copy in copies:
+        copy.wait()
 
 
 def edge_slice(block, axis_name, dim, low_side):
@@ -612,8 +675,8 @@
     return halo_rows, side, corners
 
 
-def paired_ffn(hidden_pre, conv_weight):
-    halo_rows, side, corners = halo_arrays(hidden_pre)
+def ffn(hidden_pre, conv_weight, halo):
+    halo_rows, side, corners = halo
     block = hidden_pre[0]
     rows, cols, channels = block.shape
     lane_tiles = channels // LANES // 2
@@ -625,24 +688,22 @@
     hidden_grad = vmem_call(
         functools.partial(conv_kernel, rows, len(halo_rows)),
         struct((rows, cols, channels), jnp.bfloat16),
-        [pltpu.VMEM((9 * 2 * pitch, LANES), jnp.float32), source, source, grad, grad, result, result],
-        n_in=2 * len(halo_rows) + 3, flops=60 * size, bytes_accessed=6 * size,
+        [pltpu.VMEM((9 * 2 * pitch, LANES), jnp.float32), source, source, grad, grad, result, result,
+         pltpu.VMEM((rows, cols, channels), jnp.bfloat16), pltpu.SemaphoreType.DMA((2, pitch // TILES))],
+        n_in=2 * len(halo_rows) + 3, flops=2 * size, bytes_accessed=size, vmem_mib=12, out_hbm=True,
     )(*halo_rows, side, *corners, block, conv_weight)
     return hidden_grad[None]
 
 
 def per_device(queries, attn_keys, attn_values, attn_cotangent, clip_ids, hidden_pre, conv_weight):
-    paired = (
-        lax.axis_size("height") == 2
-        and lax.axis_size("width") == 2
-        and 3 <= lax.axis_size("tm") <= 4
-        and HEADS % 2 == 0
-        and queries.shape[0] == 1
-    )
-    attention = paired_attention if paired else general_attention
-    grads = attention(queries, attn_keys, attn_values, attn_cotangent, clip_ids)
-    hidden_grad = paired_ffn(hidden_pre, conv_weight) if lax.axis_size("width") == 2 and hidden_pre.shape[0] == 1 and hidden_pre.shape[3] % (2 * LANES) == 0 else mixed_ffn(hidden_pre, conv_weight)
-    return (*grads, hidden_grad)
+    blocked = lax.axis_size("width") == 2 and hidden_pre.shape[0] == 1 and hidden_pre.shape[3] % (2 * LANES) == 0
+    pairs = lax.axis_size("height") == 2 and 3 <= lax.axis_size("tm") <= 4 and HEADS % 2 == 0
+    if blocked and pairs:
+        return paired(queries, attn_keys, attn_values, attn_cotangent, clip_ids, hidden_pre, conv_weight)
+    grads = general_attention(queries, attn_keys, attn_values, attn_cotangent, clip_ids)
+    if blocked:
+        return (*grads, ffn(hidden_pre, conv_weight, halo_arrays(hidden_pre)))
+    return (*grads, mixed_ffn(hidden_pre, conv_weight))
 
 
 def solution(mesh):

time: 65.6 us -> 54.3 us (0.83)
  the two profiles are of different devices: /device:TPU:9 before, /device:TPU:25 now
where the time goes in v3:
time: 54.3 us; the launch traced here: 54 us
  starting transfers between devices  18.3 us (34%)
  Pallas kernels  17.8 us (33%)
  waiting for transfers between devices  16.8 us (31%)
  between operations  0.79 us (1%)
    ppermute x2, waiting for transfers between devices, along_frames(): far = lax.ppermute(own, 'tm', moves[1])  8.8 us
    pallas_call x1, Pallas kernels, ffn(): vmem_call(functools.partial(conv_kernel, rows, len(halo_rows)), struct((r...  7.35 us
    ppermute x2, starting transfers between devices, along_frames(): far = lax.ppermute(own, 'tm', moves[1])  4.45 us
    ppermute x1, waiting for transfers between devices, paired(): far = lax.ppermute(total, 'height', SWAP)  3.85 us
    ppermute x2, starting transfers between devices, along_frames(): near = lax.ppermute(own, 'tm', moves[0])  3.61 us
    pallas_call x1, Pallas kernels, paired(): vmem_call(query_kernel, (share, share, back, back), [pltpu.VMEM((2, half,...  2.96 us
    pallas_call x1, Pallas kernels, paired(): vmem_call(state_kernel, (pair, pair), [pltpu.VMEM((2, 2, half, LANES), jn...  2.12 us
    ppermute x1, starting transfers between devices, halo_arrays(): halo_rows = [lax.ppermute(edge, 'height', SWAP)]  1.86 us
  transfers between devices with their start and end apart: 16, of which 7 were waited for; matrix products, arithmetic and copies ran while one was open for 1% of the time, Pallas kernels for 26%

profile of v3, /device:TPU:25, one launch (start us, length us, event | category | flops | bytes accessed | tf_op | source)
XLA Modules:
  0.0 54.0 jit_solution(3917778054931165092)
XLA Ops:
  0.6 2.1 %shard_map.102 = (f32[2,280,128]{2,1,0:T(8,128)S(1)}, f32[2,280,128]{2,1,0:T(8,128)S(1)}) custom-call(bf16[128,1120]{1,0:T(8,128)(2,1)} %bitcast.22, bf16[128,1120]{1,0:T(8,128)(2,1)} %bitcast.25), custom_call_target="tpu_custom_call" | custom-call | flops 36700160 | bytes 1146880 | tf_op jit(solution)/shard_map/pallas_call | solution.py:426
  2.8 0.7 %collective-permute-start = (f32[2,280,128]{2,1,0:T(8,128)S(1)}, f32[2,280,128]{2,1,0:T(8,128)S(1)}, u32[]{:S(2)}, u32[]{:S(2)}) collective-permute-start(f32[2,280,128]{2,1,0:T(8,128)S(1)} %get-tuple-element.32), channel_id=1, source_target_pairs={{0,1},{1,0},{2,3},{3,2},{4,5},{5,4},{6,7},{7,6},{8,9},{9,8},{10,11... | collective-permute-start | bytes 860168 | tf_op jit(solution)/shard_map/ppermute | solution.py:430
  3.5 1.2 %collective-permute-done.came_ref = f32[2,280,128]{2,1,0:T(8,128)S(1)} collective-permute-done((f32[2,280,128]{2,1,0:T(8,128)S(1)}, f32[2,280,128]{2,1,0:T(8,128)S(1)}, u32[]{:S(2)}, u32[]{:S(2)}) %collective-permute-start) | collective-permute-done | bytes 286752 | tf_op jit(solution)/shard_map/ppermute | solution.py:430
  4.7 1.3 %collective-permute-start.1 = (f32[280,128]{1,0:T(8,128)S(1)}, f32[280,128]{1,0:T(8,128)S(1)}, u32[]{:S(2)}, u32[]{:S(2)}) collective-permute-start(f32[280,128]{1,0:T(8,128)S(1)} %get-tuple-element.38), channel_id=1, source_target_pairs={{0,2},{2,0},{1,3},{3,1},{4,6},{6,4},{5,7},{7,5},{8,10},{10,8},{9,1... | collective-permute-start | bytes 430088 | tf_op jit(solution)/shard_map/ppermute | solution.py:432
  6.0 1.7 %shard_map.104 = (bf16[2,5,128,128]{3,2,1,0:T(8,128)(2,1)S(1)}, bf16[2,5,128,128]{3,2,1,0:T(8,128)(2,1)S(1)}) custom-call(bf16[128,1120]{1,0:T(8,128)(2,1)} %bitcast.29, bf16[128,1120]{1,0:T(8,128)(2,1)} %bitcast.30), custom_call_target="tpu_custom_call" | custom-call | bytes 1720320 | tf_op jit(solution)/shard_map/pallas_call | solution.py:436
  7.7 0.3 collective-permute-start.4
  8.0 0.7 %shard_map.105 = f32[8,128]{1,0:T(8,128)S(1)} custom-call(s32[4]{0:T(128)} %clip_ref.1), custom_call_target="tpu_custom_call" | custom-call | bytes 4096 | tf_op jit(solution)/shard_map/pallas_call | solution.py:419
  8.7 1.0 %collective-permute-done.1 = f32[280,128]{1,0:T(8,128)S(1)} collective-permute-done((f32[280,128]{1,0:T(8,128)S(1)}, f32[280,128]{1,0:T(8,128)S(1)}, u32[]{:S(2)}, u32[]{:S(2)}) %collective-permute-start.1) | collective-permute-done | bytes 143392 | tf_op jit(solution)/shard_map/ppermute | solution.py:432
  9.8 1.3 %collective-permute-start.3 = (f32[280,128]{1,0:T(8,128)S(1)}, f32[280,128]{1,0:T(8,128)S(1)}, u32[]{:S(2)}, u32[]{:S(2)}) collective-permute-start(f32[280,128]{1,0:T(8,128)S(1)} %add.21), channel_id=1, source_target_pairs={{0,8},{4,12},{1,9},{5,13},{2,10},{6,14},{3,11},{7,15},{16,24},{20,... | collective-permute-start | bytes 430088 | tf_op jit(solution)/shard_map/ppermute | solution.py:446
  11.1 1.3 %collective-permute-start.2 = (f32[280,128]{1,0:T(8,128)S(1)}, f32[280,128]{1,0:T(8,128)S(1)}, u32[]{:S(2)}, u32[]{:S(2)}) collective-permute-start(f32[280,128]{1,0:T(8,128)S(1)} %add.21), channel_id=1, source_target_pairs={{0,4},{4,8},{8,12},{1,5},{5,9},{9,13},{2,6},{6,10},{10,14},{3,7},{... | collective-permute-start | bytes 430088 | tf_op jit(solution)/shard_map/ppermute | solution.py:445
  12.4 8.8 %collective-permute-done.3 = f32[280,128]{1,0:T(8,128)S(1)} collective-permute-done((f32[280,128]{1,0:T(8,128)S(1)}, f32[280,128]{1,0:T(8,128)S(1)}, u32[]{:S(2)}, u32[]{:S(2)}) %collective-permute-start.3) | collective-permute-done | bytes 143392 | tf_op jit(solution)/shard_map/ppermute | solution.py:446
  21.3 1.1 %collective-permute-start.5 = (f32[280,128]{1,0:T(8,128)S(1)}, f32[280,128]{1,0:T(8,128)S(1)}, u32[]{:S(2)}, u32[]{:S(2)}) collective-permute-start(f32[280,128]{1,0:T(8,128)S(1)} %multiply_add_fusion.1.state_ref), channel_id=1, source_target_pairs={{0,1},{1,0},{2,3},{3,2},{4,5},{5,4},{6,7},{7,6},{8,9},{9,8},{10,11... | collective-permute-start | bytes 430088 | tf_op jit(solution)/shard_map/ppermute | solution.py:457
  22.4 1.9 %collective-permute-start.10 = (bf16[2,16,5632]{2,1,0:T(8,128)(2,1)S(1)}, bf16[2,16,5632]{2,1,0:T(8,128)(2,1)S(1)}, u32[]{:S(2)}, u32[]{:S(2)}) collective-permute-start(bf16[2,16,5632]{2,1,0:T(8,128)(2,1)S(1)} %dynamic-slice_bitcast_fusion), channel_id=1, source_target_pairs={{0,2},{2,0},{1,3},{3,1},{4,6},{6,4},{5,7},{7,5},{8,10},{10,8},{9,1... | collective-permute-start | bytes 1081352 | tf_op jit(solution)/shard_map/ppermute | solution.py:665
  24.2 3.0 %shard_map.106 = (f32[280,128]{1,0:T(8,128)S(1)}, f32[280,128]{1,0:T(8,128)S(1)}, bf16[5,128,128]{2,1,0:T(8,128)(2,1)S(1)}, bf16[5,128,128]{2,1,0:T(8,128)(2,1)S(1)}) custom-call(f32[280,128]{1,0:T(8,128)S(1)} %multiply_add_fusion.1.state_ref, f32[280,128]{1,0:T(8,128)S(1)} %collective-permute-done.5.came_ref, ...), custom_call_target="tpu_custom_call" | custom-call | flops 256901120 | bytes 1146880 | tf_op jit(solution)/shard_map/pallas_call | solution.py:459
  27.2 0.4 collective-permute-start.6
  27.6 0.2 dynamic-slice_bitcast_fusion.1
  27.8 0.3 collective-permute-start.11
  28.0 0.6 %collective-permute-done.6 = f32[280,128]{1,0:T(8,128)S(1)} collective-permute-done((f32[280,128]{1,0:T(8,128)S(1)}, f32[280,128]{1,0:T(8,128)S(1)}, u32[]{:S(2)}, u32[]{:S(2)}) %collective-permute-start.6) | collective-permute-done | bytes 143392 | tf_op jit(solution)/shard_map/ppermute | solution.py:464
  28.7 3.2 %collective-permute-start.8 = (f32[280,128]{1,0:T(8,128)S(1)}, f32[280,128]{1,0:T(8,128)S(1)}, u32[]{:S(2)}, u32[]{:S(2)}) collective-permute-start(f32[280,128]{1,0:T(8,128)S(1)} %add.24), channel_id=1, source_target_pairs={{8,0},{12,4},{9,1},{13,5},{10,2},{14,6},{11,3},{15,7},{24,16},{28,... | collective-permute-start | bytes 430088 | tf_op jit(solution)/shard_map/ppermute | solution.py:446
  31.8 2.3 %collective-permute-start.7 = (f32[280,128]{1,0:T(8,128)S(1)}, f32[280,128]{1,0:T(8,128)S(1)}, u32[]{:S(2)}, u32[]{:S(2)}) collective-permute-start(f32[280,128]{1,0:T(8,128)S(1)} %add.24), channel_id=1, source_target_pairs={{4,0},{8,4},{12,8},{5,1},{9,5},{13,9},{6,2},{10,6},{14,10},{7,3},{... | collective-permute-start | bytes 430088 | tf_op jit(solution)/shard_map/ppermute | solution.py:445
  34.2 1.0 %collective-permute-start.9 = (bf16[5,128,128]{2,1,0:T(8,128)(2,1)S(1)}, bf16[5,128,128]{2,1,0:T(8,128)(2,1)S(1)}, u32[]{:S(2)}, u32[]{:S(2)}) collective-permute-start(bf16[5,128,128]{2,1,0:T(8,128)(2,1)S(1)} %get-tuple-element.48), channel_id=1, source_target_pairs={{0,2},{2,0},{1,3},{3,1},{4,6},{6,4},{5,7},{7,5},{8,10},{10,8},{9,1... | collective-permute-start | bytes 491528 | tf_op jit(solution)/shard_map/ppermute | solution.py:469
  35.2 1.0 %collective-permute-start.12 = (bf16[2,2,5632]{2,1,0:T(2,128)(2,1)S(1)}, bf16[2,2,5632]{2,1,0:T(2,128)(2,1)S(1)}, u32[]{:S(2)}, u32[]{:S(2)}) collective-permute-start(bf16[2,2,5632]{2,1,0:T(2,128)(2,1)S(1)} %constant_dynamic-slice_fusion), channel_id=1, source_target_pairs={{0,1},{1,0},{2,3},{3,2},{4,5},{5,4},{6,7},{7,6},{8,9},{9,8},{10,11... | collective-permute-start | bytes 135176 | tf_op jit(solution)/shard_map/ppermute | solution.py:674
  36.2 0.9 %collective-permute-done.12.refs_2_ = bf16[2,2,5632]{2,1,0:T(2,128)(2,1)S(1)} collective-permute-done((bf16[2,2,5632]{2,1,0:T(2,128)(2,1)S(1)}, bf16[2,2,5632]{2,1,0:T(2,128)(2,1)S(1)}, u32[]{:S(2)}, u32[]{:S(2)}) %collective-permute-start.12) | collective-permute-done | bytes 45088 | tf_op jit(solution)/shard_map/ppermute | solution.py:674
  37.1 7.4 %shard_map.108 = bf16[8,16,5632]{2,1,0:T(8,128)(2,1)} custom-call(bf16[2,16,5632]{2,1,0:T(8,128)(2,1)S(1)} %collective-permute-done.10.refs_0_, bf16[8,2,5632]{2,1,0:T(2,128)(2,1)S(1)} %collective-permute-done.11.refs_1_, bf16[2,2,5632]{2,1,0:T(2,128)(2,1)S(1)} %collective-permute-done.12.refs_2_, bf16[8,16,5632]{2,1,0:T(8,128)(2,1)S(1)} %bitcast.21, ...), custom_call_target="tpu_custom_call" | custom-call | flops 1441792 | bytes 720896 | tf_op jit(solution)/shard_map/pallas_call | solution.py:688
  44.4 0.9 %shard_map.107 = bf16[128,1120]{1,0:T(8,128)(2,1)} custom-call(bf16[5,128,128]{2,1,0:T(8,128)(2,1)S(1)} %get-tuple-element.46.mine_ref, bf16[5,128,128]{2,1,0:T(8,128)(2,1)S(1)} %collective-permute-done.9.came_ref), custom_call_target="tpu_custom_call" | custom-call | bytes 573440 | tf_op jit(solution)/shard_map/pallas_call | solution.py:471
  45.4 0.6 %collective-permute-start.13 = (f32[280,128]{1,0:T(8,128)S(1)}, f32[280,128]{1,0:T(8,128)S(1)}, u32[]{:S(2)}, u32[]{:S(2)}) collective-permute-start(f32[280,128]{1,0:T(8,128)S(1)} %multiply_add_fusion.here_ref), channel_id=1, source_target_pairs={{0,2},{2,0},{1,3},{3,1},{4,6},{6,4},{5,7},{7,5},{8,10},{10,8},{9,1... | collective-permute-start | bytes 430088 | tf_op jit(solution)/shard_map/ppermute | solution.py:478
  46.0 0.6 %collective-permute-start.15 = (f32[280,128]{1,0:T(8,128)S(1)}, f32[280,128]{1,0:T(8,128)S(1)}, u32[]{:S(2)}, u32[]{:S(2)}) collective-permute-start(f32[280,128]{1,0:T(8,128)S(1)} %multiply_add_fusion.here_ref), channel_id=1, source_target_pairs={{0,1},{1,0},{2,3},{3,2},{4,5},{5,4},{6,7},{7,6},{8,9},{9,8},{10,11... | collective-permute-start | bytes 430088 | tf_op jit(solution)/shard_map/ppermute | solution.py:479
  46.6 3.8 %collective-permute-done.13.here_ref = f32[280,128]{1,0:T(8,128)S(1)} collective-permute-done((f32[280,128]{1,0:T(8,128)S(1)}, f32[280,128]{1,0:T(8,128)S(1)}, u32[]{:S(2)}, u32[]{:S(2)}) %collective-permute-start.13) | collective-permute-done | bytes 143392 | tf_op jit(solution)/shard_map/ppermute | solution.py:478
  50.5 1.2 %collective-permute-start.14 = (f32[280,128]{1,0:T(8,128)S(1)}, f32[280,128]{1,0:T(8,128)S(1)}, u32[]{:S(2)}, u32[]{:S(2)}) collective-permute-start(f32[280,128]{1,0:T(8,128)S(1)} %collective-permute-done.13.here_ref), channel_id=1, source_target_pairs={{0,1},{1,0},{2,3},{3,2},{4,5},{5,4},{6,7},{7,6},{8,9},{9,8},{10,11... | collective-permute-start | bytes 430088 | tf_op jit(solution)/shard_map/ppermute | solution.py:485
  51.6 0.6 %shard_map.109 = (bf16[5,128,128]{2,1,0:T(8,128)(2,1)S(1)}, bf16[5,128,128]{2,1,0:T(8,128)(2,1)S(1)}) custom-call(bf16[128,1120]{1,0:T(8,128)(2,1)S(1)} %bitcast.23, bf16[128,1120]{1,0:T(8,128)(2,1)S(1)} %bitcast.26, f32[280,128]{1,0:T(8,128)S(1)} %multiply_add_fusion.here_ref, f32[280,128]{1,0:T(8,128)S(1)} %collective-permute-done.15.came_ref), custom_call_target="tpu_custom_call" | custom-call | flops 73400320 | bytes 573440 | tf_op jit(solution)/shard_map/pallas_call | solution.py:482
  52.3 0.4 collective-permute-done.14.came_ref
  52.6 1.4 %shard_map.110 = (bf16[128,1120]{1,0:T(8,128)(2,1)}, bf16[128,1120]{1,0:T(8,128)(2,1)}) custom-call(bf16[128,1120]{1,0:T(8,128)(2,1)S(1)} %bitcast.24, bf16[128,1120]{1,0:T(8,128)(2,1)S(1)} %bitcast.27, f32[280,128]{1,0:T(8,128)S(1)} %collective-permute-done.13.here_ref, f32[280,128]{1,0:T(8,128)S(1)} %collective-permute-done.14.came_ref, ...), custom_call_target="tpu_custom_call" | custom-call | flops 73400320 | bytes 573440 | tf_op jit(solution)/shard_map/pallas_call | solution.py:487
  (25 shorter events, 0.3 us)
Async XLA Ops:
  0.6 21.7 %copy-start = (bf16[1,8,16,5632]{3,2,1,0:T(8,128)(2,1)S(1)}, bf16[1,8,16,5632]{3,2,1,0:T(8,128)(2,1)}, u32[]{:S(2)}) copy-start(bf16[1,8,16,5632]{3,2,1,0:T(8,128)(2,1)} %param.12) | copy-start | bytes 4325380
  2.8 1.9 %collective-permute-start = (f32[2,280,128]{2,1,0:T(8,128)S(1)}, f32[2,280,128]{2,1,0:T(8,128)S(1)}, u32[]{:S(2)}, u32[]{:S(2)}) collective-permute-start(f32[2,280,128]{2,1,0:T(8,128)S(1)} %get-tuple-element.32), channel_id=1, source_target_pairs={{0,1},{1,0},{2,3},{3,2},{4,5},{5,4},{6,7},{7,6},{8,9},{9,8},{10,11... | collective-permute-start | bytes 860168 | tf_op jit(solution)/shard_map/ppermute | solution.py:430
  4.7 5.0 %collective-permute-start.1 = (f32[280,128]{1,0:T(8,128)S(1)}, f32[280,128]{1,0:T(8,128)S(1)}, u32[]{:S(2)}, u32[]{:S(2)}) collective-permute-start(f32[280,128]{1,0:T(8,128)S(1)} %get-tuple-element.38), channel_id=1, source_target_pairs={{0,2},{2,0},{1,3},{3,1},{4,6},{6,4},{5,7},{7,5},{8,10},{10,8},{9,1... | collective-permute-start | bytes 430088 | tf_op jit(solution)/shard_map/ppermute | solution.py:432
  7.7 13.5 %collective-permute-start.4 = (bf16[2,5,128,128]{3,2,1,0:T(8,128)(2,1)S(1)}, bf16[2,5,128,128]{3,2,1,0:T(8,128)(2,1)S(1)}, u32[]{:S(2)}, u32[]{:S(2)}) collective-permute-start(bf16[2,5,128,128]{3,2,1,0:T(8,128)(2,1)S(1)} %get-tuple-element.36), channel_id=1, source_target_pairs={{0,2},{2,0},{1,3},{3,1},{4,6},{6,4},{5,7},{7,5},{8,10},{10,8},{9,1... | collective-permute-start | bytes 983048 | tf_op jit(solution)/shard_map/ppermute | solution.py:441
  9.8 11.4 %collective-permute-start.3 = (f32[280,128]{1,0:T(8,128)S(1)}, f32[280,128]{1,0:T(8,128)S(1)}, u32[]{:S(2)}, u32[]{:S(2)}) collective-permute-start(f32[280,128]{1,0:T(8,128)S(1)} %add.21), channel_id=1, source_target_pairs={{0,8},{4,12},{1,9},{5,13},{2,10},{6,14},{3,11},{7,15},{16,24},{20,... | collective-permute-start | bytes 430088 | tf_op jit(solution)/shard_map/ppermute | solution.py:446
  11.1 10.1 %collective-permute-start.2 = (f32[280,128]{1,0:T(8,128)S(1)}, f32[280,128]{1,0:T(8,128)S(1)}, u32[]{:S(2)}, u32[]{:S(2)}) collective-permute-start(f32[280,128]{1,0:T(8,128)S(1)} %add.21), channel_id=1, source_target_pairs={{0,4},{4,8},{8,12},{1,5},{5,9},{9,13},{2,6},{6,10},{10,14},{3,7},{... | collective-permute-start | bytes 430088 | tf_op jit(solution)/shard_map/ppermute | solution.py:445
  21.2 15.8 %copy-start.3 = (f32[9,5632]{1,0:T(8,128)S(1)}, f32[9,5632]{1,0:T(8,128)}, u32[]{:S(2)}) copy-start(f32[9,5632]{1,0:T(8,128)} %refs_4_.1) | copy-start | bytes 608260
  21.3 3.0 %collective-permute-start.5 = (f32[280,128]{1,0:T(8,128)S(1)}, f32[280,128]{1,0:T(8,128)S(1)}, u32[]{:S(2)}, u32[]{:S(2)}) collective-permute-start(f32[280,128]{1,0:T(8,128)S(1)} %multiply_add_fusion.1.state_ref), channel_id=1, source_target_pairs={{0,1},{1,0},{2,3},{3,2},{4,5},{5,4},{6,7},{7,6},{8,9},{9,8},{10,11... | collective-permute-start | bytes 430088 | tf_op jit(solution)/shard_map/ppermute | solution.py:457
  22.4 12.7 %collective-permute-start.10 = (bf16[2,16,5632]{2,1,0:T(8,128)(2,1)S(1)}, bf16[2,16,5632]{2,1,0:T(8,128)(2,1)S(1)}, u32[]{:S(2)}, u32[]{:S(2)}) collective-permute-start(bf16[2,16,5632]{2,1,0:T(8,128)(2,1)S(1)} %dynamic-slice_bitcast_fusion), channel_id=1, source_target_pairs={{0,2},{2,0},{1,3},{3,1},{4,6},{6,4},{5,7},{7,5},{8,10},{10,8},{9,1... | collective-permute-start | bytes 1081352 | tf_op jit(solution)/shard_map/ppermute | solution.py:665
  27.2 1.4 %collective-permute-start.6 = (f32[280,128]{1,0:T(8,128)S(1)}, f32[280,128]{1,0:T(8,128)S(1)}, u32[]{:S(2)}, u32[]{:S(2)}) collective-permute-start(f32[280,128]{1,0:T(8,128)S(1)} %get-tuple-element.45), channel_id=1, source_target_pairs={{0,1},{1,0},{2,3},{3,2},{4,5},{5,4},{6,7},{7,6},{8,9},{9,8},{10,11... | collective-permute-start | bytes 430088 | tf_op jit(solution)/shard_map/ppermute | solution.py:464
  27.8 8.4 %collective-permute-start.11 = (bf16[8,2,5632]{2,1,0:T(2,128)(2,1)S(1)}, bf16[8,2,5632]{2,1,0:T(2,128)(2,1)S(1)}, u32[]{:S(2)}, u32[]{:S(2)}) collective-permute-start(bf16[8,2,5632]{2,1,0:T(2,128)(2,1)S(1)} %dynamic-slice_bitcast_fusion.1), channel_id=1, source_target_pairs={{0,1},{1,0},{2,3},{3,2},{4,5},{5,4},{6,7},{7,6},{8,9},{9,8},{10,11... | collective-permute-start | bytes 540680 | tf_op jit(solution)/shard_map/ppermute | solution.py:673
  28.7 16.7 %collective-permute-start.8 = (f32[280,128]{1,0:T(8,128)S(1)}, f32[280,128]{1,0:T(8,128)S(1)}, u32[]{:S(2)}, u32[]{:S(2)}) collective-permute-start(f32[280,128]{1,0:T(8,128)S(1)} %add.24), channel_id=1, source_target_pairs={{8,0},{12,4},{9,1},{13,5},{10,2},{14,6},{11,3},{15,7},{24,16},{28,... | collective-permute-start | bytes 430088 | tf_op jit(solution)/shard_map/ppermute | solution.py:446
  31.8 13.5 %collective-permute-start.7 = (f32[280,128]{1,0:T(8,128)S(1)}, f32[280,128]{1,0:T(8,128)S(1)}, u32[]{:S(2)}, u32[]{:S(2)}) collective-permute-start(f32[280,128]{1,0:T(8,128)S(1)} %add.24), channel_id=1, source_target_pairs={{4,0},{8,4},{12,8},{5,1},{9,5},{13,9},{6,2},{10,6},{14,10},{7,3},{... | collective-permute-start | bytes 430088 | tf_op jit(solution)/shard_map/ppermute | solution.py:445
  34.2 10.3 %collective-permute-start.9 = (bf16[5,128,128]{2,1,0:T(8,128)(2,1)S(1)}, bf16[5,128,128]{2,1,0:T(8,128)(2,1)S(1)}, u32[]{:S(2)}, u32[]{:S(2)}) collective-permute-start(bf16[5,128,128]{2,1,0:T(8,128)(2,1)S(1)} %get-tuple-element.48), channel_id=1, source_target_pairs={{0,2},{2,0},{1,3},{3,1},{4,6},{6,4},{5,7},{7,5},{8,10},{10,8},{9,1... | collective-permute-start | bytes 491528 | tf_op jit(solution)/shard_map/ppermute | solution.py:469
  35.2 1.9 %collective-permute-start.12 = (bf16[2,2,5632]{2,1,0:T(2,128)(2,1)S(1)}, bf16[2,2,5632]{2,1,0:T(2,128)(2,1)S(1)}, u32[]{:S(2)}, u32[]{:S(2)}) collective-permute-start(bf16[2,2,5632]{2,1,0:T(2,128)(2,1)S(1)} %constant_dynamic-slice_fusion), channel_id=1, source_target_pairs={{0,1},{1,0},{2,3},{3,2},{4,5},{5,4},{6,7},{7,6},{8,9},{9,8},{10,11... | collective-permute-start | bytes 135176 | tf_op jit(solution)/shard_map/ppermute | solution.py:674
  37.0 14.6 %copy-start.1 = (bf16[1,8,16,1120]{3,2,1,0:T(8,128)(2,1)S(1)}, bf16[1,8,16,1120]{3,2,1,0:T(8,128)(2,1)}, u32[]{:S(2)}) copy-start(bf16[1,8,16,1120]{3,2,1,0:T(8,128)(2,1)} %param.8) | copy-start | bytes 860164
  37.1 14.6 %copy-start.2 = (bf16[1,8,16,1120]{3,2,1,0:T(8,128)(2,1)S(1)}, bf16[1,8,16,1120]{3,2,1,0:T(8,128)(2,1)}, u32[]{:S(2)}) copy-start(bf16[1,8,16,1120]{3,2,1,0:T(8,128)(2,1)} %param.9) | copy-start | bytes 860164
  45.4 5.1 %collective-permute-start.13 = (f32[280,128]{1,0:T(8,128)S(1)}, f32[280,128]{1,0:T(8,128)S(1)}, u32[]{:S(2)}, u32[]{:S(2)}) collective-permute-start(f32[280,128]{1,0:T(8,128)S(1)} %multiply_add_fusion.here_ref), channel_id=1, source_target_pairs={{0,2},{2,0},{1,3},{3,1},{4,6},{6,4},{5,7},{7,5},{8,10},{10,8},{9,1... | collective-permute-start | bytes 430088 | tf_op jit(solution)/shard_map/ppermute | solution.py:478
  46.0 5.7 %collective-permute-start.15 = (f32[280,128]{1,0:T(8,128)S(1)}, f32[280,128]{1,0:T(8,128)S(1)}, u32[]{:S(2)}, u32[]{:S(2)}) collective-permute-start(f32[280,128]{1,0:T(8,128)S(1)} %multiply_add_fusion.here_ref), channel_id=1, source_target_pairs={{0,1},{1,0},{2,3},{3,2},{4,5},{5,4},{6,7},{7,6},{8,9},{9,8},{10,11... | collective-permute-start | bytes 430088 | tf_op jit(solution)/shard_map/ppermute | solution.py:479
  50.5 2.2 %collective-permute-start.14 = (f32[280,128]{1,0:T(8,128)S(1)}, f32[280,128]{1,0:T(8,128)S(1)}, u32[]{:S(2)}, u32[]{:S(2)}) collective-permute-start(f32[280,128]{1,0:T(8,128)S(1)} %collective-permute-done.13.here_ref), channel_id=1, source_target_pairs={{0,1},{1,0},{2,3},{3,2},{4,5},{5,4},{6,7},{7,6},{8,9},{9,8},{10,11... | collective-permute-start | bytes 430088 | tf_op jit(solution)/shard_map/ppermute | solution.py:485

commit v4 on v3

--- a/solution.py
+++ b/solution.py
@@ -220,9 +220,10 @@
     return jnp.where(column == 0, first, 0.0).astype(jnp.bfloat16)
 
 
-def vmem_call(kernel, out_shape, scratch=(), smem_first=False, n_in=0, flops=0, bytes_accessed=0, vmem_mib=8, in_hbm=False, out_hbm=False):
+def vmem_call(kernel, out_shape, scratch=(), smem_first=False, n_in=0, flops=0, bytes_accessed=0, vmem_mib=8, in_hbm=False, out_hbm=False, n_given=0):
     vmem = pl.BlockSpec(memory_space=pltpu.VMEM)
     in_specs = [pl.BlockSpec(memory_space=pltpu.HBM) if in_hbm else vmem] * n_in
+    in_specs += [pl.BlockSpec(memory_space=pltpu.HBM)] * n_given
     if smem_first:
         in_specs[0] = pl.BlockSpec(memory_space=pltpu.SMEM)
     return pl.pallas_call(
@@ -231,6 +232,7 @@
         in_specs=in_specs,
         out_specs=jax.tree.map(lambda _: pl.BlockSpec(memory_space=pltpu.HBM) if out_hbm else vmem, out_shape),
         scratch_shapes=list(scratch),
+        input_output_aliases={n_in: 0} if n_given else {},
         cost_estimate=pl.CostEstimate(flops=flops, bytes_accessed=bytes_accessed, transcendentals=0),
         compiler_params=pltpu.CompilerParams(vmem_limit_bytes=vmem_mib << 20),
     )
@@ -286,21 +288,7 @@
     other_ref[...] = keep_ref[1 - row] + came_ref[1 - row]
 
 
-def heads_kernel(query_hbm, cotangent_hbm, mine_ref, other_ref, groups, query_ref, cotangent_ref, sems):
-    stage((query_hbm, cotangent_hbm), (query_ref, cotangent_ref), sems)
-    none = tail_block(query_ref.shape[0], 0.0)
-    per_group = HEADS // 2
-    row = lax.axis_index("height")
-    for head in range(HEADS):
-        group, place = divmod(head, per_group)
-        feature = jnp.maximum(head_slice(query_ref, head), 0)
-        groups[group, 0, place] = jnp.concatenate([feature, none], axis=1)
-        groups[group, 1, place] = jnp.concatenate([head_slice(cotangent_ref, head), none], axis=1)
-    mine_ref[...] = groups[row]
-    other_ref[...] = groups[1 - row]
-
-
-def mask_kernel(clip_ref, out_ref):
+def write_masks(clip_ref, out_ref):
     frame = lax.axis_index("tm")
     last = lax.axis_size("tm") - 1
     here = clip_ref[frame]
@@ -312,6 +300,24 @@
         same = inside & (clip_ref[jnp.clip(other, 0, last)] == here)
         masks = jnp.where(line == at, jnp.where(same, 1.0, 0.0), masks)
     out_ref[...] = masks
+
+
+def heads_kernel(query_hbm, cotangent_hbm, clip_hbm, mine_ref, other_ref, mask_ref, groups, query_ref, cotangent_ref, sems, clip_ref, clip_sem):
+    clip_copy = pltpu.make_async_copy(clip_hbm, clip_ref, clip_sem)
+    clip_copy.start()
+    stage((query_hbm, cotangent_hbm), (query_ref, cotangent_ref), sems)
+    clip_copy.wait()
+    write_masks(clip_ref, mask_ref)
+    none = tail_block(query_ref.shape[0], 0.0)
+    per_group = HEADS // 2
+    row = lax.axis_index("height")
+    for head in range(HEADS):
+        group, place = divmod(head, per_group)
+        feature = jnp.maximum(head_slice(query_ref, head), 0)
+        groups[group, 0, place] = jnp.concatenate([feature, none], axis=1)
+        groups[group, 1, place] = jnp.concatenate([head_slice(cotangent_ref, head), none], axis=1)
+    mine_ref[...] = groups[row]
+    other_ref[...] = groups[1 - row]
 
 
 def query_kernel(state_ref, came_ref, mine_ref, other_ref, keep_ref, send_ref, own_out, other_out, state, halves):
@@ -416,9 +422,6 @@
     share = struct((half, LANES))
     pair = struct((2, half, LANES))
 
-    masks = vmem_call(mask_kernel, struct((8, LANES)), smem_first=True, n_in=1, bytes_accessed=4096)(
-        pltpu.with_memory_space_constraint(clip_ids, pltpu.HBM)
-    )
     key_hbm, value_hbm = (
         pltpu.with_memory_space_constraint(part, pltpu.HBM) for part in (key, value)
     )
@@ -427,17 +430,26 @@
         state_kernel, (pair, pair), [pltpu.VMEM((2, 2, half, LANES), jnp.float32), *staged], n_in=2, in_hbm=True,
         flops=2 * tokens * flat * LANES, bytes_accessed=4 * tokens * flat + 8 * half * LANES * 2,
     )(key_hbm, value_hbm)
+    hidden, send = lax.optimization_barrier((hidden_pre, send))
+    edges = row_edges(hidden)
     came = lax.ppermute(send, "width", SWAP)
+    came, edges = lax.optimization_barrier((came, edges))
     mine, other = vmem_call(pick_kernel, (share, share), n_in=2, bytes_accessed=24 * half * LANES)(keep, came)
     came = lax.ppermute(other, "height", SWAP)
 
     packed = struct((2, per_group, tokens, LANES), jnp.bfloat16)
-    query, cotangent, mine = lax.optimization_barrier((query, cotangent, mine))
-    heads_mine, heads_other = vmem_call(
-        heads_kernel, (packed, packed), [pltpu.VMEM((2, 2, per_group, tokens, LANES), jnp.bfloat16), *staged], n_in=2, in_hbm=True,
-        bytes_accessed=12 * tokens * flat,
-    )(*(pltpu.with_memory_space_constraint(part, pltpu.HBM) for part in (query, cotangent)))
-    _, own = lax.optimization_barrier((heads_other, mine + came))
+    query, cotangent, hidden, _ = lax.optimization_barrier((query, cotangent, hidden, mine))
+    heads_mine, heads_other, masks = vmem_call(
+        heads_kernel,
+        (packed, packed, struct((8, LANES))),
+        [pltpu.VMEM((2, 2, per_group, tokens, LANES), jnp.bfloat16), *staged,
+         pltpu.SMEM(clip_ids.shape, jnp.int32), pltpu.SemaphoreType.DMA],
+        n_in=3, in_hbm=True, bytes_accessed=12 * tokens * flat,
+    )(*(pltpu.with_memory_space_constraint(part, pltpu.HBM) for part in (query, cotangent, clip_ids)))
+    side = side_edge(hidden[0])
+    edges, _ = lax.optimization_barrier((edges, heads_other))
+    halo = halo_arrays(edges, side)
+    _, own = lax.optimization_barrier(((heads_other, side), mine + came))
     heads_sent = lax.ppermute(heads_other, "height", SWAP)
 
     def along_frames(own, step, beside):
@@ -449,11 +461,9 @@
         return own + masks[at : at + 1] * near + masks[at + 1 : at + 2] * far, beside
 
     def fetch(own, near, far):
-        block, _ = lax.optimization_barrier((hidden_pre, own))
-        near, far, arrived = lax.optimization_barrier((near, far, heads_sent))
-        return near, far, (halo_arrays(block), arrived)
-
-    state, (halo, heads_came) = along_frames(own, 1, fetch)
+        return lax.optimization_barrier((near, far, heads_sent))
+
+    state, heads_came = along_frames(own, 1, fetch)
     came = lax.ppermute(state, "width", SWAP)
     back = struct((per_group, tokens, LANES), jnp.bfloat16)
     keep, send, back_mine, back_other = vmem_call(
@@ -462,7 +472,7 @@
         flops=14 * tokens * flat * LANES, bytes_accessed=8 * tokens * flat,
     )(state, came, heads_mine, heads_came)
     came = lax.ppermute(send, "width", SWAP)
-    own = keep + came
+    own, halo = lax.optimization_barrier((keep + came, halo))
 
     def convolve(own, near, far):
         other, _ = lax.optimization_barrier((back_other, own))
@@ -471,8 +481,8 @@
         query_grad = vmem_call(
             join_kernel, struct((tokens, flat), jnp.bfloat16), n_in=2, bytes_accessed=4 * tokens * flat
         )(back_mine, back_came)
-        near, far, grads = lax.optimization_barrier((near, far, (query_grad, hidden_grad)))
-        return near, far, grads
+        near, far, hidden_grad = lax.optimization_barrier((near, far, hidden_grad))
+        return near, far, (query_grad, hidden_grad)
 
     total, (query_grad, hidden_grad) = along_frames(own, -1, convolve)
     far = lax.ppermute(total, "height", SWAP)
@@ -482,6 +492,7 @@
     near_grads = vmem_call(functools.partial(key_kernel, True), (back, back), state, n_in=4, **cost)(
         key, value, total, near_came
     )
+    far, query_grad = lax.optimization_barrier((far, query_grad))
     far_came = lax.ppermute(far, "width", SWAP)
     out = struct((tokens, flat), jnp.bfloat16)
     key_grad, value_gradient = vmem_call(functools.partial(key_kernel, False), (out, out), state, n_in=6, **cost)(
@@ -510,13 +521,15 @@
 
 TILES = 8
 REACH = 2
-
-
-def conv_kernel(rows_per_frame, row_refs, *refs):
+UNROLL = 2
+
+
+def conv_kernel(bases, row_refs, *refs):
     halo_rows, refs = refs[:row_refs], refs[row_refs:]
     side_ref, refs = refs[0], refs[1:]
     corners, refs = refs[:row_refs], refs[row_refs:]
-    block_ref, weight_ref, out_hbm, taps, value_in, gate_in, value_grad, gate_grad, value_out, gate_out, out_ref, sems = refs
+    block_ref, weight_ref = refs[:2]
+    out_hbm, taps, value_in, gate_in, value_grad, gate_grad, *results, out_ref, sems = refs[-8 - 2 * UNROLL :]
     rows, cols, channels = block_ref.shape
     lane_tiles = channels // LANES // 2
     pitch = -(-lane_tiles // TILES) * TILES
@@ -525,9 +538,11 @@
     wide, tall = cols + 2 * REACH, rows + 2 * REACH
     grad_wide = wide - 2
 
-    for tile in range(2 * lane_tiles):
-        place = tile if tile < lane_tiles else pitch + tile - lane_tiles
-        taps[pl.ds(place, 9, stride=2 * pitch), :] = weight_ref[:, tile * LANES : (tile + 1) * LANES]
+    for base in bases:
+        for tile in range(base, min(base + TILES, lane_tiles)):
+            for place, source in ((tile, tile), (pitch + tile, lane_tiles + tile)):
+                lanes = slice(source * LANES, (source + 1) * LANES)
+                taps[pl.ds(place, 9, stride=2 * pitch), :] = weight_ref[:, lanes]
 
     def source_at(at_row, at_col):
         return pl.multiple_of((at_row * wide + at_col) * TILES, TILES)
@@ -561,7 +576,7 @@
                     ref[pl.ds(grad_at(at, col), TILES), :] = zero
 
     copies = []
-    for base in range(0, lane_tiles, TILES):
+    for base in bases:
         count = min(TILES, lane_tiles - base)
 
         def spread(load, at_row, at_col, length):
@@ -620,27 +635,36 @@
                 value_grad[place, :] = glu * gated
                 gate_grad[place, :] = glu * value * (squash + gated * (1.0 - squash))
 
-        @pl.loop(0, rows)
-        def _(at):
-            for ref, kernel, result in ((value_grad, value_taps, value_out), (gate_grad, gate_taps, gate_out)):
-                cache = {}
-
-                def read(a, col):
-                    if (a, col) not in cache:
-                        cache[a, col] = ref[pl.ds(grad_at(at + a, col), TILES), :]
-                    return cache[a, col]
-
-                for col in range(cols):
+        def gather(at, results):
+            cache = {}
+
+            def read(ref, a, col):
+                if (id(ref), a, col) not in cache:
+                    cache[id(ref), a, col] = ref[pl.ds(grad_at(at + a, col), TILES), :]
+                return cache[id(ref), a, col]
+
+            for col in range(cols):
+                for ref, kernel, result in zip((value_grad, gate_grad), (value_taps, gate_taps), results):
                     total = None
                     for a in (-1, 0, 1):
                         for b in (-1, 0, 1):
-                            term = kernel[3 * (a + 1) + b + 1] * read(1 - a, col + 1 - b)
+                            term = kernel[3 * (a + 1) + b + 1] * read(ref, 1 - a, col + 1 - b)
                             total = term if total is None else total + term
-                    result[col * TILES : (col + 1) * TILES, :] = total
-            for result, offset in ((value_out, base), (gate_out, lane_tiles + base)):
+                    result[pl.ds(col, TILES, stride=cols), :] = total
+
+        def settle(at, results):
+            for result, offset in zip(results, (base, lane_tiles + base)):
                 for tile in range(count):
                     lanes = slice((offset + tile) * LANES, (offset + tile + 1) * LANES)
-                    out_ref[at, :, lanes] = result[pl.ds(tile, cols, stride=TILES), :].astype(jnp.bfloat16)
+                    out_ref[at, :, lanes] = result[tile * cols : (tile + 1) * cols, :].astype(jnp.bfloat16)
+
+        @pl.loop(0, rows // UNROLL)
+        def _(at):
+            for step in range(UNROLL):
+                gather(at * UNROLL + step, results[2 * step : 2 * step + 2])
+                if step:
+                    settle(at * UNROLL + step - 1, results[2 * step - 2 : 2 * step])
+            settle(at * UNROLL + UNROLL - 1, results[2 * UNROLL - 2 :])
 
         for at, offset in enumerate((base, lane_tiles + base)):
             lanes = pl.ds(offset * LANES, count * LANES)
@@ -651,33 +675,36 @@
         copy.wait()
 
 
-def edge_slice(block, axis_name, dim, low_side):
+def edge_slice(block, dim, low_side):
     start = jnp.where(low_side, 0, block.shape[dim] - REACH)
     return lax.dynamic_slice_in_dim(block, start, REACH, axis=dim)
 
 
-def halo_arrays(hidden_pre):
+def row_edges(hidden_pre):
     block = hidden_pre[0]
+    if lax.axis_size("height") == 2:
+        return [edge_slice(block, 0, lax.axis_index("height") == 1)]
+    return [block[block.shape[0] - REACH :], block[:REACH]]
+
+
+def side_edge(block):
+    return edge_slice(block, 1, lax.axis_index("width") == 1)
+
+
+def halo_arrays(edges, side):
     height = lax.axis_size("height")
-    column = lax.axis_index("width")
     if height == 2:
-        edge = edge_slice(block, "height", 0, lax.axis_index("height") == 1)
-        halo_rows = [lax.ppermute(edge, "height", SWAP)]
+        moves = [SWAP]
     else:
-        up = [(at, at + 1) for at in range(height - 1)]
-        down = [(at + 1, at) for at in range(height - 1)]
-        halo_rows = [
-            lax.ppermute(block[block.shape[0] - REACH :], "height", up),
-            lax.ppermute(block[:REACH], "height", down),
-        ]
-    side = lax.ppermute(edge_slice(block, "width", 1, column == 1), "width", SWAP)
-    corners = [lax.ppermute(edge_slice(part, "width", 1, column == 1), "width", SWAP) for part in halo_rows]
+        moves = [[(at, at + 1) for at in range(height - 1)], [(at + 1, at) for at in range(height - 1)]]
+    halo_rows = [lax.ppermute(edge, "height", move) for edge, move in zip(edges, moves)]
+    side = lax.ppermute(side, "width", SWAP)
+    corners = [lax.ppermute(side_edge(part), "width", SWAP) for part in halo_rows]
     return halo_rows, side, corners
 
 
-def ffn(hidden_pre, conv_weight, halo):
+def conv_part(bases, halo, block, conv_weight, given=()):
     halo_rows, side, corners = halo
-    block = hidden_pre[0]
     rows, cols, channels = block.shape
     lane_tiles = channels // LANES // 2
     pitch = -(-lane_tiles // TILES) * TILES
@@ -685,14 +712,23 @@
     grad = pltpu.VMEM(((rows + 2) * (cols + 2) * TILES, LANES), jnp.float32)
     result = pltpu.VMEM((cols * TILES, LANES), jnp.float32)
     size = rows * cols * channels
-    hidden_grad = vmem_call(
-        functools.partial(conv_kernel, rows, len(halo_rows)),
+    return vmem_call(
+        functools.partial(conv_kernel, bases, len(halo_rows)),
         struct((rows, cols, channels), jnp.bfloat16),
-        [pltpu.VMEM((9 * 2 * pitch, LANES), jnp.float32), source, source, grad, grad, result, result,
+        [pltpu.VMEM((9 * 2 * pitch, LANES), jnp.float32), source, source, grad, grad, *[result] * (2 * UNROLL),
          pltpu.VMEM((rows, cols, channels), jnp.bfloat16), pltpu.SemaphoreType.DMA((2, pitch // TILES))],
-        n_in=2 * len(halo_rows) + 3, flops=2 * size, bytes_accessed=size, vmem_mib=12, out_hbm=True,
-    )(*halo_rows, side, *corners, block, conv_weight)
-    return hidden_grad[None]
+        n_in=2 * len(halo_rows) + 3, n_given=len(given), flops=size * len(bases), bytes_accessed=size, vmem_mib=12,
+        out_hbm=True,
+    )(*halo_rows, side, *corners, block, conv_weight, *given)
+
+
+def conv_bases(hidden_pre):
+    lane_tiles = hidden_pre.shape[3] // LANES // 2
+    return list(range(0, lane_tiles, TILES))
+
+
+def ffn(hidden_pre, conv_weight, halo):
+    return conv_part(conv_bases(hidden_pre), halo, hidden_pre[0], conv_weight)[None]
 
 
 def per_device(queries, attn_keys, attn_values, attn_cotangent, clip_ids, hidden_pre, conv_weight):
@@ -702,7 +738,7 @@
         return paired(queries, attn_keys, attn_values, attn_cotangent, clip_ids, hidden_pre, conv_weight)
     grads = general_attention(queries, attn_keys, attn_values, attn_cotangent, clip_ids)
     if blocked:
-        return (*grads, ffn(hidden_pre, conv_weight, halo_arrays(hidden_pre)))
+        return (*grads, ffn(hidden_pre, conv_weight, halo_arrays(row_edges(hidden_pre), side_edge(hidden_pre[0]))))
     return (*grads, mixed_ffn(hidden_pre, conv_weight))
 
 

time: 54.3 us -> 52.5 us (0.967)
  the two profiles are of different devices: /device:TPU:25 before, /device:TPU:9 now
where the time goes in v4:
time: 52.5 us; the launch traced here: 52.2 us
  starting transfers between devices  19.3 us (37%)
  Pallas kernels  17.2 us (33%)
  waiting for transfers between devices  13.5 us (26%)
  local copies, waits for them, and re-layouts  1.28 us (2%)
  between operations  0.78 us (1%)
    pallas_call x1, Pallas kernels, conv_part(): vmem_call(functools.partial(conv_kernel, bases, len(halo_rows)), struct((...  7.5 us
    ppermute x2, starting transfers between devices, along_frames(): far = lax.ppermute(own, 'tm', moves[1])  5.5 us
    ppermute x2, waiting for transfers between devices, along_frames(): near = lax.ppermute(own, 'tm', moves[0])  4.69 us
    ppermute x2, waiting for transfers between devices, along_frames(): far = lax.ppermute(own, 'tm', moves[1])  4.48 us
    ppermute x2, starting transfers between devices, along_frames(): near = lax.ppermute(own, 'tm', moves[0])  3.84 us
    pallas_call x1, Pallas kernels, paired(): vmem_call(query_kernel, (share, share, back, back), [pltpu.VMEM((2, half,...  2.97 us
    pallas_call x1, Pallas kernels, paired(): vmem_call(state_kernel, (pair, pair), [pltpu.VMEM((2, 2, half, LANES), jn...  2.12 us
    pallas_call x1, Pallas kernels, paired(): vmem_call(heads_kernel, (packed, packed, struct((8, LANES))), [pltpu.VMEM...  1.7 us
  transfers between devices with their start and end apart: 16, of which 10 were waited for; matrix products, arithmetic and copies ran while one was open for 3% of the time, Pallas kernels for 26%

profile of v4, /device:TPU:9, one launch (start us, length us, event | category | flops | bytes accessed | tf_op | source)
XLA Modules:
  0.0 52.2 jit_solution(16822318593447459037)
XLA Ops:
  0.6 2.1 %shard_map.102 = (f32[2,280,128]{2,1,0:T(8,128)S(1)}, f32[2,280,128]{2,1,0:T(8,128)S(1)}) custom-call(bf16[128,1120]{1,0:T(8,128)(2,1)} %bitcast.22, bf16[128,1120]{1,0:T(8,128)(2,1)} %bitcast.25), custom_call_target="tpu_custom_call" | custom-call | flops 36700160 | bytes 1146880 | tf_op jit(solution)/shard_map/pallas_call | solution.py:429
  2.8 0.7 %collective-permute-start = (f32[2,280,128]{2,1,0:T(8,128)S(1)}, f32[2,280,128]{2,1,0:T(8,128)S(1)}, u32[]{:S(2)}, u32[]{:S(2)}) collective-permute-start(f32[2,280,128]{2,1,0:T(8,128)S(1)} %get-tuple-element.44), channel_id=1, source_target_pairs={{0,1},{1,0},{2,3},{3,2},{4,5},{5,4},{6,7},{7,6},{8,9},{9,8},{10,11... | collective-permute-start | bytes 860168 | tf_op jit(solution)/shard_map/ppermute | solution.py:435
  3.5 1.0 %dynamic-slice_bitcast_fusion = bf16[2,16,5632]{2,1,0:T(8,128)(2,1)S(1)} fusion(bf16[1,8,16,5632]{3,2,1,0:T(8,128)(2,1)} %param.12, s32[]{:T(128)S(6)} %select_n.11), kind=kLoop, calls=%fused_computation | loop fusion | bytes 720900 | tf_op jit(solution)/shard_map/dynamic_slice | solution.py:680
  4.7 1.3 %collective-permute-start.1 = (f32[280,128]{1,0:T(8,128)S(1)}, f32[280,128]{1,0:T(8,128)S(1)}, u32[]{:S(2)}, u32[]{:S(2)}) collective-permute-start(f32[280,128]{1,0:T(8,128)S(1)} %get-tuple-element.51), channel_id=1, source_target_pairs={{0,2},{2,0},{1,3},{3,1},{4,6},{6,4},{5,7},{7,5},{8,10},{10,8},{9,1... | collective-permute-start | bytes 430088 | tf_op jit(solution)/shard_map/ppermute | solution.py:438
  6.0 1.7 %shard_map.104 = (bf16[2,5,128,128]{3,2,1,0:T(8,128)(2,1)S(1)}, bf16[2,5,128,128]{3,2,1,0:T(8,128)(2,1)S(1)}, f32[8,128]{1,0:T(8,128)S(1)}) custom-call(bf16[128,1120]{1,0:T(8,128)(2,1)} %bitcast.30, bf16[128,1120]{1,0:T(8,128)(2,1)} %bitcast.31, s32[4]{0:T(128)} %clip_hbm.1), custom_call_target="tpu_custom_call" | custom-call | bytes 1720320 | tf_op jit(solution)/shard_map/pallas_call | solution.py:442
  7.7 0.3 collective-permute-start.4
  8.1 1.2 %collective-permute-start.7 = (bf16[2,16,5632]{2,1,0:T(8,128)(2,1)S(1)}, bf16[2,16,5632]{2,1,0:T(8,128)(2,1)S(1)}, u32[]{:S(2)}, u32[]{:S(2)}) collective-permute-start(bf16[2,16,5632]{2,1,0:T(8,128)(2,1)S(1)} %dynamic-slice_bitcast_fusion), channel_id=1, source_target_pairs={{0,2},{2,0},{1,3},{3,1},{4,6},{6,4},{5,7},{7,5},{8,10},{10,8},{9,1... | collective-permute-start | bytes 1081352 | tf_op jit(solution)/shard_map/ppermute | solution.py:700
  9.5 0.3 collective-permute-done.1
  9.8 4.2 %collective-permute-start.3 = (f32[280,128]{1,0:T(8,128)S(1)}, f32[280,128]{1,0:T(8,128)S(1)}, u32[]{:S(2)}, u32[]{:S(2)}) collective-permute-start(f32[280,128]{1,0:T(8,128)S(1)} %add.21), channel_id=1, source_target_pairs={{0,8},{4,12},{1,9},{5,13},{2,10},{6,14},{3,11},{7,15},{16,24},{20,... | collective-permute-start | bytes 430088 | tf_op jit(solution)/shard_map/ppermute | solution.py:458
  14.0 1.9 %collective-permute-start.2 = (f32[280,128]{1,0:T(8,128)S(1)}, f32[280,128]{1,0:T(8,128)S(1)}, u32[]{:S(2)}, u32[]{:S(2)}) collective-permute-start(f32[280,128]{1,0:T(8,128)S(1)} %add.21), channel_id=1, source_target_pairs={{0,4},{4,8},{8,12},{1,5},{5,9},{9,13},{2,6},{6,10},{10,14},{3,7},{... | collective-permute-start | bytes 430088 | tf_op jit(solution)/shard_map/ppermute | solution.py:457
  16.0 4.5 %collective-permute-done.3 = f32[280,128]{1,0:T(8,128)S(1)} collective-permute-done((f32[280,128]{1,0:T(8,128)S(1)}, f32[280,128]{1,0:T(8,128)S(1)}, u32[]{:S(2)}, u32[]{:S(2)}) %collective-permute-start.3) | collective-permute-done | bytes 143392 | tf_op jit(solution)/shard_map/ppermute | solution.py:458
  20.5 3.1 %collective-permute-done.2 = f32[280,128]{1,0:T(8,128)S(1)} collective-permute-done((f32[280,128]{1,0:T(8,128)S(1)}, f32[280,128]{1,0:T(8,128)S(1)}, u32[]{:S(2)}, u32[]{:S(2)}) %collective-permute-start.2) | collective-permute-done | bytes 143392 | tf_op jit(solution)/shard_map/ppermute | solution.py:457
  23.6 0.6 %collective-permute-start.5 = (f32[280,128]{1,0:T(8,128)S(1)}, f32[280,128]{1,0:T(8,128)S(1)}, u32[]{:S(2)}, u32[]{:S(2)}) collective-permute-start(f32[280,128]{1,0:T(8,128)S(1)} %multiply_add_fusion.1.state_ref), channel_id=1, source_target_pairs={{0,1},{1,0},{2,3},{3,2},{4,5},{5,4},{6,7},{7,6},{8,9},{9,8},{10,11... | collective-permute-start | bytes 430088 | tf_op jit(solution)/shard_map/ppermute | solution.py:467
  24.2 0.9 %collective-permute-done.5.came_ref = f32[280,128]{1,0:T(8,128)S(1)} collective-permute-done((f32[280,128]{1,0:T(8,128)S(1)}, f32[280,128]{1,0:T(8,128)S(1)}, u32[]{:S(2)}, u32[]{:S(2)}) %collective-permute-start.5) | collective-permute-done | bytes 143392 | tf_op jit(solution)/shard_map/ppermute | solution.py:467
  25.2 3.0 %shard_map.105 = (f32[280,128]{1,0:T(8,128)S(1)}, f32[280,128]{1,0:T(8,128)S(1)}, bf16[5,128,128]{2,1,0:T(8,128)(2,1)S(1)}, bf16[5,128,128]{2,1,0:T(8,128)(2,1)S(1)}) custom-call(f32[280,128]{1,0:T(8,128)S(1)} %multiply_add_fusion.1.state_ref, f32[280,128]{1,0:T(8,128)S(1)} %collective-permute-done.5.came_ref, ...), custom_call_target="tpu_custom_call" | custom-call | flops 256901120 | bytes 1146880 | tf_op jit(solution)/shard_map/pallas_call | solution.py:469
  28.1 0.4 collective-permute-start.6
  28.6 0.2 collective-permute-start.9
  28.8 0.7 %collective-permute-done.6 = f32[280,128]{1,0:T(8,128)S(1)} collective-permute-done((f32[280,128]{1,0:T(8,128)S(1)}, f32[280,128]{1,0:T(8,128)S(1)}, u32[]{:S(2)}, u32[]{:S(2)}) %collective-permute-start.6) | collective-permute-done | bytes 143392 | tf_op jit(solution)/shard_map/ppermute | solution.py:474
  29.6 0.3 collective-permute-done.9.refs_2_
  29.9 1.3 %collective-permute-start.11 = (f32[280,128]{1,0:T(8,128)S(1)}, f32[280,128]{1,0:T(8,128)S(1)}, u32[]{:S(2)}, u32[]{:S(2)}) collective-permute-start(f32[280,128]{1,0:T(8,128)S(1)} %add.24), channel_id=1, source_target_pairs={{8,0},{12,4},{9,1},{13,5},{10,2},{14,6},{11,3},{15,7},{24,16},{28,... | collective-permute-start | bytes 430088 | tf_op jit(solution)/shard_map/ppermute | solution.py:458
  31.2 1.9 %collective-permute-start.10 = (f32[280,128]{1,0:T(8,128)S(1)}, f32[280,128]{1,0:T(8,128)S(1)}, u32[]{:S(2)}, u32[]{:S(2)}) collective-permute-start(f32[280,128]{1,0:T(8,128)S(1)} %add.24), channel_id=1, source_target_pairs={{4,0},{8,4},{12,8},{5,1},{9,5},{13,9},{6,2},{10,6},{14,10},{7,3},{... | collective-permute-start | bytes 430088 | tf_op jit(solution)/shard_map/ppermute | solution.py:457
  33.1 1.2 %collective-permute-start.13 = (bf16[5,128,128]{2,1,0:T(8,128)(2,1)S(1)}, bf16[5,128,128]{2,1,0:T(8,128)(2,1)S(1)}, u32[]{:S(2)}, u32[]{:S(2)}) collective-permute-start(bf16[5,128,128]{2,1,0:T(8,128)(2,1)S(1)} %get-tuple-element.70), channel_id=1, source_target_pairs={{0,2},{2,0},{1,3},{3,1},{4,6},{6,4},{5,7},{7,5},{8,10},{10,8},{9,1... | collective-permute-start | bytes 491528 | tf_op jit(solution)/shard_map/ppermute | solution.py:479
  34.4 7.5 %shard_map.106 = bf16[8,16,5632]{2,1,0:T(8,128)(2,1)} custom-call(bf16[2,16,5632]{2,1,0:T(8,128)(2,1)S(1)} %collective-permute-done.7.refs_0_, bf16[8,2,5632]{2,1,0:T(2,128)(2,1)S(1)} %collective-permute-done.8.refs_1_, bf16[2,2,5632]{2,1,0:T(2,128)(2,1)S(1)} %collective-permute-done.9.refs_2_, bf16[8,16,5632]{2,1,0:T(8,128)(2,1)S(1)} %bitcast.21, ...), custom_call_target="tpu_custom_call" | custom-call | flops 2162688 | bytes 720896 | tf_op jit(solution)/shard_map/pallas_call | solution.py:715
  41.9 1.6 %collective-permute-done.10 = f32[280,128]{1,0:T(8,128)S(1)} collective-permute-done((f32[280,128]{1,0:T(8,128)S(1)}, f32[280,128]{1,0:T(8,128)S(1)}, u32[]{:S(2)}, u32[]{:S(2)}) %collective-permute-start.10) | collective-permute-done | bytes 143392 | tf_op jit(solution)/shard_map/ppermute | solution.py:457
  43.5 1.2 %collective-permute-start.12 = (f32[280,128]{1,0:T(8,128)S(1)}, f32[280,128]{1,0:T(8,128)S(1)}, u32[]{:S(2)}, u32[]{:S(2)}) collective-permute-start(f32[280,128]{1,0:T(8,128)S(1)} %multiply_add_fusion.here_ref), channel_id=1, source_target_pairs={{0,2},{2,0},{1,3},{3,1},{4,6},{6,4},{5,7},{7,5},{8,10},{10,8},{9,1... | collective-permute-start | bytes 430088 | tf_op jit(solution)/shard_map/ppermute | solution.py:488
  44.8 1.0 %collective-permute-start.15 = (f32[280,128]{1,0:T(8,128)S(1)}, f32[280,128]{1,0:T(8,128)S(1)}, u32[]{:S(2)}, u32[]{:S(2)}) collective-permute-start(f32[280,128]{1,0:T(8,128)S(1)} %multiply_add_fusion.here_ref), channel_id=1, source_target_pairs={{0,1},{1,0},{2,3},{3,2},{4,5},{5,4},{6,7},{7,6},{8,9},{9,8},{10,11... | collective-permute-start | bytes 430088 | tf_op jit(solution)/shard_map/ppermute | solution.py:489
  45.8 0.9 %shard_map.107 = bf16[128,1120]{1,0:T(8,128)(2,1)} custom-call(bf16[5,128,128]{2,1,0:T(8,128)(2,1)S(1)} %get-tuple-element.68.mine_ref, bf16[5,128,128]{2,1,0:T(8,128)(2,1)S(1)} %collective-permute-done.13.came_ref), custom_call_target="tpu_custom_call" | custom-call | bytes 573440 | tf_op jit(solution)/shard_map/pallas_call | solution.py:481
  46.7 1.4 %collective-permute-done.12.here_ref = f32[280,128]{1,0:T(8,128)S(1)} collective-permute-done((f32[280,128]{1,0:T(8,128)S(1)}, f32[280,128]{1,0:T(8,128)S(1)}, u32[]{:S(2)}, u32[]{:S(2)}) %collective-permute-start.12) | collective-permute-done | bytes 143392 | tf_op jit(solution)/shard_map/ppermute | solution.py:488
  48.2 1.6 %collective-permute-start.14 = (f32[280,128]{1,0:T(8,128)S(1)}, f32[280,128]{1,0:T(8,128)S(1)}, u32[]{:S(2)}, u32[]{:S(2)}) collective-permute-start(f32[280,128]{1,0:T(8,128)S(1)} %collective-permute-done.12.here_ref), channel_id=1, source_target_pairs={{0,1},{1,0},{2,3},{3,2},{4,5},{5,4},{6,7},{7,6},{8,9},{9,8},{10,11... | collective-permute-start | bytes 430088 | tf_op jit(solution)/shard_map/ppermute | solution.py:496
  49.8 0.6 %shard_map.108 = (bf16[5,128,128]{2,1,0:T(8,128)(2,1)S(1)}, bf16[5,128,128]{2,1,0:T(8,128)(2,1)S(1)}) custom-call(bf16[128,1120]{1,0:T(8,128)(2,1)S(1)} %bitcast.23, bf16[128,1120]{1,0:T(8,128)(2,1)S(1)} %bitcast.26, f32[280,128]{1,0:T(8,128)S(1)} %multiply_add_fusion.here_ref, f32[280,128]{1,0:T(8,128)S(1)} %collective-permute-done.15.came_ref), custom_call_target="tpu_custom_call" | custom-call | flops 73400320 | bytes 573440 | tf_op jit(solution)/shard_map/pallas_call | solution.py:492
  50.4 0.4 collective-permute-done.14.came_ref
  50.8 1.4 %shard_map.109 = (bf16[128,1120]{1,0:T(8,128)(2,1)}, bf16[128,1120]{1,0:T(8,128)(2,1)}) custom-call(bf16[128,1120]{1,0:T(8,128)(2,1)S(1)} %bitcast.24, bf16[128,1120]{1,0:T(8,128)(2,1)S(1)} %bitcast.27, f32[280,128]{1,0:T(8,128)S(1)} %collective-permute-done.12.here_ref, f32[280,128]{1,0:T(8,128)S(1)} %collective-permute-done.14.came_ref, ...), custom_call_target="tpu_custom_call" | custom-call | flops 73400320 | bytes 573440 | tf_op jit(solution)/shard_map/pallas_call | solution.py:498
  (24 shorter events, 0.7 us)
Async XLA Ops:
  0.6 8.6 %copy-start = (bf16[1,8,16,5632]{3,2,1,0:T(8,128)(2,1)S(1)}, bf16[1,8,16,5632]{3,2,1,0:T(8,128)(2,1)}, u32[]{:S(2)}) copy-start(bf16[1,8,16,5632]{3,2,1,0:T(8,128)(2,1)} %param.12) | copy-start | bytes 4325380
  2.8 1.9 %collective-permute-start = (f32[2,280,128]{2,1,0:T(8,128)S(1)}, f32[2,280,128]{2,1,0:T(8,128)S(1)}, u32[]{:S(2)}, u32[]{:S(2)}) collective-permute-start(f32[2,280,128]{2,1,0:T(8,128)S(1)} %get-tuple-element.44), channel_id=1, source_target_pairs={{0,1},{1,0},{2,3},{3,2},{4,5},{5,4},{6,7},{7,6},{8,9},{9,8},{10,11... | collective-permute-start | bytes 860168 | tf_op jit(solution)/shard_map/ppermute | solution.py:435
  4.7 5.0 %collective-permute-start.1 = (f32[280,128]{1,0:T(8,128)S(1)}, f32[280,128]{1,0:T(8,128)S(1)}, u32[]{:S(2)}, u32[]{:S(2)}) collective-permute-start(f32[280,128]{1,0:T(8,128)S(1)} %get-tuple-element.51), channel_id=1, source_target_pairs={{0,2},{2,0},{1,3},{3,1},{4,6},{6,4},{5,7},{7,5},{8,10},{10,8},{9,1... | collective-permute-start | bytes 430088 | tf_op jit(solution)/shard_map/ppermute | solution.py:438
  7.7 26.6 %copy-start.3 = (f32[9,5632]{1,0:T(8,128)S(1)}, f32[9,5632]{1,0:T(8,128)}, u32[]{:S(2)}) copy-start(f32[9,5632]{1,0:T(8,128)} %refs_4_.1) | copy-start | bytes 608260
  7.7 15.8 %collective-permute-start.4 = (bf16[2,5,128,128]{3,2,1,0:T(8,128)(2,1)S(1)}, bf16[2,5,128,128]{3,2,1,0:T(8,128)(2,1)S(1)}, u32[]{:S(2)}, u32[]{:S(2)}) collective-permute-start(bf16[2,5,128,128]{3,2,1,0:T(8,128)(2,1)S(1)} %get-tuple-element.49), channel_id=1, source_target_pairs={{0,2},{2,0},{1,3},{3,1},{4,6},{6,4},{5,7},{7,5},{8,10},{10,8},{9,1... | collective-permute-start | bytes 983048 | tf_op jit(solution)/shard_map/ppermute | solution.py:453
  8.1 20.5 %collective-permute-start.7 = (bf16[2,16,5632]{2,1,0:T(8,128)(2,1)S(1)}, bf16[2,16,5632]{2,1,0:T(8,128)(2,1)S(1)}, u32[]{:S(2)}, u32[]{:S(2)}) collective-permute-start(bf16[2,16,5632]{2,1,0:T(8,128)(2,1)S(1)} %dynamic-slice_bitcast_fusion), channel_id=1, source_target_pairs={{0,2},{2,0},{1,3},{3,1},{4,6},{6,4},{5,7},{7,5},{8,10},{10,8},{9,1... | collective-permute-start | bytes 1081352 | tf_op jit(solution)/shard_map/ppermute | solution.py:700
  9.8 10.7 %collective-permute-start.3 = (f32[280,128]{1,0:T(8,128)S(1)}, f32[280,128]{1,0:T(8,128)S(1)}, u32[]{:S(2)}, u32[]{:S(2)}) collective-permute-start(f32[280,128]{1,0:T(8,128)S(1)} %add.21), channel_id=1, source_target_pairs={{0,8},{4,12},{1,9},{5,13},{2,10},{6,14},{3,11},{7,15},{16,24},{20,... | collective-permute-start | bytes 430088 | tf_op jit(solution)/shard_map/ppermute | solution.py:458
  14.0 9.5 %collective-permute-start.2 = (f32[280,128]{1,0:T(8,128)S(1)}, f32[280,128]{1,0:T(8,128)S(1)}, u32[]{:S(2)}, u32[]{:S(2)}) collective-permute-start(f32[280,128]{1,0:T(8,128)S(1)} %add.21), channel_id=1, source_target_pairs={{0,4},{4,8},{8,12},{1,5},{5,9},{9,13},{2,6},{6,10},{10,14},{3,7},{... | collective-permute-start | bytes 430088 | tf_op jit(solution)/shard_map/ppermute | solution.py:457
  23.6 1.6 %collective-permute-start.5 = (f32[280,128]{1,0:T(8,128)S(1)}, f32[280,128]{1,0:T(8,128)S(1)}, u32[]{:S(2)}, u32[]{:S(2)}) collective-permute-start(f32[280,128]{1,0:T(8,128)S(1)} %multiply_add_fusion.1.state_ref), channel_id=1, source_target_pairs={{0,1},{1,0},{2,3},{3,2},{4,5},{5,4},{6,7},{7,6},{8,9},{9,8},{10,11... | collective-permute-start | bytes 430088 | tf_op jit(solution)/shard_map/ppermute | solution.py:467
  24.2 5.4 %collective-permute-start.8 = (bf16[8,2,5632]{2,1,0:T(2,128)(2,1)S(1)}, bf16[8,2,5632]{2,1,0:T(2,128)(2,1)S(1)}, u32[]{:S(2)}, u32[]{:S(2)}) collective-permute-start(bf16[8,2,5632]{2,1,0:T(2,128)(2,1)S(1)} %dynamic-slice_bitcast_fusion.1), channel_id=1, source_target_pairs={{0,1},{1,0},{2,3},{3,2},{4,5},{5,4},{6,7},{7,6},{8,9},{9,8},{10,11... | collective-permute-start | bytes 540680 | tf_op jit(solution)/shard_map/ppermute | solution.py:701
  28.1 1.4 %collective-permute-start.6 = (f32[280,128]{1,0:T(8,128)S(1)}, f32[280,128]{1,0:T(8,128)S(1)}, u32[]{:S(2)}, u32[]{:S(2)}) collective-permute-start(f32[280,128]{1,0:T(8,128)S(1)} %get-tuple-element.59), channel_id=1, source_target_pairs={{0,1},{1,0},{2,3},{3,2},{4,5},{5,4},{6,7},{7,6},{8,9},{9,8},{10,11... | collective-permute-start | bytes 430088 | tf_op jit(solution)/shard_map/ppermute | solution.py:474
  28.6 1.3 %collective-permute-start.9 = (bf16[2,2,5632]{2,1,0:T(2,128)(2,1)S(1)}, bf16[2,2,5632]{2,1,0:T(2,128)(2,1)S(1)}, u32[]{:S(2)}, u32[]{:S(2)}) collective-permute-start(bf16[2,2,5632]{2,1,0:T(2,128)(2,1)S(1)} %constant_dynamic-slice_fusion), channel_id=1, source_target_pairs={{0,1},{1,0},{2,3},{3,2},{4,5},{5,4},{6,7},{7,6},{8,9},{9,8},{10,11... | collective-permute-start | bytes 135176 | tf_op jit(solution)/shard_map/ppermute | solution.py:702
  29.9 12.0 %collective-permute-start.11 = (f32[280,128]{1,0:T(8,128)S(1)}, f32[280,128]{1,0:T(8,128)S(1)}, u32[]{:S(2)}, u32[]{:S(2)}) collective-permute-start(f32[280,128]{1,0:T(8,128)S(1)} %add.24), channel_id=1, source_target_pairs={{8,0},{12,4},{9,1},{13,5},{10,2},{14,6},{11,3},{15,7},{24,16},{28,... | collective-permute-start | bytes 430088 | tf_op jit(solution)/shard_map/ppermute | solution.py:458
  31.2 12.3 %collective-permute-start.10 = (f32[280,128]{1,0:T(8,128)S(1)}, f32[280,128]{1,0:T(8,128)S(1)}, u32[]{:S(2)}, u32[]{:S(2)}) collective-permute-start(f32[280,128]{1,0:T(8,128)S(1)} %add.24), channel_id=1, source_target_pairs={{4,0},{8,4},{12,8},{5,1},{9,5},{13,9},{6,2},{10,6},{14,10},{7,3},{... | collective-permute-start | bytes 430088 | tf_op jit(solution)/shard_map/ppermute | solution.py:457
  33.1 12.7 %collective-permute-start.13 = (bf16[5,128,128]{2,1,0:T(8,128)(2,1)S(1)}, bf16[5,128,128]{2,1,0:T(8,128)(2,1)S(1)}, u32[]{:S(2)}, u32[]{:S(2)}) collective-permute-start(bf16[5,128,128]{2,1,0:T(8,128)(2,1)S(1)} %get-tuple-element.70), channel_id=1, source_target_pairs={{0,2},{2,0},{1,3},{3,1},{4,6},{6,4},{5,7},{7,5},{8,10},{10,8},{9,1... | collective-permute-start | bytes 491528 | tf_op jit(solution)/shard_map/ppermute | solution.py:479
  34.4 15.4 %copy-start.1 = (bf16[1,8,16,1120]{3,2,1,0:T(8,128)(2,1)S(1)}, bf16[1,8,16,1120]{3,2,1,0:T(8,128)(2,1)}, u32[]{:S(2)}) copy-start(bf16[1,8,16,1120]{3,2,1,0:T(8,128)(2,1)} %param.8) | copy-start | bytes 860164
  34.4 15.4 %copy-start.2 = (bf16[1,8,16,1120]{3,2,1,0:T(8,128)(2,1)S(1)}, bf16[1,8,16,1120]{3,2,1,0:T(8,128)(2,1)}, u32[]{:S(2)}) copy-start(bf16[1,8,16,1120]{3,2,1,0:T(8,128)(2,1)} %param.9) | copy-start | bytes 860164
  43.5 4.6 %collective-permute-start.12 = (f32[280,128]{1,0:T(8,128)S(1)}, f32[280,128]{1,0:T(8,128)S(1)}, u32[]{:S(2)}, u32[]{:S(2)}) collective-permute-start(f32[280,128]{1,0:T(8,128)S(1)} %multiply_add_fusion.here_ref), channel_id=1, source_target_pairs={{0,2},{2,0},{1,3},{3,1},{4,6},{6,4},{5,7},{7,5},{8,10},{10,8},{9,1... | collective-permute-start | bytes 430088 | tf_op jit(solution)/shard_map/ppermute | solution.py:488
  44.8 5.0 %collective-permute-start.15 = (f32[280,128]{1,0:T(8,128)S(1)}, f32[280,128]{1,0:T(8,128)S(1)}, u32[]{:S(2)}, u32[]{:S(2)}) collective-permute-start(f32[280,128]{1,0:T(8,128)S(1)} %multiply_add_fusion.here_ref), channel_id=1, source_target_pairs={{0,1},{1,0},{2,3},{3,2},{4,5},{5,4},{6,7},{7,6},{8,9},{9,8},{10,11... | collective-permute-start | bytes 430088 | tf_op jit(solution)/shard_map/ppermute | solution.py:489
  48.2 2.6 %collective-permute-start.14 = (f32[280,128]{1,0:T(8,128)S(1)}, f32[280,128]{1,0:T(8,128)S(1)}, u32[]{:S(2)}, u32[]{:S(2)}) collective-permute-start(f32[280,128]{1,0:T(8,128)S(1)} %collective-permute-done.12.here_ref), channel_id=1, source_target_pairs={{0,1},{1,0},{2,3},{3,2},{4,5},{5,4},{6,7},{7,6},{8,9},{9,8},{10,11... | collective-permute-start | bytes 430088 | tf_op jit(solution)/shard_map/ppermute | solution.py:496

commit v5 on v4

--- a/solution.py
+++ b/solution.py
@@ -238,6 +238,68 @@
     )
 
 
+ROWS = 8
+SPARE = LANES - HEAD_DIM
+PIECES = HEAD_DIM // SPARE
+
+
+def packed_tiles(tiles):
+    return next(kept for kept in range(tiles + 1) if (tiles - kept) * PIECES - (-tiles // SPARE) <= kept)
+
+
+def tile_of(at):
+    return slice(at * ROWS, (at + 1) * ROWS)
+
+
+def pack_rows(read, write, tiles):
+    kept = packed_tiles(tiles)
+    moved = (tiles - kept) * PIECES
+    lane = lax.broadcasted_iota(jnp.int32, (ROWS, LANES), 1)
+    rows = [read(at) for at in range(tiles)]
+    for at in range(kept):
+        block = rows[at]
+        if at < moved:
+            extra, piece = divmod(at, PIECES)
+            shifted = pltpu.roll(rows[kept + extra], HEAD_DIM - SPARE * piece, 1)
+            block = jnp.where(lane < HEAD_DIM, block, shifted)
+        else:
+            first = (at - moved) * SPARE
+            for step in range(min(SPARE, tiles - first)):
+                norm = rows[first + step]
+                norm = pltpu.roll(norm, step, 1) if step else norm
+                block = jnp.where(lane == HEAD_DIM + step, norm, block)
+        write(at, block)
+
+
+def unpack_rows(read, write, tiles):
+    kept = packed_tiles(tiles)
+    moved = (tiles - kept) * PIECES
+    lane = lax.broadcasted_iota(jnp.int32, (ROWS, LANES), 1)
+    rows = [read(at) for at in range(kept)]
+    for at in range(tiles):
+        if at < kept:
+            block = rows[at]
+        else:
+            for piece in range(PIECES):
+                shifted = pltpu.roll(rows[(at - kept) * PIECES + piece], SPARE * (piece + 1), 1)
+                block = shifted if piece == 0 else jnp.where(lane < SPARE * piece, block, shifted)
+        group, step = divmod(at, SPARE)
+        norm = rows[moved + group]
+        norm = pltpu.roll(norm, LANES - step, 1) if step else norm
+        write(at, jnp.where(lane == HEAD_DIM, norm, block))
+
+
+def store_into(ref, *index):
+    def write(at, block):
+        ref[(*index, tile_of(at))] = block
+
+    return write
+
+
+def unpack_into(state, index, packed):
+    unpack_rows(lambda at: packed[tile_of(at)], store_into(state, index), state.shape[1] // ROWS)
+
+
 PARTS = 4
 
 
@@ -261,12 +323,14 @@
     half = halves.shape[2]
     per_group = HEADS // 2
     column = lax.axis_index("width")
-    for group in range(2):
-        for place in range(per_group):
-            head = group * per_group + place
-            feature = jnp.maximum(head_slice(key_ref, head), 0)
-            wide = jnp.concatenate([head_slice(value_ref, head), one], axis=1)
-            store_rows(halves, group, place * HEAD_DIM, dot_tokens(feature, wide), half)
+    blocks = []
+    for head in range(HEADS):
+        feature = jnp.maximum(head_slice(key_ref, head), 0)
+        wide = jnp.concatenate([head_slice(value_ref, head), one], axis=1)
+        blocks.append(dot_tokens(feature, wide))
+    for head in range(HEADS):
+        group, place = divmod(head, per_group)
+        store_rows(halves, group, place * HEAD_DIM, blocks[head], half)
     keep_ref[...] = halves[column]
     send_ref[...] = halves[1 - column]
 
@@ -284,8 +348,9 @@
 
 def pick_kernel(keep_ref, came_ref, mine_ref, other_ref):
     row = lax.axis_index("height")
-    mine_ref[...] = keep_ref[row] + came_ref[row]
-    other_ref[...] = keep_ref[1 - row] + came_ref[1 - row]
+    tiles = keep_ref.shape[1] // ROWS
+    for out, at_row in ((mine_ref, row), (other_ref, 1 - row)):
+        pack_rows(lambda at: keep_ref[at_row, tile_of(at)] + came_ref[at_row, tile_of(at)], store_into(out), tiles)
 
 
 def write_masks(clip_ref, out_ref):
@@ -322,31 +387,47 @@
 
 def query_kernel(state_ref, came_ref, mine_ref, other_ref, keep_ref, send_ref, own_out, other_out, state, halves):
     column = lax.axis_index("width")
-    half = state_ref.shape[0]
+    half = state.shape[1]
     per_group = HEADS // 2
     tokens = mine_ref.shape[2]
-    state[column] = state_ref[...]
-    state[1 - column] = came_ref[...]
+    unpack_into(state, column, state_ref)
+    unpack_into(state, 1 - column, came_ref)
     lane = lax.broadcasted_iota(jnp.int32, (2 * tokens, LANES), 1)
+    features, cots, highs, lows, products = [], [], [], [], []
     for place in range(per_group):
-        feature = jnp.concatenate([mine_ref[0, place], other_ref[0, place]], axis=0)
-        cotangent = jnp.concatenate([mine_ref[1, place], other_ref[1, place]], axis=0).astype(jnp.float32)
+        features.append(jnp.concatenate([mine_ref[0, place], other_ref[0, place]], axis=0)[:, :HEAD_DIM])
+        cots.append(jnp.concatenate([mine_ref[1, place], other_ref[1, place]], axis=0))
         high, low = split_terms(load_rows(state, place * HEAD_DIM, half))
-        narrow = feature[:, :HEAD_DIM]
-        product = dot_rows(narrow, high) + dot_rows(narrow, low)
+        highs.append(high)
+        lows.append(low)
+        pad = jnp.zeros((LANES - HEAD_DIM, LANES), jnp.bfloat16)
+        full = jnp.concatenate([mine_ref[0, place], other_ref[0, place]], axis=0)
+        both = jnp.concatenate([high, pad, low, pad], axis=0)
+        products.append(dot_rows(jnp.concatenate([full, full], axis=1), both))
+    scaleds = []
+    for place in range(per_group):
+        cotangent = cots[place].astype(jnp.float32)
+        product = products[place]
         inverse = 1.0 / (product[:, HEAD_DIM : HEAD_DIM + 1] + EPSILON)
         against = jnp.sum(cotangent * product, axis=1, keepdims=True)
         norm_grad = -(against * inverse) * inverse
-        scaled = jnp.where(lane == HEAD_DIM, norm_grad, cotangent * inverse)
-        scaled_high, scaled_low = split_terms(scaled)
-        grad = dot_tokens(narrow, scaled_high) + dot_tokens(narrow, scaled_low)
+        scaleds.append(split_terms(jnp.where(lane == HEAD_DIM, norm_grad, cotangent * inverse)))
+    for place in range(per_group):
+        narrow, (scaled_high, scaled_low) = features[place], scaleds[place]
+        both = dot_tokens(narrow, jnp.concatenate([scaled_high, scaled_low], axis=1))
+        grad = both[:, :LANES] + both[:, LANES:]
         store_rows(halves, None, place * HEAD_DIM, grad, half)
-        back = dot_columns(scaled_high, high) + dot_columns(scaled_high, low) + dot_columns(scaled_low, high)
+    for place in range(per_group):
+        narrow, high, low = features[place], highs[place], lows[place]
+        scaled_high, scaled_low = scaleds[place]
+        terms = jnp.concatenate([high, low], axis=1)
+        back = dot_columns(jnp.concatenate([scaled_high] * 2, axis=1), terms)
+        back = back + dot_columns(jnp.concatenate([scaled_low] * 2, axis=1), terms)
         back = jnp.where(narrow > 0, back, 0.0).astype(jnp.bfloat16)
         own_out[place, :, :HEAD_DIM] = back[:tokens]
         other_out[place, :, :HEAD_DIM] = back[tokens:]
-    keep_ref[...] = halves[column]
-    send_ref[...] = halves[1 - column]
+    for out, part in ((keep_ref, column), (send_ref, 1 - column)):
+        pack_rows(lambda at: halves[part, tile_of(at)], store_into(out), half // ROWS)
 
 
 def load_rows(state, first, half):
@@ -372,21 +453,22 @@
 
 def key_kernel(mine, key_ref, value_ref, here_ref, came_ref, *refs):
     column, row = lax.axis_index("width"), lax.axis_index("height")
-    half = here_ref.shape[0]
     given, (key_out, value_out, total) = refs[:-3], refs[-3:]
-    total[column] = here_ref[...]
-    total[1 - column] = came_ref[...]
+    half = total.shape[1]
+    unpack_into(total, column, here_ref)
+    unpack_into(total, 1 - column, came_ref)
     one = tail_block(key_ref.shape[0], 1.0)
     for group in range(2):
         @pl.when(row == (group if mine else 1 - group))
         def _():
-            for place in range(HEADS // 2):
-                grads = key_heads(key_ref, value_ref, total, half, group, place, one)
+            places = range(HEADS // 2)
+            grads = [key_heads(key_ref, value_ref, total, half, group, place, one) for place in places]
+            for place in places:
                 for at, out in enumerate((key_out, value_out)):
                     if mine:
-                        out[place, :, :HEAD_DIM] = grads[at]
+                        out[place, :, :HEAD_DIM] = grads[place][at]
                         continue
-                    for which, part in ((group, grads[at]), (1 - group, given[at][place, :, :HEAD_DIM])):
+                    for which, part in ((group, grads[place][at]), (1 - group, given[at][place, :, :HEAD_DIM])):
                         first = (which * (HEADS // 2) + place) * HEAD_DIM
                         out[:, first : first + HEAD_DIM] = part
 
@@ -419,7 +501,7 @@
     query, key, value, cotangent = (
         part.reshape(tokens, flat) for part in (queries, attn_keys, attn_values, attn_cotangent)
     )
-    share = struct((half, LANES))
+    share = struct((packed_tiles(half // ROWS) * ROWS, LANES))
     pair = struct((2, half, LANES))
 
     key_hbm, value_hbm = (

time: 52.5 us -> 49.1 us (0.935)
  waiting for transfers between devices: 13.5 us -> 10.4 us
  Pallas kernels: 17.2 us -> 16.3 us
    pallas_call x1, Pallas kernels: 2.97 us -> 1.58 us  [paired(): vmem_call(query_kernel, (share, share, back, back), [pltpu.VMEM((2, half,...]
    ppermute x2, waiting for transfers between devices: 4.69 us -> 3.31 us  [along_frames(): near = lax.ppermute(own, 'tm', moves[0])]
    ppermute x2, waiting for transfers between devices: 4.48 us -> 3.6 us  [along_frames(): far = lax.ppermute(own, 'tm', moves[1])]
  transfers between devices with their start and end apart: 16 -> 16, of which waited for: 10 -> 9; matrix products, arithmetic and copies ran while one was open for 3% -> 3% of each run, Pallas kernels for 26% -> 26%
where the time goes in v5:
time: 49.1 us; the launch traced here: 48.3 us
  starting transfers between devices  19.4 us (40%)
  Pallas kernels  16.3 us (33%)
  waiting for transfers between devices  10.4 us (21%)
  local copies, waits for them, and re-layouts  1.28 us (3%)
  between operations  0.8 us (2%)
    pallas_call x1, Pallas kernels, conv_part(): vmem_call(functools.partial(conv_kernel, bases, len(halo_rows)), struct((...  7.5 us
    ppermute x2, starting transfers between devices, along_frames(): far = lax.ppermute(own, 'tm', moves[1])  5.5 us
    ppermute x2, starting transfers between devices, along_frames(): near = lax.ppermute(own, 'tm', moves[0])  3.84 us
    ppermute x2, waiting for transfers between devices, along_frames(): far = lax.ppermute(own, 'tm', moves[1])  3.6 us
    ppermute x2, waiting for transfers between devices, along_frames(): near = lax.ppermute(own, 'tm', moves[0])  3.31 us
    pallas_call x1, Pallas kernels, paired(): vmem_call(state_kernel, (pair, pair), [pltpu.VMEM((2, 2, half, LANES), jn...  2.12 us
    pallas_call x1, Pallas kernels, paired(): vmem_call(heads_kernel, (packed, packed, struct((8, LANES))), [pltpu.VMEM...  1.7 us
    ppermute x1, starting transfers between devices, paired(): far_came = lax.ppermute(far, 'width', SWAP)  1.62 us
  transfers between devices with their start and end apart: 16, of which 9 were waited for; matrix products, arithmetic and copies ran while one was open for 3% of the time, Pallas kernels for 26%

profile of v5, /device:TPU:9, one launch (start us, length us, event | category | flops | bytes accessed | tf_op | source)
XLA Modules:
  0.0 48.3 jit_solution(3814473298731862724)
XLA Ops:
  0.6 2.1 %shard_map.102 = (f32[2,280,128]{2,1,0:T(8,128)S(1)}, f32[2,280,128]{2,1,0:T(8,128)S(1)}) custom-call(bf16[128,1120]{1,0:T(8,128)(2,1)} %bitcast.22, bf16[128,1120]{1,0:T(8,128)(2,1)} %bitcast.25), custom_call_target="tpu_custom_call" | custom-call | flops 36700160 | bytes 1146880 | tf_op jit(solution)/shard_map/pallas_call | solution.py:511
  2.8 0.7 %collective-permute-start = (f32[2,280,128]{2,1,0:T(8,128)S(1)}, f32[2,280,128]{2,1,0:T(8,128)S(1)}, u32[]{:S(2)}, u32[]{:S(2)}) collective-permute-start(f32[2,280,128]{2,1,0:T(8,128)S(1)} %get-tuple-element.44), channel_id=1, source_target_pairs={{0,1},{1,0},{2,3},{3,2},{4,5},{5,4},{6,7},{7,6},{8,9},{9,8},{10,11... | collective-permute-start | bytes 860168 | tf_op jit(solution)/shard_map/ppermute | solution.py:517
  3.5 1.0 %dynamic-slice_bitcast_fusion = bf16[2,16,5632]{2,1,0:T(8,128)(2,1)S(1)} fusion(bf16[1,8,16,5632]{3,2,1,0:T(8,128)(2,1)} %param.12, s32[]{:T(128)S(6)} %select_n.11), kind=kLoop, calls=%fused_computation | loop fusion | bytes 720900 | tf_op jit(solution)/shard_map/dynamic_slice | solution.py:762
  4.7 0.2 shard_map.103
  4.9 1.3 %collective-permute-start.1 = (f32[248,128]{1,0:T(8,128)S(1)}, f32[248,128]{1,0:T(8,128)S(1)}, u32[]{:S(2)}, u32[]{:S(2)}) collective-permute-start(f32[248,128]{1,0:T(8,128)S(1)} %get-tuple-element.51), channel_id=1, source_target_pairs={{0,2},{2,0},{1,3},{3,1},{4,6},{6,4},{5,7},{7,5},{8,10},{10,8},{9,1... | collective-permute-start | bytes 380936 | tf_op jit(solution)/shard_map/ppermute | solution.py:520
  6.2 1.7 %shard_map.104 = (bf16[2,5,128,128]{3,2,1,0:T(8,128)(2,1)S(1)}, bf16[2,5,128,128]{3,2,1,0:T(8,128)(2,1)S(1)}, f32[8,128]{1,0:T(8,128)S(1)}) custom-call(bf16[128,1120]{1,0:T(8,128)(2,1)} %bitcast.30, bf16[128,1120]{1,0:T(8,128)(2,1)} %bitcast.31, s32[4]{0:T(128)} %clip_hbm.1), custom_call_target="tpu_custom_call" | custom-call | bytes 1720320 | tf_op jit(solution)/shard_map/pallas_call | solution.py:524
  7.9 0.3 collective-permute-start.4
  8.2 1.2 %collective-permute-start.7 = (bf16[2,16,5632]{2,1,0:T(8,128)(2,1)S(1)}, bf16[2,16,5632]{2,1,0:T(8,128)(2,1)S(1)}, u32[]{:S(2)}, u32[]{:S(2)}) collective-permute-start(bf16[2,16,5632]{2,1,0:T(8,128)(2,1)S(1)} %dynamic-slice_bitcast_fusion), channel_id=1, source_target_pairs={{0,2},{2,0},{1,3},{3,1},{4,6},{6,4},{5,7},{7,5},{8,10},{10,8},{9,1... | collective-permute-start | bytes 1081352 | tf_op jit(solution)/shard_map/ppermute | solution.py:782
  9.4 0.2 dynamic-slice_bitcast_fusion.1
  9.7 4.2 %collective-permute-start.3 = (f32[248,128]{1,0:T(8,128)S(1)}, f32[248,128]{1,0:T(8,128)S(1)}, u32[]{:S(2)}, u32[]{:S(2)}) collective-permute-start(f32[248,128]{1,0:T(8,128)S(1)} %add.21), channel_id=1, source_target_pairs={{0,8},{4,12},{1,9},{5,13},{2,10},{6,14},{3,11},{7,15},{16,24},{20,... | collective-permute-start | bytes 380936 | tf_op jit(solution)/shard_map/ppermute | solution.py:540
  13.9 1.9 %collective-permute-start.2 = (f32[248,128]{1,0:T(8,128)S(1)}, f32[248,128]{1,0:T(8,128)S(1)}, u32[]{:S(2)}, u32[]{:S(2)}) collective-permute-start(f32[248,128]{1,0:T(8,128)S(1)} %add.21), channel_id=1, source_target_pairs={{0,4},{4,8},{8,12},{1,5},{5,9},{9,13},{2,6},{6,10},{10,14},{3,7},{... | collective-permute-start | bytes 380936 | tf_op jit(solution)/shard_map/ppermute | solution.py:539
  15.8 3.6 %collective-permute-done.3 = f32[248,128]{1,0:T(8,128)S(1)} collective-permute-done((f32[248,128]{1,0:T(8,128)S(1)}, f32[248,128]{1,0:T(8,128)S(1)}, u32[]{:S(2)}, u32[]{:S(2)}) %collective-permute-start.3) | collective-permute-done | bytes 127008 | tf_op jit(solution)/shard_map/ppermute | solution.py:540
  19.4 2.7 %collective-permute-done.2 = f32[248,128]{1,0:T(8,128)S(1)} collective-permute-done((f32[248,128]{1,0:T(8,128)S(1)}, f32[248,128]{1,0:T(8,128)S(1)}, u32[]{:S(2)}, u32[]{:S(2)}) %collective-permute-start.2) | collective-permute-done | bytes 127008 | tf_op jit(solution)/shard_map/ppermute | solution.py:539
  22.2 0.8 %collective-permute-start.5 = (f32[248,128]{1,0:T(8,128)S(1)}, f32[248,128]{1,0:T(8,128)S(1)}, u32[]{:S(2)}, u32[]{:S(2)}) collective-permute-start(f32[248,128]{1,0:T(8,128)S(1)} %multiply_add_fusion.1.state_ref), channel_id=1, source_target_pairs={{0,1},{1,0},{2,3},{3,2},{4,5},{5,4},{6,7},{7,6},{8,9},{9,8},{10,11... | collective-permute-start | bytes 380936 | tf_op jit(solution)/shard_map/ppermute | solution.py:549
  23.0 0.9 %collective-permute-done.5.came_ref = f32[248,128]{1,0:T(8,128)S(1)} collective-permute-done((f32[248,128]{1,0:T(8,128)S(1)}, f32[248,128]{1,0:T(8,128)S(1)}, u32[]{:S(2)}, u32[]{:S(2)}) %collective-permute-start.5) | collective-permute-done | bytes 127008 | tf_op jit(solution)/shard_map/ppermute | solution.py:549
  24.0 1.6 %shard_map.105 = (f32[248,128]{1,0:T(8,128)S(1)}, f32[248,128]{1,0:T(8,128)S(1)}, bf16[5,128,128]{2,1,0:T(8,128)(2,1)S(1)}, bf16[5,128,128]{2,1,0:T(8,128)(2,1)S(1)}) custom-call(f32[248,128]{1,0:T(8,128)S(1)} %multiply_add_fusion.1.state_ref, f32[248,128]{1,0:T(8,128)S(1)} %collective-permute-done.5.came_ref, ...), custom_call_target="tpu_custom_call" | custom-call | flops 256901120 | bytes 1146880 | tf_op jit(solution)/shard_map/pallas_call | solution.py:551
  25.5 0.4 collective-permute-start.6
  26.0 0.2 collective-permute-start.9
  26.2 0.7 %collective-permute-done.6 = f32[248,128]{1,0:T(8,128)S(1)} collective-permute-done((f32[248,128]{1,0:T(8,128)S(1)}, f32[248,128]{1,0:T(8,128)S(1)}, u32[]{:S(2)}, u32[]{:S(2)}) %collective-permute-start.6) | collective-permute-done | bytes 127008 | tf_op jit(solution)/shard_map/ppermute | solution.py:556
  27.0 0.3 collective-permute-done.9.refs_2_
  27.3 1.3 %collective-permute-start.11 = (f32[248,128]{1,0:T(8,128)S(1)}, f32[248,128]{1,0:T(8,128)S(1)}, u32[]{:S(2)}, u32[]{:S(2)}) collective-permute-start(f32[248,128]{1,0:T(8,128)S(1)} %add.24), channel_id=1, source_target_pairs={{8,0},{12,4},{9,1},{13,5},{10,2},{14,6},{11,3},{15,7},{24,16},{28,... | collective-permute-start | bytes 380936 | tf_op jit(solution)/shard_map/ppermute | solution.py:540
  28.6 1.9 %collective-permute-start.10 = (f32[248,128]{1,0:T(8,128)S(1)}, f32[248,128]{1,0:T(8,128)S(1)}, u32[]{:S(2)}, u32[]{:S(2)}) collective-permute-start(f32[248,128]{1,0:T(8,128)S(1)} %add.24), channel_id=1, source_target_pairs={{4,0},{8,4},{12,8},{5,1},{9,5},{13,9},{6,2},{10,6},{14,10},{7,3},{... | collective-permute-start | bytes 380936 | tf_op jit(solution)/shard_map/ppermute | solution.py:539
  30.5 1.2 %collective-permute-start.13 = (bf16[5,128,128]{2,1,0:T(8,128)(2,1)S(1)}, bf16[5,128,128]{2,1,0:T(8,128)(2,1)S(1)}, u32[]{:S(2)}, u32[]{:S(2)}) collective-permute-start(bf16[5,128,128]{2,1,0:T(8,128)(2,1)S(1)} %get-tuple-element.70), channel_id=1, source_target_pairs={{0,2},{2,0},{1,3},{3,1},{4,6},{6,4},{5,7},{7,5},{8,10},{10,8},{9,1... | collective-permute-start | bytes 491528 | tf_op jit(solution)/shard_map/ppermute | solution.py:561
  31.7 7.5 %shard_map.106 = bf16[8,16,5632]{2,1,0:T(8,128)(2,1)} custom-call(bf16[2,16,5632]{2,1,0:T(8,128)(2,1)S(1)} %collective-permute-done.7.refs_0_, bf16[8,2,5632]{2,1,0:T(2,128)(2,1)S(1)} %collective-permute-done.8.refs_1_, bf16[2,2,5632]{2,1,0:T(2,128)(2,1)S(1)} %collective-permute-done.9.refs_2_, bf16[8,16,5632]{2,1,0:T(8,128)(2,1)S(1)} %bitcast.21, ...), custom_call_target="tpu_custom_call" | custom-call | flops 2162688 | bytes 720896 | tf_op jit(solution)/shard_map/pallas_call | solution.py:797
  39.3 0.6 %collective-permute-done.10 = f32[248,128]{1,0:T(8,128)S(1)} collective-permute-done((f32[248,128]{1,0:T(8,128)S(1)}, f32[248,128]{1,0:T(8,128)S(1)}, u32[]{:S(2)}, u32[]{:S(2)}) %collective-permute-start.10) | collective-permute-done | bytes 127008 | tf_op jit(solution)/shard_map/ppermute | solution.py:539
  39.9 1.2 %collective-permute-start.12 = (f32[248,128]{1,0:T(8,128)S(1)}, f32[248,128]{1,0:T(8,128)S(1)}, u32[]{:S(2)}, u32[]{:S(2)}) collective-permute-start(f32[248,128]{1,0:T(8,128)S(1)} %multiply_add_fusion.here_ref), channel_id=1, source_target_pairs={{0,2},{2,0},{1,3},{3,1},{4,6},{6,4},{5,7},{7,5},{8,10},{10,8},{9,1... | collective-permute-start | bytes 380936 | tf_op jit(solution)/shard_map/ppermute | solution.py:570
  41.1 1.0 %collective-permute-start.15 = (f32[248,128]{1,0:T(8,128)S(1)}, f32[248,128]{1,0:T(8,128)S(1)}, u32[]{:S(2)}, u32[]{:S(2)}) collective-permute-start(f32[248,128]{1,0:T(8,128)S(1)} %multiply_add_fusion.here_ref), channel_id=1, source_target_pairs={{0,1},{1,0},{2,3},{3,2},{4,5},{5,4},{6,7},{7,6},{8,9},{9,8},{10,11... | collective-permute-start | bytes 380936 | tf_op jit(solution)/shard_map/ppermute | solution.py:571
  42.1 0.9 %shard_map.107 = bf16[128,1120]{1,0:T(8,128)(2,1)} custom-call(bf16[5,128,128]{2,1,0:T(8,128)(2,1)S(1)} %get-tuple-element.68.mine_ref, bf16[5,128,128]{2,1,0:T(8,128)(2,1)S(1)} %collective-permute-done.13.came_ref), custom_call_target="tpu_custom_call" | custom-call | bytes 573440 | tf_op jit(solution)/shard_map/pallas_call | solution.py:563
  43.0 1.1 %collective-permute-done.12.here_ref = f32[248,128]{1,0:T(8,128)S(1)} collective-permute-done((f32[248,128]{1,0:T(8,128)S(1)}, f32[248,128]{1,0:T(8,128)S(1)}, u32[]{:S(2)}, u32[]{:S(2)}) %collective-permute-start.12) | collective-permute-done | bytes 127008 | tf_op jit(solution)/shard_map/ppermute | solution.py:570
  44.1 1.6 %collective-permute-start.14 = (f32[248,128]{1,0:T(8,128)S(1)}, f32[248,128]{1,0:T(8,128)S(1)}, u32[]{:S(2)}, u32[]{:S(2)}) collective-permute-start(f32[248,128]{1,0:T(8,128)S(1)} %collective-permute-done.12.here_ref), channel_id=1, source_target_pairs={{0,1},{1,0},{2,3},{3,2},{4,5},{5,4},{6,7},{7,6},{8,9},{9,8},{10,11... | collective-permute-start | bytes 380936 | tf_op jit(solution)/shard_map/ppermute | solution.py:578
  45.8 0.8 %shard_map.108 = (bf16[5,128,128]{2,1,0:T(8,128)(2,1)S(1)}, bf16[5,128,128]{2,1,0:T(8,128)(2,1)S(1)}) custom-call(bf16[128,1120]{1,0:T(8,128)(2,1)S(1)} %bitcast.23, bf16[128,1120]{1,0:T(8,128)(2,1)S(1)} %bitcast.26, f32[248,128]{1,0:T(8,128)S(1)} %multiply_add_fusion.here_ref, f32[248,128]{1,0:T(8,128)S(1)} %collective-permute-done.15.came_ref), custom_call_target="tpu_custom_call" | custom-call | flops 73400320 | bytes 573440 | tf_op jit(solution)/shard_map/pallas_call | solution.py:574
  46.7 1.6 %shard_map.109 = (bf16[128,1120]{1,0:T(8,128)(2,1)}, bf16[128,1120]{1,0:T(8,128)(2,1)}) custom-call(bf16[128,1120]{1,0:T(8,128)(2,1)S(1)} %bitcast.24, bf16[128,1120]{1,0:T(8,128)(2,1)S(1)} %bitcast.27, f32[248,128]{1,0:T(8,128)S(1)} %collective-permute-done.12.here_ref, f32[248,128]{1,0:T(8,128)S(1)} %collective-permute-done.14.came_ref, ...), custom_call_target="tpu_custom_call" | custom-call | flops 73400320 | bytes 573440 | tf_op jit(solution)/shard_map/pallas_call | solution.py:580
  (24 shorter events, 0.6 us)
Async XLA Ops:
  0.6 8.8 %copy-start = (bf16[1,8,16,5632]{3,2,1,0:T(8,128)(2,1)S(1)}, bf16[1,8,16,5632]{3,2,1,0:T(8,128)(2,1)}, u32[]{:S(2)}) copy-start(bf16[1,8,16,5632]{3,2,1,0:T(8,128)(2,1)} %param.12) | copy-start | bytes 4325380
  2.8 1.9 %collective-permute-start = (f32[2,280,128]{2,1,0:T(8,128)S(1)}, f32[2,280,128]{2,1,0:T(8,128)S(1)}, u32[]{:S(2)}, u32[]{:S(2)}) collective-permute-start(f32[2,280,128]{2,1,0:T(8,128)S(1)} %get-tuple-element.44), channel_id=1, source_target_pairs={{0,1},{1,0},{2,3},{3,2},{4,5},{5,4},{6,7},{7,6},{8,9},{9,8},{10,11... | collective-permute-start | bytes 860168 | tf_op jit(solution)/shard_map/ppermute | solution.py:517
  4.9 4.7 %collective-permute-start.1 = (f32[248,128]{1,0:T(8,128)S(1)}, f32[248,128]{1,0:T(8,128)S(1)}, u32[]{:S(2)}, u32[]{:S(2)}) collective-permute-start(f32[248,128]{1,0:T(8,128)S(1)} %get-tuple-element.51), channel_id=1, source_target_pairs={{0,2},{2,0},{1,3},{3,1},{4,6},{6,4},{5,7},{7,5},{8,10},{10,8},{9,1... | collective-permute-start | bytes 380936 | tf_op jit(solution)/shard_map/ppermute | solution.py:520
  7.9 23.8 %copy-start.3 = (f32[9,5632]{1,0:T(8,128)S(1)}, f32[9,5632]{1,0:T(8,128)}, u32[]{:S(2)}) copy-start(f32[9,5632]{1,0:T(8,128)} %refs_4_.1) | copy-start | bytes 608260
  7.9 14.3 %collective-permute-start.4 = (bf16[2,5,128,128]{3,2,1,0:T(8,128)(2,1)S(1)}, bf16[2,5,128,128]{3,2,1,0:T(8,128)(2,1)S(1)}, u32[]{:S(2)}, u32[]{:S(2)}) collective-permute-start(bf16[2,5,128,128]{3,2,1,0:T(8,128)(2,1)S(1)} %get-tuple-element.49), channel_id=1, source_target_pairs={{0,2},{2,0},{1,3},{3,1},{4,6},{6,4},{5,7},{7,5},{8,10},{10,8},{9,1... | collective-permute-start | bytes 983048 | tf_op jit(solution)/shard_map/ppermute | solution.py:535
  8.2 17.7 %collective-permute-start.7 = (bf16[2,16,5632]{2,1,0:T(8,128)(2,1)S(1)}, bf16[2,16,5632]{2,1,0:T(8,128)(2,1)S(1)}, u32[]{:S(2)}, u32[]{:S(2)}) collective-permute-start(bf16[2,16,5632]{2,1,0:T(8,128)(2,1)S(1)} %dynamic-slice_bitcast_fusion), channel_id=1, source_target_pairs={{0,2},{2,0},{1,3},{3,1},{4,6},{6,4},{5,7},{7,5},{8,10},{10,8},{9,1... | collective-permute-start | bytes 1081352 | tf_op jit(solution)/shard_map/ppermute | solution.py:782
  9.7 9.8 %collective-permute-start.3 = (f32[248,128]{1,0:T(8,128)S(1)}, f32[248,128]{1,0:T(8,128)S(1)}, u32[]{:S(2)}, u32[]{:S(2)}) collective-permute-start(f32[248,128]{1,0:T(8,128)S(1)} %add.21), channel_id=1, source_target_pairs={{0,8},{4,12},{1,9},{5,13},{2,10},{6,14},{3,11},{7,15},{16,24},{20,... | collective-permute-start | bytes 380936 | tf_op jit(solution)/shard_map/ppermute | solution.py:540
  13.9 8.3 %collective-permute-start.2 = (f32[248,128]{1,0:T(8,128)S(1)}, f32[248,128]{1,0:T(8,128)S(1)}, u32[]{:S(2)}, u32[]{:S(2)}) collective-permute-start(f32[248,128]{1,0:T(8,128)S(1)} %add.21), channel_id=1, source_target_pairs={{0,4},{4,8},{8,12},{1,5},{5,9},{9,13},{2,6},{6,10},{10,14},{3,7},{... | collective-permute-start | bytes 380936 | tf_op jit(solution)/shard_map/ppermute | solution.py:539
  22.2 1.8 %collective-permute-start.5 = (f32[248,128]{1,0:T(8,128)S(1)}, f32[248,128]{1,0:T(8,128)S(1)}, u32[]{:S(2)}, u32[]{:S(2)}) collective-permute-start(f32[248,128]{1,0:T(8,128)S(1)} %multiply_add_fusion.1.state_ref), channel_id=1, source_target_pairs={{0,1},{1,0},{2,3},{3,2},{4,5},{5,4},{6,7},{7,6},{8,9},{9,8},{10,11... | collective-permute-start | bytes 380936 | tf_op jit(solution)/shard_map/ppermute | solution.py:549
  23.0 4.0 %collective-permute-start.8 = (bf16[8,2,5632]{2,1,0:T(2,128)(2,1)S(1)}, bf16[8,2,5632]{2,1,0:T(2,128)(2,1)S(1)}, u32[]{:S(2)}, u32[]{:S(2)}) collective-permute-start(bf16[8,2,5632]{2,1,0:T(2,128)(2,1)S(1)} %dynamic-slice_bitcast_fusion.1), channel_id=1, source_target_pairs={{0,1},{1,0},{2,3},{3,2},{4,5},{5,4},{6,7},{7,6},{8,9},{9,8},{10,11... | collective-permute-start | bytes 540680 | tf_op jit(solution)/shard_map/ppermute | solution.py:783
  25.5 1.4 %collective-permute-start.6 = (f32[248,128]{1,0:T(8,128)S(1)}, f32[248,128]{1,0:T(8,128)S(1)}, u32[]{:S(2)}, u32[]{:S(2)}) collective-permute-start(f32[248,128]{1,0:T(8,128)S(1)} %get-tuple-element.59), channel_id=1, source_target_pairs={{0,1},{1,0},{2,3},{3,2},{4,5},{5,4},{6,7},{7,6},{8,9},{9,8},{10,11... | collective-permute-start | bytes 380936 | tf_op jit(solution)/shard_map/ppermute | solution.py:556
  26.0 1.3 %collective-permute-start.9 = (bf16[2,2,5632]{2,1,0:T(2,128)(2,1)S(1)}, bf16[2,2,5632]{2,1,0:T(2,128)(2,1)S(1)}, u32[]{:S(2)}, u32[]{:S(2)}) collective-permute-start(bf16[2,2,5632]{2,1,0:T(2,128)(2,1)S(1)} %constant_dynamic-slice_fusion), channel_id=1, source_target_pairs={{0,1},{1,0},{2,3},{3,2},{4,5},{5,4},{6,7},{7,6},{8,9},{9,8},{10,11... | collective-permute-start | bytes 135176 | tf_op jit(solution)/shard_map/ppermute | solution.py:784
  27.3 11.9 %collective-permute-start.11 = (f32[248,128]{1,0:T(8,128)S(1)}, f32[248,128]{1,0:T(8,128)S(1)}, u32[]{:S(2)}, u32[]{:S(2)}) collective-permute-start(f32[248,128]{1,0:T(8,128)S(1)} %add.24), channel_id=1, source_target_pairs={{8,0},{12,4},{9,1},{13,5},{10,2},{14,6},{11,3},{15,7},{24,16},{28,... | collective-permute-start | bytes 380936 | tf_op jit(solution)/shard_map/ppermute | solution.py:540
  28.6 11.2 %collective-permute-start.10 = (f32[248,128]{1,0:T(8,128)S(1)}, f32[248,128]{1,0:T(8,128)S(1)}, u32[]{:S(2)}, u32[]{:S(2)}) collective-permute-start(f32[248,128]{1,0:T(8,128)S(1)} %add.24), channel_id=1, source_target_pairs={{4,0},{8,4},{12,8},{5,1},{9,5},{13,9},{6,2},{10,6},{14,10},{7,3},{... | collective-permute-start | bytes 380936 | tf_op jit(solution)/shard_map/ppermute | solution.py:539
  30.5 11.5 %collective-permute-start.13 = (bf16[5,128,128]{2,1,0:T(8,128)(2,1)S(1)}, bf16[5,128,128]{2,1,0:T(8,128)(2,1)S(1)}, u32[]{:S(2)}, u32[]{:S(2)}) collective-permute-start(bf16[5,128,128]{2,1,0:T(8,128)(2,1)S(1)} %get-tuple-element.70), channel_id=1, source_target_pairs={{0,2},{2,0},{1,3},{3,1},{4,6},{6,4},{5,7},{7,5},{8,10},{10,8},{9,1... | collective-permute-start | bytes 491528 | tf_op jit(solution)/shard_map/ppermute | solution.py:561
  31.7 14.0 %copy-start.1 = (bf16[1,8,16,1120]{3,2,1,0:T(8,128)(2,1)S(1)}, bf16[1,8,16,1120]{3,2,1,0:T(8,128)(2,1)}, u32[]{:S(2)}) copy-start(bf16[1,8,16,1120]{3,2,1,0:T(8,128)(2,1)} %param.8) | copy-start | bytes 860164
  31.7 14.0 %copy-start.2 = (bf16[1,8,16,1120]{3,2,1,0:T(8,128)(2,1)S(1)}, bf16[1,8,16,1120]{3,2,1,0:T(8,128)(2,1)}, u32[]{:S(2)}) copy-start(bf16[1,8,16,1120]{3,2,1,0:T(8,128)(2,1)} %param.9) | copy-start | bytes 860164
  39.9 4.3 %collective-permute-start.12 = (f32[248,128]{1,0:T(8,128)S(1)}, f32[248,128]{1,0:T(8,128)S(1)}, u32[]{:S(2)}, u32[]{:S(2)}) collective-permute-start(f32[248,128]{1,0:T(8,128)S(1)} %multiply_add_fusion.here_ref), channel_id=1, source_target_pairs={{0,2},{2,0},{1,3},{3,1},{4,6},{6,4},{5,7},{7,5},{8,10},{10,8},{9,1... | collective-permute-start | bytes 380936 | tf_op jit(solution)/shard_map/ppermute | solution.py:570
  41.1 4.7 %collective-permute-start.15 = (f32[248,128]{1,0:T(8,128)S(1)}, f32[248,128]{1,0:T(8,128)S(1)}, u32[]{:S(2)}, u32[]{:S(2)}) collective-permute-start(f32[248,128]{1,0:T(8,128)S(1)} %multiply_add_fusion.here_ref), channel_id=1, source_target_pairs={{0,1},{1,0},{2,3},{3,2},{4,5},{5,4},{6,7},{7,6},{8,9},{9,8},{10,11... | collective-permute-start | bytes 380936 | tf_op jit(solution)/shard_map/ppermute | solution.py:571
  44.1 2.6 %collective-permute-start.14 = (f32[248,128]{1,0:T(8,128)S(1)}, f32[248,128]{1,0:T(8,128)S(1)}, u32[]{:S(2)}, u32[]{:S(2)}) collective-permute-start(f32[248,128]{1,0:T(8,128)S(1)} %collective-permute-done.12.here_ref), channel_id=1, source_target_pairs={{0,1},{1,0},{2,3},{3,2},{4,5},{5,4},{6,7},{7,6},{8,9},{9,8},{10,11... | collective-permute-start | bytes 380936 | tf_op jit(solution)/shard_map/ppermute | solution.py:578

commit v6 on v5

--- a/solution.py
+++ b/solution.py
@@ -193,10 +193,16 @@
 LANES = 128
 
 
-def split_terms(value):
-    high = value.astype(jnp.bfloat16)
-    low = (value - high.astype(jnp.float32)).astype(jnp.bfloat16)
-    return high, low
+def split_terms(value, count=2):
+    terms = []
+    for _ in range(count):
+        terms.append(value.astype(jnp.bfloat16))
+        value = value - terms[-1].astype(jnp.float32)
+    return terms
+
+
+def beside(*parts):
+    return jnp.concatenate(parts, axis=1)
 
 
 def dot_tokens(left, right):
@@ -393,36 +399,34 @@
     unpack_into(state, column, state_ref)
     unpack_into(state, 1 - column, came_ref)
     lane = lax.broadcasted_iota(jnp.int32, (2 * tokens, LANES), 1)
-    features, cots, highs, lows, products = [], [], [], [], []
-    for place in range(per_group):
-        features.append(jnp.concatenate([mine_ref[0, place], other_ref[0, place]], axis=0)[:, :HEAD_DIM])
+    places = range(per_group)
+    features, cots, states, products = [], [], [], []
+    pad = jnp.zeros((LANES - HEAD_DIM, LANES), jnp.bfloat16)
+    for place in places:
+        full = jnp.concatenate([mine_ref[0, place], other_ref[0, place]], axis=0)
+        features.append(full[:, :HEAD_DIM])
         cots.append(jnp.concatenate([mine_ref[1, place], other_ref[1, place]], axis=0))
-        high, low = split_terms(load_rows(state, place * HEAD_DIM, half))
-        highs.append(high)
-        lows.append(low)
-        pad = jnp.zeros((LANES - HEAD_DIM, LANES), jnp.bfloat16)
-        full = jnp.concatenate([mine_ref[0, place], other_ref[0, place]], axis=0)
-        both = jnp.concatenate([high, pad, low, pad], axis=0)
-        products.append(dot_rows(jnp.concatenate([full, full], axis=1), both))
+        high, low, rest = split_terms(load_rows(state, place * HEAD_DIM, half), 3)
+        states.append((high, low, rest))
+        product = dot_rows(beside(full, full), jnp.concatenate([high, pad, low, pad], axis=0))
+        products.append(product + dot_rows(features[-1], rest))
     scaleds = []
-    for place in range(per_group):
+    for place in places:
         cotangent = cots[place].astype(jnp.float32)
         product = products[place]
         inverse = 1.0 / (product[:, HEAD_DIM : HEAD_DIM + 1] + EPSILON)
         against = jnp.sum(cotangent * product, axis=1, keepdims=True)
         norm_grad = -(against * inverse) * inverse
-        scaleds.append(split_terms(jnp.where(lane == HEAD_DIM, norm_grad, cotangent * inverse)))
-    for place in range(per_group):
-        narrow, (scaled_high, scaled_low) = features[place], scaleds[place]
-        both = dot_tokens(narrow, jnp.concatenate([scaled_high, scaled_low], axis=1))
-        grad = both[:, :LANES] + both[:, LANES:]
-        store_rows(halves, None, place * HEAD_DIM, grad, half)
-    for place in range(per_group):
-        narrow, high, low = features[place], highs[place], lows[place]
-        scaled_high, scaled_low = scaleds[place]
-        terms = jnp.concatenate([high, low], axis=1)
-        back = dot_columns(jnp.concatenate([scaled_high] * 2, axis=1), terms)
-        back = back + dot_columns(jnp.concatenate([scaled_low] * 2, axis=1), terms)
+        scaleds.append(split_terms(jnp.where(lane == HEAD_DIM, norm_grad, cotangent * inverse), 3))
+    for place in places:
+        both = dot_tokens(features[place], beside(*scaleds[place][:2]))
+        store_rows(halves, None, place * HEAD_DIM, both[:, :LANES] + both[:, LANES:], half)
+    for place in places:
+        narrow, (high, low, rest) = features[place], states[place]
+        first, second, third = scaleds[place]
+        back = dot_columns(beside(first, third), beside(rest, high))
+        back = back + dot_columns(beside(second, second), beside(high, low))
+        back = back + dot_columns(beside(first, first), beside(high, low))
         back = jnp.where(narrow > 0, back, 0.0).astype(jnp.bfloat16)
         own_out[place, :, :HEAD_DIM] = back[:tokens]
         other_out[place, :, :HEAD_DIM] = back[tokens:]
@@ -446,7 +450,7 @@
     feature = jnp.maximum(head_slice(key_ref, head), 0)
     wide = jnp.concatenate([head_slice(value_ref, head), one], axis=1)
     high, low = split_terms(load_rows(total, place * HEAD_DIM, half))
-    grad = dot_columns(wide, high) + dot_columns(wide, low)
+    grad = dot_columns(beside(wide, wide), beside(high, low))
     product = dot_rows(feature, high) + dot_rows(feature, low)
     return jnp.where(feature > 0, grad, 0.0).astype(jnp.bfloat16), product[:, :HEAD_DIM].astype(jnp.bfloat16)
 
@@ -534,13 +538,13 @@
     _, own = lax.optimization_barrier(((heads_other, side), mine + came))
     heads_sent = lax.ppermute(heads_other, "height", SWAP)
 
-    def along_frames(own, step, beside):
+    def along_frames(own, step, meanwhile):
         moves = [[(at, at + step * hop) for at in range(frames) if 0 <= at + step * hop < frames] for hop in (1, 2)]
         near = lax.ppermute(own, "tm", moves[0])
         far = lax.ppermute(own, "tm", moves[1])
-        near, far, beside = beside(own, near, far)
+        near, far, others = meanwhile(own, near, far)
         at = 0 if step > 0 else 2
-        return own + masks[at : at + 1] * near + masks[at + 1 : at + 2] * far, beside
+        return own + masks[at : at + 1] * near + masks[at + 1 : at + 2] * far, others
 
     def fetch(own, near, far):
         return lax.optimization_barrier((near, far, heads_sent))
@@ -603,7 +607,7 @@
 
 TILES = 8
 REACH = 2
-UNROLL = 2
+UNROLL = 8
 
 
 def conv_kernel(bases, row_refs, *refs):

time: 49.1 us -> 48.9 us (level)
  transfers between devices with their start and end apart: 16 -> 16, of which waited for: 9 -> 9; matrix products, arithmetic and copies ran while one was open for 3% -> 3% of each run, Pallas kernels for 26% -> 25%
where the time goes in v6:
time: 48.9 us; the launch traced here: 48.4 us
  starting transfers between devices  19.4 us (40%)
  Pallas kernels  16 us (33%)
  waiting for transfers between devices  10.8 us (22%)
  local copies, waits for them, and re-layouts  1.28 us (3%)
  between operations  0.8 us (2%)
    pallas_call x1, Pallas kernels, conv_part(): vmem_call(functools.partial(conv_kernel, bases, len(halo_rows)), struct((...  7.19 us
    ppermute x2, starting transfers between devices, along_frames(): far = lax.ppermute(own, 'tm', moves[1])  5.5 us
    ppermute x2, starting transfers between devices, along_frames(): near = lax.ppermute(own, 'tm', moves[0])  3.84 us
    ppermute x2, waiting for transfers between devices, along_frames(): near = lax.ppermute(own, 'tm', moves[0])  3.61 us
    ppermute x2, waiting for transfers between devices, along_frames(): far = lax.ppermute(own, 'tm', moves[1])  3.6 us
    pallas_call x1, Pallas kernels, paired(): vmem_call(state_kernel, (pair, pair), [pltpu.VMEM((2, 2, half, LANES), jn...  2.12 us
    pallas_call x1, Pallas kernels, paired(): vmem_call(query_kernel, (share, share, back, back), [pltpu.VMEM((2, half,...  1.74 us
    pallas_call x1, Pallas kernels, paired(): vmem_call(heads_kernel, (packed, packed, struct((8, LANES))), [pltpu.VMEM...  1.7 us
  transfers between devices with their start and end apart: 16, of which 9 were waited for; matrix products, arithmetic and copies ran while one was open for 3% of the time, Pallas kernels for 25%

profile of v6, /device:TPU:9, one launch (start us, length us, event | category | flops | bytes accessed | tf_op | source)
XLA Modules:
  0.0 48.4 jit_solution(12278631184957510269)
XLA Ops:
  0.6 2.1 %shard_map.102 = (f32[2,280,128]{2,1,0:T(8,128)S(1)}, f32[2,280,128]{2,1,0:T(8,128)S(1)}) custom-call(bf16[128,1120]{1,0:T(8,128)(2,1)} %bitcast.22, bf16[128,1120]{1,0:T(8,128)(2,1)} %bitcast.25), custom_call_target="tpu_custom_call" | custom-call | flops 36700160 | bytes 1146880 | tf_op jit(solution)/shard_map/pallas_call | solution.py:515
  2.8 0.7 %collective-permute-start = (f32[2,280,128]{2,1,0:T(8,128)S(1)}, f32[2,280,128]{2,1,0:T(8,128)S(1)}, u32[]{:S(2)}, u32[]{:S(2)}) collective-permute-start(f32[2,280,128]{2,1,0:T(8,128)S(1)} %get-tuple-element.44), channel_id=1, source_target_pairs={{0,1},{1,0},{2,3},{3,2},{4,5},{5,4},{6,7},{7,6},{8,9},{9,8},{10,11... | collective-permute-start | bytes 860168 | tf_op jit(solution)/shard_map/ppermute | solution.py:521
  3.5 1.0 %dynamic-slice_bitcast_fusion = bf16[2,16,5632]{2,1,0:T(8,128)(2,1)S(1)} fusion(bf16[1,8,16,5632]{3,2,1,0:T(8,128)(2,1)} %param.12, s32[]{:T(128)S(6)} %select_n.11), kind=kLoop, calls=%fused_computation | loop fusion | bytes 720900 | tf_op jit(solution)/shard_map/dynamic_slice | solution.py:766
  4.7 0.2 shard_map.103
  4.9 1.3 %collective-permute-start.1 = (f32[248,128]{1,0:T(8,128)S(1)}, f32[248,128]{1,0:T(8,128)S(1)}, u32[]{:S(2)}, u32[]{:S(2)}) collective-permute-start(f32[248,128]{1,0:T(8,128)S(1)} %get-tuple-element.51), channel_id=1, source_target_pairs={{0,2},{2,0},{1,3},{3,1},{4,6},{6,4},{5,7},{7,5},{8,10},{10,8},{9,1... | collective-permute-start | bytes 380936 | tf_op jit(solution)/shard_map/ppermute | solution.py:524
  6.2 1.7 %shard_map.104 = (bf16[2,5,128,128]{3,2,1,0:T(8,128)(2,1)S(1)}, bf16[2,5,128,128]{3,2,1,0:T(8,128)(2,1)S(1)}, f32[8,128]{1,0:T(8,128)S(1)}) custom-call(bf16[128,1120]{1,0:T(8,128)(2,1)} %bitcast.30, bf16[128,1120]{1,0:T(8,128)(2,1)} %bitcast.31, s32[4]{0:T(128)} %clip_hbm.1), custom_call_target="tpu_custom_call" | custom-call | bytes 1720320 | tf_op jit(solution)/shard_map/pallas_call | solution.py:528
  7.9 0.3 collective-permute-start.4
  8.2 1.2 %collective-permute-start.7 = (bf16[2,16,5632]{2,1,0:T(8,128)(2,1)S(1)}, bf16[2,16,5632]{2,1,0:T(8,128)(2,1)S(1)}, u32[]{:S(2)}, u32[]{:S(2)}) collective-permute-start(bf16[2,16,5632]{2,1,0:T(8,128)(2,1)S(1)} %dynamic-slice_bitcast_fusion), channel_id=1, source_target_pairs={{0,2},{2,0},{1,3},{3,1},{4,6},{6,4},{5,7},{7,5},{8,10},{10,8},{9,1... | collective-permute-start | bytes 1081352 | tf_op jit(solution)/shard_map/ppermute | solution.py:786
  9.7 4.2 %collective-permute-start.3 = (f32[248,128]{1,0:T(8,128)S(1)}, f32[248,128]{1,0:T(8,128)S(1)}, u32[]{:S(2)}, u32[]{:S(2)}) collective-permute-start(f32[248,128]{1,0:T(8,128)S(1)} %add.21), channel_id=1, source_target_pairs={{0,8},{4,12},{1,9},{5,13},{2,10},{6,14},{3,11},{7,15},{16,24},{20,... | collective-permute-start | bytes 380936 | tf_op jit(solution)/shard_map/ppermute | solution.py:544
  13.9 1.9 %collective-permute-start.2 = (f32[248,128]{1,0:T(8,128)S(1)}, f32[248,128]{1,0:T(8,128)S(1)}, u32[]{:S(2)}, u32[]{:S(2)}) collective-permute-start(f32[248,128]{1,0:T(8,128)S(1)} %add.21), channel_id=1, source_target_pairs={{0,4},{4,8},{8,12},{1,5},{5,9},{9,13},{2,6},{6,10},{10,14},{3,7},{... | collective-permute-start | bytes 380936 | tf_op jit(solution)/shard_map/ppermute | solution.py:543
  15.8 3.6 %collective-permute-done.3 = f32[248,128]{1,0:T(8,128)S(1)} collective-permute-done((f32[248,128]{1,0:T(8,128)S(1)}, f32[248,128]{1,0:T(8,128)S(1)}, u32[]{:S(2)}, u32[]{:S(2)}) %collective-permute-start.3) | collective-permute-done | bytes 127008 | tf_op jit(solution)/shard_map/ppermute | solution.py:544
  19.4 2.7 %collective-permute-done.2 = f32[248,128]{1,0:T(8,128)S(1)} collective-permute-done((f32[248,128]{1,0:T(8,128)S(1)}, f32[248,128]{1,0:T(8,128)S(1)}, u32[]{:S(2)}, u32[]{:S(2)}) %collective-permute-start.2) | collective-permute-done | bytes 127008 | tf_op jit(solution)/shard_map/ppermute | solution.py:543
  22.2 0.8 %collective-permute-start.5 = (f32[248,128]{1,0:T(8,128)S(1)}, f32[248,128]{1,0:T(8,128)S(1)}, u32[]{:S(2)}, u32[]{:S(2)}) collective-permute-start(f32[248,128]{1,0:T(8,128)S(1)} %multiply_add_fusion.1.state_ref), channel_id=1, source_target_pairs={{0,1},{1,0},{2,3},{3,2},{4,5},{5,4},{6,7},{7,6},{8,9},{9,8},{10,11... | collective-permute-start | bytes 380936 | tf_op jit(solution)/shard_map/ppermute | solution.py:553
  23.0 0.9 %collective-permute-done.5.came_ref = f32[248,128]{1,0:T(8,128)S(1)} collective-permute-done((f32[248,128]{1,0:T(8,128)S(1)}, f32[248,128]{1,0:T(8,128)S(1)}, u32[]{:S(2)}, u32[]{:S(2)}) %collective-permute-start.5) | collective-permute-done | bytes 127008 | tf_op jit(solution)/shard_map/ppermute | solution.py:553
  24.0 1.7 %shard_map.105 = (f32[248,128]{1,0:T(8,128)S(1)}, f32[248,128]{1,0:T(8,128)S(1)}, bf16[5,128,128]{2,1,0:T(8,128)(2,1)S(1)}, bf16[5,128,128]{2,1,0:T(8,128)(2,1)S(1)}) custom-call(f32[248,128]{1,0:T(8,128)S(1)} %multiply_add_fusion.1.state_ref, f32[248,128]{1,0:T(8,128)S(1)} %collective-permute-done.5.came_ref, ...), custom_call_target="tpu_custom_call" | custom-call | flops 256901120 | bytes 1146880 | tf_op jit(solution)/shard_map/pallas_call | solution.py:555
  25.7 0.4 collective-permute-start.6
  26.2 0.2 collective-permute-start.9
  26.4 0.7 %collective-permute-done.6 = f32[248,128]{1,0:T(8,128)S(1)} collective-permute-done((f32[248,128]{1,0:T(8,128)S(1)}, f32[248,128]{1,0:T(8,128)S(1)}, u32[]{:S(2)}, u32[]{:S(2)}) %collective-permute-start.6) | collective-permute-done | bytes 127008 | tf_op jit(solution)/shard_map/ppermute | solution.py:560
  27.1 0.3 collective-permute-done.9.refs_2_
  27.5 1.3 %collective-permute-start.11 = (f32[248,128]{1,0:T(8,128)S(1)}, f32[248,128]{1,0:T(8,128)S(1)}, u32[]{:S(2)}, u32[]{:S(2)}) collective-permute-start(f32[248,128]{1,0:T(8,128)S(1)} %add.24), channel_id=1, source_target_pairs={{8,0},{12,4},{9,1},{13,5},{10,2},{14,6},{11,3},{15,7},{24,16},{28,... | collective-permute-start | bytes 380936 | tf_op jit(solution)/shard_map/ppermute | solution.py:544
  28.8 1.9 %collective-permute-start.10 = (f32[248,128]{1,0:T(8,128)S(1)}, f32[248,128]{1,0:T(8,128)S(1)}, u32[]{:S(2)}, u32[]{:S(2)}) collective-permute-start(f32[248,128]{1,0:T(8,128)S(1)} %add.24), channel_id=1, source_target_pairs={{4,0},{8,4},{12,8},{5,1},{9,5},{13,9},{6,2},{10,6},{14,10},{7,3},{... | collective-permute-start | bytes 380936 | tf_op jit(solution)/shard_map/ppermute | solution.py:543
  30.7 1.2 %collective-permute-start.13 = (bf16[5,128,128]{2,1,0:T(8,128)(2,1)S(1)}, bf16[5,128,128]{2,1,0:T(8,128)(2,1)S(1)}, u32[]{:S(2)}, u32[]{:S(2)}) collective-permute-start(bf16[5,128,128]{2,1,0:T(8,128)(2,1)S(1)} %get-tuple-element.70), channel_id=1, source_target_pairs={{0,2},{2,0},{1,3},{3,1},{4,6},{6,4},{5,7},{7,5},{8,10},{10,8},{9,1... | collective-permute-start | bytes 491528 | tf_op jit(solution)/shard_map/ppermute | solution.py:565
  31.9 7.2 %shard_map.106 = bf16[8,16,5632]{2,1,0:T(8,128)(2,1)} custom-call(bf16[2,16,5632]{2,1,0:T(8,128)(2,1)S(1)} %collective-permute-done.7.refs_0_, bf16[8,2,5632]{2,1,0:T(2,128)(2,1)S(1)} %collective-permute-done.8.refs_1_, bf16[2,2,5632]{2,1,0:T(2,128)(2,1)S(1)} %collective-permute-done.9.refs_2_, bf16[8,16,5632]{2,1,0:T(8,128)(2,1)S(1)} %bitcast.21, ...), custom_call_target="tpu_custom_call" | custom-call | flops 2162688 | bytes 720896 | tf_op jit(solution)/shard_map/pallas_call | solution.py:801
  39.1 0.9 %collective-permute-done.10 = f32[248,128]{1,0:T(8,128)S(1)} collective-permute-done((f32[248,128]{1,0:T(8,128)S(1)}, f32[248,128]{1,0:T(8,128)S(1)}, u32[]{:S(2)}, u32[]{:S(2)}) %collective-permute-start.10) | collective-permute-done | bytes 127008 | tf_op jit(solution)/shard_map/ppermute | solution.py:543
  40.0 1.2 %collective-permute-start.12 = (f32[248,128]{1,0:T(8,128)S(1)}, f32[248,128]{1,0:T(8,128)S(1)}, u32[]{:S(2)}, u32[]{:S(2)}) collective-permute-start(f32[248,128]{1,0:T(8,128)S(1)} %multiply_add_fusion.here_ref), channel_id=1, source_target_pairs={{0,2},{2,0},{1,3},{3,1},{4,6},{6,4},{5,7},{7,5},{8,10},{10,8},{9,1... | collective-permute-start | bytes 380936 | tf_op jit(solution)/shard_map/ppermute | solution.py:574
  41.2 1.0 %collective-permute-start.15 = (f32[248,128]{1,0:T(8,128)S(1)}, f32[248,128]{1,0:T(8,128)S(1)}, u32[]{:S(2)}, u32[]{:S(2)}) collective-permute-start(f32[248,128]{1,0:T(8,128)S(1)} %multiply_add_fusion.here_ref), channel_id=1, source_target_pairs={{0,1},{1,0},{2,3},{3,2},{4,5},{5,4},{6,7},{7,6},{8,9},{9,8},{10,11... | collective-permute-start | bytes 380936 | tf_op jit(solution)/shard_map/ppermute | solution.py:575
  42.2 0.9 %shard_map.107 = bf16[128,1120]{1,0:T(8,128)(2,1)} custom-call(bf16[5,128,128]{2,1,0:T(8,128)(2,1)S(1)} %get-tuple-element.68.mine_ref, bf16[5,128,128]{2,1,0:T(8,128)(2,1)S(1)} %collective-permute-done.13.came_ref), custom_call_target="tpu_custom_call" | custom-call | bytes 573440 | tf_op jit(solution)/shard_map/pallas_call | solution.py:567
  43.2 1.1 %collective-permute-done.12.here_ref = f32[248,128]{1,0:T(8,128)S(1)} collective-permute-done((f32[248,128]{1,0:T(8,128)S(1)}, f32[248,128]{1,0:T(8,128)S(1)}, u32[]{:S(2)}, u32[]{:S(2)}) %collective-permute-start.12) | collective-permute-done | bytes 127008 | tf_op jit(solution)/shard_map/ppermute | solution.py:574
  44.3 1.6 %collective-permute-start.14 = (f32[248,128]{1,0:T(8,128)S(1)}, f32[248,128]{1,0:T(8,128)S(1)}, u32[]{:S(2)}, u32[]{:S(2)}) collective-permute-start(f32[248,128]{1,0:T(8,128)S(1)} %collective-permute-done.12.here_ref), channel_id=1, source_target_pairs={{0,1},{1,0},{2,3},{3,2},{4,5},{5,4},{6,7},{7,6},{8,9},{9,8},{10,11... | collective-permute-start | bytes 380936 | tf_op jit(solution)/shard_map/ppermute | solution.py:582
  45.9 0.7 %shard_map.108 = (bf16[5,128,128]{2,1,0:T(8,128)(2,1)S(1)}, bf16[5,128,128]{2,1,0:T(8,128)(2,1)S(1)}) custom-call(bf16[128,1120]{1,0:T(8,128)(2,1)S(1)} %bitcast.23, bf16[128,1120]{1,0:T(8,128)(2,1)S(1)} %bitcast.26, f32[248,128]{1,0:T(8,128)S(1)} %multiply_add_fusion.here_ref, f32[248,128]{1,0:T(8,128)S(1)} %collective-permute-done.15.came_ref), custom_call_target="tpu_custom_call" | custom-call | flops 73400320 | bytes 573440 | tf_op jit(solution)/shard_map/pallas_call | solution.py:578
  46.6 0.3 collective-permute-done.14.came_ref
  46.9 1.5 %shard_map.109 = (bf16[128,1120]{1,0:T(8,128)(2,1)}, bf16[128,1120]{1,0:T(8,128)(2,1)}) custom-call(bf16[128,1120]{1,0:T(8,128)(2,1)S(1)} %bitcast.24, bf16[128,1120]{1,0:T(8,128)(2,1)S(1)} %bitcast.27, f32[248,128]{1,0:T(8,128)S(1)} %collective-permute-done.12.here_ref, f32[248,128]{1,0:T(8,128)S(1)} %collective-permute-done.14.came_ref, ...), custom_call_target="tpu_custom_call" | custom-call | flops 73400320 | bytes 573440 | tf_op jit(solution)/shard_map/pallas_call | solution.py:584
  (24 shorter events, 0.6 us)
Async XLA Ops:
  0.6 8.8 %copy-start = (bf16[1,8,16,5632]{3,2,1,0:T(8,128)(2,1)S(1)}, bf16[1,8,16,5632]{3,2,1,0:T(8,128)(2,1)}, u32[]{:S(2)}) copy-start(bf16[1,8,16,5632]{3,2,1,0:T(8,128)(2,1)} %param.12) | copy-start | bytes 4325380
  2.8 1.9 %collective-permute-start = (f32[2,280,128]{2,1,0:T(8,128)S(1)}, f32[2,280,128]{2,1,0:T(8,128)S(1)}, u32[]{:S(2)}, u32[]{:S(2)}) collective-permute-start(f32[2,280,128]{2,1,0:T(8,128)S(1)} %get-tuple-element.44), channel_id=1, source_target_pairs={{0,1},{1,0},{2,3},{3,2},{4,5},{5,4},{6,7},{7,6},{8,9},{9,8},{10,11... | collective-permute-start | bytes 860168 | tf_op jit(solution)/shard_map/ppermute | solution.py:521
  4.9 4.7 %collective-permute-start.1 = (f32[248,128]{1,0:T(8,128)S(1)}, f32[248,128]{1,0:T(8,128)S(1)}, u32[]{:S(2)}, u32[]{:S(2)}) collective-permute-start(f32[248,128]{1,0:T(8,128)S(1)} %get-tuple-element.51), channel_id=1, source_target_pairs={{0,2},{2,0},{1,3},{3,1},{4,6},{6,4},{5,7},{7,5},{8,10},{10,8},{9,1... | collective-permute-start | bytes 380936 | tf_op jit(solution)/shard_map/ppermute | solution.py:524
  7.9 24.0 %copy-start.3 = (f32[9,5632]{1,0:T(8,128)S(1)}, f32[9,5632]{1,0:T(8,128)}, u32[]{:S(2)}) copy-start(f32[9,5632]{1,0:T(8,128)} %refs_4_.1) | copy-start | bytes 608260
  7.9 14.3 %collective-permute-start.4 = (bf16[2,5,128,128]{3,2,1,0:T(8,128)(2,1)S(1)}, bf16[2,5,128,128]{3,2,1,0:T(8,128)(2,1)S(1)}, u32[]{:S(2)}, u32[]{:S(2)}) collective-permute-start(bf16[2,5,128,128]{3,2,1,0:T(8,128)(2,1)S(1)} %get-tuple-element.49), channel_id=1, source_target_pairs={{0,2},{2,0},{1,3},{3,1},{4,6},{6,4},{5,7},{7,5},{8,10},{10,8},{9,1... | collective-permute-start | bytes 983048 | tf_op jit(solution)/shard_map/ppermute | solution.py:539
  8.2 17.9 %collective-permute-start.7 = (bf16[2,16,5632]{2,1,0:T(8,128)(2,1)S(1)}, bf16[2,16,5632]{2,1,0:T(8,128)(2,1)S(1)}, u32[]{:S(2)}, u32[]{:S(2)}) collective-permute-start(bf16[2,16,5632]{2,1,0:T(8,128)(2,1)S(1)} %dynamic-slice_bitcast_fusion), channel_id=1, source_target_pairs={{0,2},{2,0},{1,3},{3,1},{4,6},{6,4},{5,7},{7,5},{8,10},{10,8},{9,1... | collective-permute-start | bytes 1081352 | tf_op jit(solution)/shard_map/ppermute | solution.py:786
  9.7 9.8 %collective-permute-start.3 = (f32[248,128]{1,0:T(8,128)S(1)}, f32[248,128]{1,0:T(8,128)S(1)}, u32[]{:S(2)}, u32[]{:S(2)}) collective-permute-start(f32[248,128]{1,0:T(8,128)S(1)} %add.21), channel_id=1, source_target_pairs={{0,8},{4,12},{1,9},{5,13},{2,10},{6,14},{3,11},{7,15},{16,24},{20,... | collective-permute-start | bytes 380936 | tf_op jit(solution)/shard_map/ppermute | solution.py:544
  13.9 8.3 %collective-permute-start.2 = (f32[248,128]{1,0:T(8,128)S(1)}, f32[248,128]{1,0:T(8,128)S(1)}, u32[]{:S(2)}, u32[]{:S(2)}) collective-permute-start(f32[248,128]{1,0:T(8,128)S(1)} %add.21), channel_id=1, source_target_pairs={{0,4},{4,8},{8,12},{1,5},{5,9},{9,13},{2,6},{6,10},{10,14},{3,7},{... | collective-permute-start | bytes 380936 | tf_op jit(solution)/shard_map/ppermute | solution.py:543
  22.2 1.8 %collective-permute-start.5 = (f32[248,128]{1,0:T(8,128)S(1)}, f32[248,128]{1,0:T(8,128)S(1)}, u32[]{:S(2)}, u32[]{:S(2)}) collective-permute-start(f32[248,128]{1,0:T(8,128)S(1)} %multiply_add_fusion.1.state_ref), channel_id=1, source_target_pairs={{0,1},{1,0},{2,3},{3,2},{4,5},{5,4},{6,7},{7,6},{8,9},{9,8},{10,11... | collective-permute-start | bytes 380936 | tf_op jit(solution)/shard_map/ppermute | solution.py:553
  23.0 4.2 %collective-permute-start.8 = (bf16[8,2,5632]{2,1,0:T(2,128)(2,1)S(1)}, bf16[8,2,5632]{2,1,0:T(2,128)(2,1)S(1)}, u32[]{:S(2)}, u32[]{:S(2)}) collective-permute-start(bf16[8,2,5632]{2,1,0:T(2,128)(2,1)S(1)} %dynamic-slice_bitcast_fusion.1), channel_id=1, source_target_pairs={{0,1},{1,0},{2,3},{3,2},{4,5},{5,4},{6,7},{7,6},{8,9},{9,8},{10,11... | collective-permute-start | bytes 540680 | tf_op jit(solution)/shard_map/ppermute | solution.py:787
  25.7 1.4 %collective-permute-start.6 = (f32[248,128]{1,0:T(8,128)S(1)}, f32[248,128]{1,0:T(8,128)S(1)}, u32[]{:S(2)}, u32[]{:S(2)}) collective-permute-start(f32[248,128]{1,0:T(8,128)S(1)} %get-tuple-element.59), channel_id=1, source_target_pairs={{0,1},{1,0},{2,3},{3,2},{4,5},{5,4},{6,7},{7,6},{8,9},{9,8},{10,11... | collective-permute-start | bytes 380936 | tf_op jit(solution)/shard_map/ppermute | solution.py:560
  26.2 1.3 %collective-permute-start.9 = (bf16[2,2,5632]{2,1,0:T(2,128)(2,1)S(1)}, bf16[2,2,5632]{2,1,0:T(2,128)(2,1)S(1)}, u32[]{:S(2)}, u32[]{:S(2)}) collective-permute-start(bf16[2,2,5632]{2,1,0:T(2,128)(2,1)S(1)} %constant_dynamic-slice_fusion), channel_id=1, source_target_pairs={{0,1},{1,0},{2,3},{3,2},{4,5},{5,4},{6,7},{7,6},{8,9},{9,8},{10,11... | collective-permute-start | bytes 135176 | tf_op jit(solution)/shard_map/ppermute | solution.py:788
  27.5 11.6 %collective-permute-start.11 = (f32[248,128]{1,0:T(8,128)S(1)}, f32[248,128]{1,0:T(8,128)S(1)}, u32[]{:S(2)}, u32[]{:S(2)}) collective-permute-start(f32[248,128]{1,0:T(8,128)S(1)} %add.24), channel_id=1, source_target_pairs={{8,0},{12,4},{9,1},{13,5},{10,2},{14,6},{11,3},{15,7},{24,16},{28,... | collective-permute-start | bytes 380936 | tf_op jit(solution)/shard_map/ppermute | solution.py:544
  28.8 11.2 %collective-permute-start.10 = (f32[248,128]{1,0:T(8,128)S(1)}, f32[248,128]{1,0:T(8,128)S(1)}, u32[]{:S(2)}, u32[]{:S(2)}) collective-permute-start(f32[248,128]{1,0:T(8,128)S(1)} %add.24), channel_id=1, source_target_pairs={{4,0},{8,4},{12,8},{5,1},{9,5},{13,9},{6,2},{10,6},{14,10},{7,3},{... | collective-permute-start | bytes 380936 | tf_op jit(solution)/shard_map/ppermute | solution.py:543
  30.7 11.5 %collective-permute-start.13 = (bf16[5,128,128]{2,1,0:T(8,128)(2,1)S(1)}, bf16[5,128,128]{2,1,0:T(8,128)(2,1)S(1)}, u32[]{:S(2)}, u32[]{:S(2)}) collective-permute-start(bf16[5,128,128]{2,1,0:T(8,128)(2,1)S(1)} %get-tuple-element.70), channel_id=1, source_target_pairs={{0,2},{2,0},{1,3},{3,1},{4,6},{6,4},{5,7},{7,5},{8,10},{10,8},{9,1... | collective-permute-start | bytes 491528 | tf_op jit(solution)/shard_map/ppermute | solution.py:565
  31.9 14.0 %copy-start.1 = (bf16[1,8,16,1120]{3,2,1,0:T(8,128)(2,1)S(1)}, bf16[1,8,16,1120]{3,2,1,0:T(8,128)(2,1)}, u32[]{:S(2)}) copy-start(bf16[1,8,16,1120]{3,2,1,0:T(8,128)(2,1)} %param.8) | copy-start | bytes 860164
  31.9 14.0 %copy-start.2 = (bf16[1,8,16,1120]{3,2,1,0:T(8,128)(2,1)S(1)}, bf16[1,8,16,1120]{3,2,1,0:T(8,128)(2,1)}, u32[]{:S(2)}) copy-start(bf16[1,8,16,1120]{3,2,1,0:T(8,128)(2,1)} %param.9) | copy-start | bytes 860164
  40.0 4.3 %collective-permute-start.12 = (f32[248,128]{1,0:T(8,128)S(1)}, f32[248,128]{1,0:T(8,128)S(1)}, u32[]{:S(2)}, u32[]{:S(2)}) collective-permute-start(f32[248,128]{1,0:T(8,128)S(1)} %multiply_add_fusion.here_ref), channel_id=1, source_target_pairs={{0,2},{2,0},{1,3},{3,1},{4,6},{6,4},{5,7},{7,5},{8,10},{10,8},{9,1... | collective-permute-start | bytes 380936 | tf_op jit(solution)/shard_map/ppermute | solution.py:574
  41.2 4.7 %collective-permute-start.15 = (f32[248,128]{1,0:T(8,128)S(1)}, f32[248,128]{1,0:T(8,128)S(1)}, u32[]{:S(2)}, u32[]{:S(2)}) collective-permute-start(f32[248,128]{1,0:T(8,128)S(1)} %multiply_add_fusion.here_ref), channel_id=1, source_target_pairs={{0,1},{1,0},{2,3},{3,2},{4,5},{5,4},{6,7},{7,6},{8,9},{9,8},{10,11... | collective-permute-start | bytes 380936 | tf_op jit(solution)/shard_map/ppermute | solution.py:575
  44.3 2.6 %collective-permute-start.14 = (f32[248,128]{1,0:T(8,128)S(1)}, f32[248,128]{1,0:T(8,128)S(1)}, u32[]{:S(2)}, u32[]{:S(2)}) collective-permute-start(f32[248,128]{1,0:T(8,128)S(1)} %collective-permute-done.12.here_ref), channel_id=1, source_target_pairs={{0,1},{1,0},{2,3},{3,2},{4,5},{5,4},{6,7},{7,6},{8,9},{9,8},{10,11... | collective-permute-start | bytes 380936 | tf_op jit(solution)/shard_map/ppermute | solution.py:582

commit v7 on v6

--- a/solution.py
+++ b/solution.py
@@ -540,16 +540,19 @@
 
     def along_frames(own, step, meanwhile):
         moves = [[(at, at + step * hop) for at in range(frames) if 0 <= at + step * hop < frames] for hop in (1, 2)]
-        near = lax.ppermute(own, "tm", moves[0])
-        far = lax.ppermute(own, "tm", moves[1])
+        hops = (1, 2) if step > 0 else (2, 1)
+        sent = {hop: lax.ppermute(own, "tm", moves[hop - 1]) for hop in hops}
+        near, far = sent[1], sent[2]
         near, far, others = meanwhile(own, near, far)
         at = 0 if step > 0 else 2
         return own + masks[at : at + 1] * near + masks[at + 1 : at + 2] * far, others
 
     def fetch(own, near, far):
-        return lax.optimization_barrier((near, far, heads_sent))
-
-    state, heads_came = along_frames(own, 1, fetch)
+        block, _ = lax.optimization_barrier((hidden_pre[0], own))
+        near, far, kept = lax.optimization_barrier((near, far, (heads_sent, spread_block(block, conv_weight))))
+        return near, far, kept
+
+    state, (heads_came, spread_out) = along_frames(own, 1, fetch)
     came = lax.ppermute(state, "width", SWAP)
     back = struct((per_group, tokens, LANES), jnp.bfloat16)
     keep, send, back_mine, back_other = vmem_call(
@@ -563,11 +566,11 @@
     def convolve(own, near, far):
         other, _ = lax.optimization_barrier((back_other, own))
         back_came = lax.ppermute(other, "height", SWAP)
-        hidden_grad = ffn(hidden_pre, conv_weight, halo)
+        hidden_grad = ffn(hidden_pre, halo, spread_out)
         query_grad = vmem_call(
             join_kernel, struct((tokens, flat), jnp.bfloat16), n_in=2, bytes_accessed=4 * tokens * flat
         )(back_mine, back_came)
-        near, far, hidden_grad = lax.optimization_barrier((near, far, hidden_grad))
+        far, near, hidden_grad = lax.optimization_barrier((far, near, hidden_grad))
         return near, far, (query_grad, hidden_grad)
 
     total, (query_grad, hidden_grad) = along_frames(own, -1, convolve)
@@ -610,13 +613,37 @@
 UNROLL = 8
 
 
-def conv_kernel(bases, row_refs, *refs):
+def spread(load, refs, offsets, count, start, length):
+    for ref, offset in zip(refs, offsets):
+        for tile in range(count):
+            part = load(slice((offset + tile) * LANES, (offset + tile + 1) * LANES)).astype(jnp.float32)
+            ref[pl.ds(start + tile, length, stride=TILES), :] = part
+
+
+def spread_kernel(block_ref, weight_ref, source, taps):
+    rows, cols, channels = block_ref.shape
+    lane_tiles = channels // LANES // 2
+    pitch = -(-lane_tiles // TILES) * TILES
+    wide = cols + 2 * REACH
+    for tile in range(lane_tiles):
+        for place, at in ((tile, tile), (pitch + tile, lane_tiles + tile)):
+            taps[pl.ds(place, 9, stride=2 * pitch), :] = weight_ref[:, at * LANES : (at + 1) * LANES]
+
+    @pl.loop(0, rows)
+    def _(at):
+        start = pl.multiple_of(((at + REACH) * wide + REACH) * TILES, TILES)
+        for base in range(0, lane_tiles, TILES):
+            refs = source.at[base // TILES, 0], source.at[base // TILES, 1]
+            count = min(TILES, lane_tiles - base)
+            spread(lambda lanes: block_ref[at, :, lanes], refs, (base, lane_tiles + base), count, start, cols)
+
+
+def conv_kernel(row_refs, *refs):
     halo_rows, refs = refs[:row_refs], refs[row_refs:]
     side_ref, refs = refs[0], refs[1:]
     corners, refs = refs[:row_refs], refs[row_refs:]
-    block_ref, weight_ref = refs[:2]
-    out_hbm, taps, value_in, gate_in, value_grad, gate_grad, *results, out_ref, sems = refs[-8 - 2 * UNROLL :]
-    rows, cols, channels = block_ref.shape
+    _, taps, out_hbm, source, value_grad, gate_grad, *results, out_ref, sems = refs
+    rows, cols, channels = out_ref.shape
     lane_tiles = channels // LANES // 2
     pitch = -(-lane_tiles // TILES) * TILES
     row, column = lax.axis_index("height"), lax.axis_index("width")
@@ -624,12 +651,6 @@
     wide, tall = cols + 2 * REACH, rows + 2 * REACH
     grad_wide = wide - 2
 
-    for base in bases:
-        for tile in range(base, min(base + TILES, lane_tiles)):
-            for place, source in ((tile, tile), (pitch + tile, lane_tiles + tile)):
-                lanes = slice(source * LANES, (source + 1) * LANES)
-                taps[pl.ds(place, 9, stride=2 * pitch), :] = weight_ref[:, lanes]
-
     def source_at(at_row, at_col):
         return pl.multiple_of((at_row * wide + at_col) * TILES, TILES)
 
@@ -637,19 +658,12 @@
         return pl.multiple_of((at_row * grad_wide + at_col) * TILES, TILES)
 
     zero = jnp.zeros((TILES, LANES), jnp.float32)
-    low_border = jnp.where(first_row, 0, rows + REACH)
     outer_col = jnp.where(column == 0, 0, cols + REACH)
     side_col = jnp.where(column == 0, cols + REACH, 0)
     grad_outer_col = jnp.where(column == 0, 0, grad_wide - 1)
     start_col = jnp.where(column == 0, REACH, REACH - 1)
     low, high = jnp.where(first_row, REACH, REACH - 1), jnp.where(last_row, rows + REACH, rows + REACH + 1)
 
-    for ref in (value_in, gate_in):
-        @pl.loop(0, tall)
-        def _(at):
-            for extra in range(REACH):
-                ref[pl.ds(source_at(at, outer_col + extra), TILES), :] = zero
-
     for ref in (value_grad, gate_grad):
         @pl.loop(0, rows + 2)
         def _(at):
@@ -662,27 +676,34 @@
                     ref[pl.ds(grad_at(at, col), TILES), :] = zero
 
     copies = []
-    for base in bases:
+    for base in range(0, lane_tiles, TILES):
         count = min(TILES, lane_tiles - base)
-
-        def spread(load, at_row, at_col, length):
-            for ref, offset in ((value_in, base), (gate_in, lane_tiles + base)):
-                for tile in range(count):
-                    part = load(slice((offset + tile) * LANES, (offset + tile + 1) * LANES)).astype(jnp.float32)
-                    ref[pl.ds(source_at(at_row, at_col) + tile, length, stride=TILES), :] = part
+        value_in, gate_in = source.at[base // TILES, 0], source.at[base // TILES, 1]
+        offsets = base, lane_tiles + base
 
         @pl.loop(0, rows)
         def _(at):
-            spread(lambda lanes: block_ref[at, :, lanes], at + REACH, REACH, cols)
-            spread(lambda lanes: side_ref[at, :, lanes], at + REACH, side_col, REACH)
+            spread(
+                lambda lanes: side_ref[at, :, lanes], (value_in, gate_in), offsets, count,
+                source_at(at + REACH, side_col), REACH,
+            )
+            for ref in (value_in, gate_in):
+                for extra in range(REACH):
+                    ref[pl.ds(source_at(at + REACH, outer_col + extra), TILES), :] = zero
 
         for edge, at, which in ((first_row, 0, 0), (last_row, rows + REACH, row_refs - 1)):
             rows_ref, corner_ref = halo_rows[which], corners[which]
             for extra in range(REACH):
                 @pl.when(jnp.logical_not(edge))
                 def _():
-                    spread(lambda lanes: rows_ref[extra, :, lanes], at + extra, REACH, cols)
-                    spread(lambda lanes: corner_ref[extra, :, lanes], at + extra, side_col, REACH)
+                    for ref, col, length in ((rows_ref, REACH, cols), (corner_ref, side_col, REACH)):
+                        spread(
+                            lambda lanes: ref[extra, :, lanes], (value_in, gate_in), offsets, count,
+                            source_at(at + extra, col), length,
+                        )
+                    for ref in (value_in, gate_in):
+                        for side in range(REACH):
+                            ref[pl.ds(source_at(at + extra, outer_col + side), TILES), :] = zero
 
                 @pl.when(edge)
                 def _():
@@ -789,32 +810,40 @@
     return halo_rows, side, corners
 
 
-def conv_part(bases, halo, block, conv_weight, given=()):
+def spread_block(block, conv_weight):
+    rows, cols, channels = block.shape
+    chunks = -(-channels // LANES // 2 // TILES)
+    size = (rows + 2 * REACH) * (cols + 2 * REACH) * TILES
+    return vmem_call(
+        spread_kernel,
+        (struct((chunks, 2, size, LANES)), struct((9 * 2 * chunks * TILES, LANES))),
+        n_in=2, flops=rows * cols * channels, bytes_accessed=rows * cols * channels,
+    )(block, conv_weight)
+
+
+def ffn(hidden_pre, halo, spread_out):
     halo_rows, side, corners = halo
-    rows, cols, channels = block.shape
-    lane_tiles = channels // LANES // 2
-    pitch = -(-lane_tiles // TILES) * TILES
-    source = pltpu.VMEM(((rows + 2 * REACH) * (cols + 2 * REACH) * TILES, LANES), jnp.float32)
+    rows, cols, channels = hidden_pre.shape[1:]
+    source, taps = spread_out
+    chunks = source.shape[0]
+    vmem, hbm = pl.BlockSpec(memory_space=pltpu.VMEM), pl.BlockSpec(memory_space=pltpu.HBM)
     grad = pltpu.VMEM(((rows + 2) * (cols + 2) * TILES, LANES), jnp.float32)
     result = pltpu.VMEM((cols * TILES, LANES), jnp.float32)
     size = rows * cols * channels
-    return vmem_call(
-        functools.partial(conv_kernel, bases, len(halo_rows)),
-        struct((rows, cols, channels), jnp.bfloat16),
-        [pltpu.VMEM((9 * 2 * pitch, LANES), jnp.float32), source, source, grad, grad, *[result] * (2 * UNROLL),
-         pltpu.VMEM((rows, cols, channels), jnp.bfloat16), pltpu.SemaphoreType.DMA((2, pitch // TILES))],
-        n_in=2 * len(halo_rows) + 3, n_given=len(given), flops=size * len(bases), bytes_accessed=size, vmem_mib=12,
-        out_hbm=True,
-    )(*halo_rows, side, *corners, block, conv_weight, *given)
-
-
-def conv_bases(hidden_pre):
-    lane_tiles = hidden_pre.shape[3] // LANES // 2
-    return list(range(0, lane_tiles, TILES))
-
-
-def ffn(hidden_pre, conv_weight, halo):
-    return conv_part(conv_bases(hidden_pre), halo, hidden_pre[0], conv_weight)[None]
+    hidden_grad, _ = pl.pallas_call(
+        functools.partial(conv_kernel, len(halo_rows)),
+        out_shape=(struct((rows, cols, channels), jnp.bfloat16), struct(source.shape)),
+        in_specs=[vmem] * (2 * len(halo_rows) + 3),
+        out_specs=(hbm, vmem),
+        scratch_shapes=[
+            grad, grad, *[result] * (2 * UNROLL),
+            pltpu.VMEM((rows, cols, channels), jnp.bfloat16), pltpu.SemaphoreType.DMA((2, chunks)),
+        ],
+        input_output_aliases={2 * len(halo_rows) + 1: 1},
+        cost_estimate=pl.CostEstimate(flops=2 * size, bytes_accessed=size, transcendentals=0),
+        compiler_params=pltpu.CompilerParams(vmem_limit_bytes=8 << 20),
+    )(*halo_rows, side, *corners, source, taps)
+    return hidden_grad[None]
 
 
 def per_device(queries, attn_keys, attn_values, attn_cotangent, clip_ids, hidden_pre, conv_weight):
@@ -824,7 +853,8 @@
         return paired(queries, attn_keys, attn_values, attn_cotangent, clip_ids, hidden_pre, conv_weight)
     grads = general_attention(queries, attn_keys, attn_values, attn_cotangent, clip_ids)
     if blocked:
-        return (*grads, ffn(hidden_pre, conv_weight, halo_arrays(row_edges(hidden_pre), side_edge(hidden_pre[0]))))
+        halo = halo_arrays(row_edges(hidden_pre), side_edge(hidden_pre[0]))
+        return (*grads, ffn(hidden_pre, halo, spread_block(hidden_pre[0], conv_weight)))
     return (*grads, mixed_ffn(hidden_pre, conv_weight))
 
 

time: 48.9 us -> 47.8 us (0.978)
  waiting for transfers between devices: 10.8 us -> 6.32 us
  starting transfers between devices: 19.4 us -> 23 us
    ppermute x4, waiting for transfers between devices: 7.21 us -> 3.81 us  [along_frames(): sent = {hop: lax.ppermute(own, 'tm', moves[hop - 1]) for hop in hops}]
    ppermute x1, starting transfers between devices: 0.78 us -> 2.98 us  [paired(): came = lax.ppermute(state, 'width', SWAP)]
    ppermute x1, waiting for transfers between devices: 1.14 us -> 0.26 us  [paired(): far = lax.ppermute(total, 'height', SWAP)]
    ppermute x1, starting transfers between devices: 1.62 us -> 2.33 us  [paired(): far_came = lax.ppermute(far, 'width', SWAP)]
    ppermute x1, starting transfers between devices: 1.2 us -> 1.74 us  [convolve(): back_came = lax.ppermute(other, 'height', SWAP)]
    pallas_call x1 -> x2, Pallas kernels: 7.19 us -> 6.97 us  [the longest x1 6.44 us: ffn(): pl.pallas_call(functools.partial(conv_kernel, len(halo_rows)), out_shape=...]
  transfers between devices with their start and end apart: 16 -> 16, of which waited for: 9 -> 8; matrix products, arithmetic and copies ran while one was open for 3% -> 3% of each run, Pallas kernels for 25% -> 25%
where the time goes in v7:
time: 47.8 us; the launch traced here: 47.4 us
  starting transfers between devices  23 us (48%)
  Pallas kernels  15.8 us (33%)
  waiting for transfers between devices  6.32 us (13%)
  local copies, waits for them, and re-layouts  1.28 us (3%)
  between operations  0.83 us (2%)
    ppermute x4, starting transfers between devices, along_frames(): sent = {hop: lax.ppermute(own, 'tm', moves[hop - 1]) for hop in hops}  8.86 us
    pallas_call x1, Pallas kernels, ffn(): pl.pallas_call(functools.partial(conv_kernel, len(halo_rows)), out_shape=...  6.44 us
    ppermute x4, waiting for transfers between devices, along_frames(): sent = {hop: lax.ppermute(own, 'tm', moves[hop - 1]) for hop in hops}  3.81 us
    ppermute x1, starting transfers between devices, paired(): came = lax.ppermute(state, 'width', SWAP)  2.98 us
    ppermute x1, starting transfers between devices, paired(): far_came = lax.ppermute(far, 'width', SWAP)  2.33 us
    pallas_call x1, Pallas kernels, paired(): vmem_call(state_kernel, (pair, pair), [pltpu.VMEM((2, 2, half, LANES), jn...  2.12 us
    ppermute x1, starting transfers between devices, convolve(): back_came = lax.ppermute(other, 'height', SWAP)  1.74 us
    pallas_call x1, Pallas kernels, paired(): vmem_call(query_kernel, (share, share, back, back), [pltpu.VMEM((2, half,...  1.73 us
  transfers between devices with their start and end apart: 16, of which 8 were waited for; matrix products, arithmetic and copies ran while one was open for 3% of the time, Pallas kernels for 25%

profile of v7, /device:TPU:9, one launch (start us, length us, event | category | flops | bytes accessed | tf_op | source)
XLA Modules:
  0.0 47.4 jit_solution(12623551893278608877)
XLA Ops:
  0.6 2.1 %shard_map.102 = (f32[2,280,128]{2,1,0:T(8,128)S(1)}, f32[2,280,128]{2,1,0:T(8,128)S(1)}) custom-call(bf16[128,1120]{1,0:T(8,128)(2,1)} %bitcast.22, bf16[128,1120]{1,0:T(8,128)(2,1)} %bitcast.25), custom_call_target="tpu_custom_call" | custom-call | flops 36700160 | bytes 1146880 | tf_op jit(solution)/shard_map/pallas_call | solution.py:515
  2.8 0.7 %collective-permute-start = (f32[2,280,128]{2,1,0:T(8,128)S(1)}, f32[2,280,128]{2,1,0:T(8,128)S(1)}, u32[]{:S(2)}, u32[]{:S(2)}) collective-permute-start(f32[2,280,128]{2,1,0:T(8,128)S(1)} %get-tuple-element.50), channel_id=1, source_target_pairs={{0,1},{1,0},{2,3},{3,2},{4,5},{5,4},{6,7},{7,6},{8,9},{9,8},{10,11... | collective-permute-start | bytes 860168 | tf_op jit(solution)/shard_map/ppermute | solution.py:521
  3.5 1.0 %dynamic-slice_bitcast_fusion = bf16[2,16,5632]{2,1,0:T(8,128)(2,1)S(1)} fusion(bf16[1,8,16,5632]{3,2,1,0:T(8,128)(2,1)} %param.12, s32[]{:T(128)S(6)} %select_n.11), kind=kLoop, calls=%fused_computation | loop fusion | bytes 720900 | tf_op jit(solution)/shard_map/dynamic_slice | solution.py:787
  4.7 0.2 shard_map.103
  4.9 1.3 %collective-permute-start.1 = (f32[248,128]{1,0:T(8,128)S(1)}, f32[248,128]{1,0:T(8,128)S(1)}, u32[]{:S(2)}, u32[]{:S(2)}) collective-permute-start(f32[248,128]{1,0:T(8,128)S(1)} %get-tuple-element.57), channel_id=1, source_target_pairs={{0,2},{2,0},{1,3},{3,1},{4,6},{6,4},{5,7},{7,5},{8,10},{10,8},{9,1... | collective-permute-start | bytes 380936 | tf_op jit(solution)/shard_map/ppermute | solution.py:524
  6.2 1.7 %shard_map.104 = (bf16[2,5,128,128]{3,2,1,0:T(8,128)(2,1)S(1)}, bf16[2,5,128,128]{3,2,1,0:T(8,128)(2,1)S(1)}, f32[8,128]{1,0:T(8,128)S(1)}) custom-call(bf16[128,1120]{1,0:T(8,128)(2,1)} %bitcast.29, bf16[128,1120]{1,0:T(8,128)(2,1)} %bitcast.30, s32[4]{0:T(128)} %clip_hbm.1), custom_call_target="tpu_custom_call" | custom-call | bytes 1720320 | tf_op jit(solution)/shard_map/pallas_call | solution.py:528
  7.9 0.3 collective-permute-start.4
  8.2 1.2 %collective-permute-start.7 = (bf16[2,16,5632]{2,1,0:T(8,128)(2,1)S(1)}, bf16[2,16,5632]{2,1,0:T(8,128)(2,1)S(1)}, u32[]{:S(2)}, u32[]{:S(2)}) collective-permute-start(bf16[2,16,5632]{2,1,0:T(8,128)(2,1)S(1)} %dynamic-slice_bitcast_fusion), channel_id=1, source_target_pairs={{0,2},{2,0},{1,3},{3,1},{4,6},{6,4},{5,7},{7,5},{8,10},{10,8},{9,1... | collective-permute-start | bytes 1081352 | tf_op jit(solution)/shard_map/ppermute | solution.py:807
  9.7 3.2 %collective-permute-start.2 = (f32[248,128]{1,0:T(8,128)S(1)}, f32[248,128]{1,0:T(8,128)S(1)}, u32[]{:S(2)}, u32[]{:S(2)}) collective-permute-start(f32[248,128]{1,0:T(8,128)S(1)} %add.21), channel_id=1, source_target_pairs={{0,4},{4,8},{8,12},{1,5},{5,9},{9,13},{2,6},{6,10},{10,14},{3,7},{... | collective-permute-start | bytes 380936 | tf_op jit(solution)/shard_map/ppermute | solution.py:544
  12.9 2.3 %collective-permute-start.3 = (f32[248,128]{1,0:T(8,128)S(1)}, f32[248,128]{1,0:T(8,128)S(1)}, u32[]{:S(2)}, u32[]{:S(2)}) collective-permute-start(f32[248,128]{1,0:T(8,128)S(1)} %add.21), channel_id=1, source_target_pairs={{0,8},{4,12},{1,9},{5,13},{2,10},{6,14},{3,11},{7,15},{16,24},{20,... | collective-permute-start | bytes 380936 | tf_op jit(solution)/shard_map/ppermute | solution.py:544
  15.2 0.5 %shard_map.105 = (f32[3,2,1920,128]{3,2,1,0:T(8,128)S(1)}, f32[432,128]{1,0:T(8,128)S(1)}) custom-call(bf16[8,16,5632]{2,1,0:T(8,128)(2,1)S(1)} %bitcast.21, f32[9,5632]{1,0:T(8,128)S(1)} %copy-done.3), custom_call_target="tpu_custom_call" | custom-call | flops 720896 | bytes 720896 | tf_op jit(solution)/shard_map/pallas_call | solution.py:817
  15.8 3.6 %collective-permute-done.3 = f32[248,128]{1,0:T(8,128)S(1)} collective-permute-done((f32[248,128]{1,0:T(8,128)S(1)}, f32[248,128]{1,0:T(8,128)S(1)}, u32[]{:S(2)}, u32[]{:S(2)}) %collective-permute-start.3) | collective-permute-done | bytes 127008 | tf_op jit(solution)/shard_map/ppermute | solution.py:544
  19.4 3.0 %collective-permute-start.5 = (f32[248,128]{1,0:T(8,128)S(1)}, f32[248,128]{1,0:T(8,128)S(1)}, u32[]{:S(2)}, u32[]{:S(2)}) collective-permute-start(f32[248,128]{1,0:T(8,128)S(1)} %multiply_add_fusion.1.state_ref), channel_id=1, source_target_pairs={{0,1},{1,0},{2,3},{3,2},{4,5},{5,4},{6,7},{7,6},{8,9},{9,8},{10,11... | collective-permute-start | bytes 380936 | tf_op jit(solution)/shard_map/ppermute | solution.py:556
  22.4 0.9 %collective-permute-done.5.came_ref = f32[248,128]{1,0:T(8,128)S(1)} collective-permute-done((f32[248,128]{1,0:T(8,128)S(1)}, f32[248,128]{1,0:T(8,128)S(1)}, u32[]{:S(2)}, u32[]{:S(2)}) %collective-permute-start.5) | collective-permute-done | bytes 127008 | tf_op jit(solution)/shard_map/ppermute | solution.py:556
  23.3 1.7 %shard_map.106 = (f32[248,128]{1,0:T(8,128)S(1)}, f32[248,128]{1,0:T(8,128)S(1)}, bf16[5,128,128]{2,1,0:T(8,128)(2,1)S(1)}, bf16[5,128,128]{2,1,0:T(8,128)(2,1)S(1)}) custom-call(f32[248,128]{1,0:T(8,128)S(1)} %multiply_add_fusion.1.state_ref, f32[248,128]{1,0:T(8,128)S(1)} %collective-permute-done.5.came_ref, ...), custom_call_target="tpu_custom_call" | custom-call | flops 256901120 | bytes 1146880 | tf_op jit(solution)/shard_map/pallas_call | solution.py:558
  25.1 0.4 collective-permute-start.6
  25.5 0.4 collective-permute-start.9
  25.9 0.5 %collective-permute-done.6 = f32[248,128]{1,0:T(8,128)S(1)} collective-permute-done((f32[248,128]{1,0:T(8,128)S(1)}, f32[248,128]{1,0:T(8,128)S(1)}, u32[]{:S(2)}, u32[]{:S(2)}) %collective-permute-start.6) | collective-permute-done | bytes 127008 | tf_op jit(solution)/shard_map/ppermute | solution.py:563
  26.5 0.3 collective-permute-done.9.refs_2_
  26.8 1.3 %collective-permute-start.10 = (f32[248,128]{1,0:T(8,128)S(1)}, f32[248,128]{1,0:T(8,128)S(1)}, u32[]{:S(2)}, u32[]{:S(2)}) collective-permute-start(f32[248,128]{1,0:T(8,128)S(1)} %add.24), channel_id=1, source_target_pairs={{8,0},{12,4},{9,1},{13,5},{10,2},{14,6},{11,3},{15,7},{24,16},{28,... | collective-permute-start | bytes 380936 | tf_op jit(solution)/shard_map/ppermute | solution.py:544
  28.1 2.1 %collective-permute-start.11 = (f32[248,128]{1,0:T(8,128)S(1)}, f32[248,128]{1,0:T(8,128)S(1)}, u32[]{:S(2)}, u32[]{:S(2)}) collective-permute-start(f32[248,128]{1,0:T(8,128)S(1)} %add.24), channel_id=1, source_target_pairs={{4,0},{8,4},{12,8},{5,1},{9,5},{13,9},{6,2},{10,6},{14,10},{7,3},{... | collective-permute-start | bytes 380936 | tf_op jit(solution)/shard_map/ppermute | solution.py:544
  30.2 1.7 %collective-permute-start.13 = (bf16[5,128,128]{2,1,0:T(8,128)(2,1)S(1)}, bf16[5,128,128]{2,1,0:T(8,128)(2,1)S(1)}, u32[]{:S(2)}, u32[]{:S(2)}) collective-permute-start(bf16[5,128,128]{2,1,0:T(8,128)(2,1)S(1)} %get-tuple-element.82), channel_id=1, source_target_pairs={{0,2},{2,0},{1,3},{3,1},{4,6},{6,4},{5,7},{7,5},{8,10},{10,8},{9,1... | collective-permute-start | bytes 491528 | tf_op jit(solution)/shard_map/ppermute | solution.py:568
  32.0 6.4 %shard_map.107 = (bf16[8,16,5632]{2,1,0:T(8,128)(2,1)}, f32[3,2,1920,128]{3,2,1,0:T(8,128)S(1)}) custom-call(bf16[2,16,5632]{2,1,0:T(8,128)(2,1)S(1)} %collective-permute-done.7.refs_0_, bf16[8,2,5632]{2,1,0:T(2,128)(2,1)S(1)} %collective-permute-done.8.refs_1_, ...), custom_call_target="tpu_custom_call", output_to_operand_aliasing={{1}: (3, {})} | custom-call | flops 1441792 | bytes 720896 | tf_op jit(solution)/shard_map/pallas_call | solution.py:833
  38.4 0.3 collective-permute-done.11
  38.7 1.4 %collective-permute-start.12 = (f32[248,128]{1,0:T(8,128)S(1)}, f32[248,128]{1,0:T(8,128)S(1)}, u32[]{:S(2)}, u32[]{:S(2)}) collective-permute-start(f32[248,128]{1,0:T(8,128)S(1)} %multiply_add_fusion.here_ref), channel_id=1, source_target_pairs={{0,2},{2,0},{1,3},{3,1},{4,6},{6,4},{5,7},{7,5},{8,10},{10,8},{9,1... | collective-permute-start | bytes 380936 | tf_op jit(solution)/shard_map/ppermute | solution.py:577
  40.1 1.3 %collective-permute-start.15 = (f32[248,128]{1,0:T(8,128)S(1)}, f32[248,128]{1,0:T(8,128)S(1)}, u32[]{:S(2)}, u32[]{:S(2)}) collective-permute-start(f32[248,128]{1,0:T(8,128)S(1)} %multiply_add_fusion.here_ref), channel_id=1, source_target_pairs={{0,1},{1,0},{2,3},{3,2},{4,5},{5,4},{6,7},{7,6},{8,9},{9,8},{10,11... | collective-permute-start | bytes 380936 | tf_op jit(solution)/shard_map/ppermute | solution.py:578
  41.4 0.9 %shard_map.108 = bf16[128,1120]{1,0:T(8,128)(2,1)} custom-call(bf16[5,128,128]{2,1,0:T(8,128)(2,1)S(1)} %get-tuple-element.80.mine_ref, bf16[5,128,128]{2,1,0:T(8,128)(2,1)S(1)} %collective-permute-done.13.came_ref), custom_call_target="tpu_custom_call" | custom-call | bytes 573440 | tf_op jit(solution)/shard_map/pallas_call | solution.py:570
  42.3 0.3 collective-permute-done.12.here_ref
  42.5 2.3 %collective-permute-start.14 = (f32[248,128]{1,0:T(8,128)S(1)}, f32[248,128]{1,0:T(8,128)S(1)}, u32[]{:S(2)}, u32[]{:S(2)}) collective-permute-start(f32[248,128]{1,0:T(8,128)S(1)} %collective-permute-done.12.here_ref), channel_id=1, source_target_pairs={{0,1},{1,0},{2,3},{3,2},{4,5},{5,4},{6,7},{7,6},{8,9},{9,8},{10,11... | collective-permute-start | bytes 380936 | tf_op jit(solution)/shard_map/ppermute | solution.py:585
  44.9 0.7 %shard_map.109 = (bf16[5,128,128]{2,1,0:T(8,128)(2,1)S(1)}, bf16[5,128,128]{2,1,0:T(8,128)(2,1)S(1)}) custom-call(bf16[128,1120]{1,0:T(8,128)(2,1)S(1)} %bitcast.23, bf16[128,1120]{1,0:T(8,128)(2,1)S(1)} %bitcast.26, f32[248,128]{1,0:T(8,128)S(1)} %multiply_add_fusion.here_ref, f32[248,128]{1,0:T(8,128)S(1)} %collective-permute-done.15.came_ref), custom_call_target="tpu_custom_call" | custom-call | flops 73400320 | bytes 573440 | tf_op jit(solution)/shard_map/pallas_call | solution.py:581
  45.6 0.3 collective-permute-done.14.came_ref
  45.9 1.5 %shard_map.110 = (bf16[128,1120]{1,0:T(8,128)(2,1)}, bf16[128,1120]{1,0:T(8,128)(2,1)}) custom-call(bf16[128,1120]{1,0:T(8,128)(2,1)S(1)} %bitcast.24, bf16[128,1120]{1,0:T(8,128)(2,1)S(1)} %bitcast.27, f32[248,128]{1,0:T(8,128)S(1)} %collective-permute-done.12.here_ref, f32[248,128]{1,0:T(8,128)S(1)} %collective-permute-done.14.came_ref, ...), custom_call_target="tpu_custom_call" | custom-call | flops 73400320 | bytes 573440 | tf_op jit(solution)/shard_map/pallas_call | solution.py:587
  (25 shorter events, 0.7 us)
Async XLA Ops:
  0.6 8.8 %copy-start = (bf16[1,8,16,5632]{3,2,1,0:T(8,128)(2,1)S(1)}, bf16[1,8,16,5632]{3,2,1,0:T(8,128)(2,1)}, u32[]{:S(2)}) copy-start(bf16[1,8,16,5632]{3,2,1,0:T(8,128)(2,1)} %param.12) | copy-start | bytes 4325380
  2.8 12.4 %copy-start.3 = (f32[9,5632]{1,0:T(8,128)S(1)}, f32[9,5632]{1,0:T(8,128)}, u32[]{:S(2)}) copy-start(f32[9,5632]{1,0:T(8,128)} %weight_ref.1) | copy-start | bytes 608260
  2.8 1.9 %collective-permute-start = (f32[2,280,128]{2,1,0:T(8,128)S(1)}, f32[2,280,128]{2,1,0:T(8,128)S(1)}, u32[]{:S(2)}, u32[]{:S(2)}) collective-permute-start(f32[2,280,128]{2,1,0:T(8,128)S(1)} %get-tuple-element.50), channel_id=1, source_target_pairs={{0,1},{1,0},{2,3},{3,2},{4,5},{5,4},{6,7},{7,6},{8,9},{9,8},{10,11... | collective-permute-start | bytes 860168 | tf_op jit(solution)/shard_map/ppermute | solution.py:521
  4.9 4.7 %collective-permute-start.1 = (f32[248,128]{1,0:T(8,128)S(1)}, f32[248,128]{1,0:T(8,128)S(1)}, u32[]{:S(2)}, u32[]{:S(2)}) collective-permute-start(f32[248,128]{1,0:T(8,128)S(1)} %get-tuple-element.57), channel_id=1, source_target_pairs={{0,2},{2,0},{1,3},{3,1},{4,6},{6,4},{5,7},{7,5},{8,10},{10,8},{9,1... | collective-permute-start | bytes 380936 | tf_op jit(solution)/shard_map/ppermute | solution.py:524
  7.9 11.4 %collective-permute-start.4 = (bf16[2,5,128,128]{3,2,1,0:T(8,128)(2,1)S(1)}, bf16[2,5,128,128]{3,2,1,0:T(8,128)(2,1)S(1)}, u32[]{:S(2)}, u32[]{:S(2)}) collective-permute-start(bf16[2,5,128,128]{3,2,1,0:T(8,128)(2,1)S(1)} %get-tuple-element.55), channel_id=1, source_target_pairs={{0,2},{2,0},{1,3},{3,1},{4,6},{6,4},{5,7},{7,5},{8,10},{10,8},{9,1... | collective-permute-start | bytes 983048 | tf_op jit(solution)/shard_map/ppermute | solution.py:539
  8.2 17.2 %collective-permute-start.7 = (bf16[2,16,5632]{2,1,0:T(8,128)(2,1)S(1)}, bf16[2,16,5632]{2,1,0:T(8,128)(2,1)S(1)}, u32[]{:S(2)}, u32[]{:S(2)}) collective-permute-start(bf16[2,16,5632]{2,1,0:T(8,128)(2,1)S(1)} %dynamic-slice_bitcast_fusion), channel_id=1, source_target_pairs={{0,2},{2,0},{1,3},{3,1},{4,6},{6,4},{5,7},{7,5},{8,10},{10,8},{9,1... | collective-permute-start | bytes 1081352 | tf_op jit(solution)/shard_map/ppermute | solution.py:807
  9.7 6.1 %collective-permute-start.2 = (f32[248,128]{1,0:T(8,128)S(1)}, f32[248,128]{1,0:T(8,128)S(1)}, u32[]{:S(2)}, u32[]{:S(2)}) collective-permute-start(f32[248,128]{1,0:T(8,128)S(1)} %add.21), channel_id=1, source_target_pairs={{0,4},{4,8},{8,12},{1,5},{5,9},{9,13},{2,6},{6,10},{10,14},{3,7},{... | collective-permute-start | bytes 380936 | tf_op jit(solution)/shard_map/ppermute | solution.py:544
  12.9 6.4 %collective-permute-start.3 = (f32[248,128]{1,0:T(8,128)S(1)}, f32[248,128]{1,0:T(8,128)S(1)}, u32[]{:S(2)}, u32[]{:S(2)}) collective-permute-start(f32[248,128]{1,0:T(8,128)S(1)} %add.21), channel_id=1, source_target_pairs={{0,8},{4,12},{1,9},{5,13},{2,10},{6,14},{3,11},{7,15},{16,24},{20,... | collective-permute-start | bytes 380936 | tf_op jit(solution)/shard_map/ppermute | solution.py:544
  19.4 4.0 %collective-permute-start.5 = (f32[248,128]{1,0:T(8,128)S(1)}, f32[248,128]{1,0:T(8,128)S(1)}, u32[]{:S(2)}, u32[]{:S(2)}) collective-permute-start(f32[248,128]{1,0:T(8,128)S(1)} %multiply_add_fusion.1.state_ref), channel_id=1, source_target_pairs={{0,1},{1,0},{2,3},{3,2},{4,5},{5,4},{6,7},{7,6},{8,9},{9,8},{10,11... | collective-permute-start | bytes 380936 | tf_op jit(solution)/shard_map/ppermute | solution.py:556
  22.3 4.1 %collective-permute-start.8 = (bf16[8,2,5632]{2,1,0:T(2,128)(2,1)S(1)}, bf16[8,2,5632]{2,1,0:T(2,128)(2,1)S(1)}, u32[]{:S(2)}, u32[]{:S(2)}) collective-permute-start(bf16[8,2,5632]{2,1,0:T(2,128)(2,1)S(1)} %dynamic-slice_bitcast_fusion.1), channel_id=1, source_target_pairs={{0,1},{1,0},{2,3},{3,2},{4,5},{5,4},{6,7},{7,6},{8,9},{9,8},{10,11... | collective-permute-start | bytes 540680 | tf_op jit(solution)/shard_map/ppermute | solution.py:808
  25.1 1.4 %collective-permute-start.6 = (f32[248,128]{1,0:T(8,128)S(1)}, f32[248,128]{1,0:T(8,128)S(1)}, u32[]{:S(2)}, u32[]{:S(2)}) collective-permute-start(f32[248,128]{1,0:T(8,128)S(1)} %get-tuple-element.68), channel_id=1, source_target_pairs={{0,1},{1,0},{2,3},{3,2},{4,5},{5,4},{6,7},{7,6},{8,9},{9,8},{10,11... | collective-permute-start | bytes 380936 | tf_op jit(solution)/shard_map/ppermute | solution.py:563
  25.5 1.3 %collective-permute-start.9 = (bf16[2,2,5632]{2,1,0:T(2,128)(2,1)S(1)}, bf16[2,2,5632]{2,1,0:T(2,128)(2,1)S(1)}, u32[]{:S(2)}, u32[]{:S(2)}) collective-permute-start(bf16[2,2,5632]{2,1,0:T(2,128)(2,1)S(1)} %constant_dynamic-slice_fusion), channel_id=1, source_target_pairs={{0,1},{1,0},{2,3},{3,2},{4,5},{5,4},{6,7},{7,6},{8,9},{9,8},{10,11... | collective-permute-start | bytes 135176 | tf_op jit(solution)/shard_map/ppermute | solution.py:809
  26.8 11.6 %collective-permute-start.10 = (f32[248,128]{1,0:T(8,128)S(1)}, f32[248,128]{1,0:T(8,128)S(1)}, u32[]{:S(2)}, u32[]{:S(2)}) collective-permute-start(f32[248,128]{1,0:T(8,128)S(1)} %add.24), channel_id=1, source_target_pairs={{8,0},{12,4},{9,1},{13,5},{10,2},{14,6},{11,3},{15,7},{24,16},{28,... | collective-permute-start | bytes 380936 | tf_op jit(solution)/shard_map/ppermute | solution.py:544
  28.1 10.6 %collective-permute-start.11 = (f32[248,128]{1,0:T(8,128)S(1)}, f32[248,128]{1,0:T(8,128)S(1)}, u32[]{:S(2)}, u32[]{:S(2)}) collective-permute-start(f32[248,128]{1,0:T(8,128)S(1)} %add.24), channel_id=1, source_target_pairs={{4,0},{8,4},{12,8},{5,1},{9,5},{13,9},{6,2},{10,6},{14,10},{7,3},{... | collective-permute-start | bytes 380936 | tf_op jit(solution)/shard_map/ppermute | solution.py:544
  30.2 14.7 %copy-start.1 = (bf16[1,8,16,1120]{3,2,1,0:T(8,128)(2,1)S(1)}, bf16[1,8,16,1120]{3,2,1,0:T(8,128)(2,1)}, u32[]{:S(2)}) copy-start(bf16[1,8,16,1120]{3,2,1,0:T(8,128)(2,1)} %param.8) | copy-start | bytes 860164
  30.2 14.7 %copy-start.2 = (bf16[1,8,16,1120]{3,2,1,0:T(8,128)(2,1)S(1)}, bf16[1,8,16,1120]{3,2,1,0:T(8,128)(2,1)}, u32[]{:S(2)}) copy-start(bf16[1,8,16,1120]{3,2,1,0:T(8,128)(2,1)} %param.9) | copy-start | bytes 860164
  30.2 11.1 %collective-permute-start.13 = (bf16[5,128,128]{2,1,0:T(8,128)(2,1)S(1)}, bf16[5,128,128]{2,1,0:T(8,128)(2,1)S(1)}, u32[]{:S(2)}, u32[]{:S(2)}) collective-permute-start(bf16[5,128,128]{2,1,0:T(8,128)(2,1)S(1)} %get-tuple-element.82), channel_id=1, source_target_pairs={{0,2},{2,0},{1,3},{3,1},{4,6},{6,4},{5,7},{7,5},{8,10},{10,8},{9,1... | collective-permute-start | bytes 491528 | tf_op jit(solution)/shard_map/ppermute | solution.py:568
  38.7 3.8 %collective-permute-start.12 = (f32[248,128]{1,0:T(8,128)S(1)}, f32[248,128]{1,0:T(8,128)S(1)}, u32[]{:S(2)}, u32[]{:S(2)}) collective-permute-start(f32[248,128]{1,0:T(8,128)S(1)} %multiply_add_fusion.here_ref), channel_id=1, source_target_pairs={{0,2},{2,0},{1,3},{3,1},{4,6},{6,4},{5,7},{7,5},{8,10},{10,8},{9,1... | collective-permute-start | bytes 380936 | tf_op jit(solution)/shard_map/ppermute | solution.py:577
  40.1 4.8 %collective-permute-start.15 = (f32[248,128]{1,0:T(8,128)S(1)}, f32[248,128]{1,0:T(8,128)S(1)}, u32[]{:S(2)}, u32[]{:S(2)}) collective-permute-start(f32[248,128]{1,0:T(8,128)S(1)} %multiply_add_fusion.here_ref), channel_id=1, source_target_pairs={{0,1},{1,0},{2,3},{3,2},{4,5},{5,4},{6,7},{7,6},{8,9},{9,8},{10,11... | collective-permute-start | bytes 380936 | tf_op jit(solution)/shard_map/ppermute | solution.py:578
  42.5 3.3 %collective-permute-start.14 = (f32[248,128]{1,0:T(8,128)S(1)}, f32[248,128]{1,0:T(8,128)S(1)}, u32[]{:S(2)}, u32[]{:S(2)}) collective-permute-start(f32[248,128]{1,0:T(8,128)S(1)} %collective-permute-done.12.here_ref), channel_id=1, source_target_pairs={{0,1},{1,0},{2,3},{3,2},{4,5},{5,4},{6,7},{7,6},{8,9},{9,8},{10,11... | collective-permute-start | bytes 380936 | tf_op jit(solution)/shard_map/ppermute | solution.py:585

commit v8 on v7

--- a/solution.py
+++ b/solution.py
@@ -716,8 +716,7 @@
 
         value_taps, gate_taps = weights(0), weights(pitch)
 
-        @pl.loop(low, high)
-        def _(at):
+        def conv_row(at):
             cache = {}
 
             def read(ref, a, col):
@@ -741,6 +740,13 @@
                 place = pl.ds(grad_at(at - 1, start_col + col - 1), TILES)
                 value_grad[place, :] = glu * gated
                 gate_grad[place, :] = glu * value * (squash + gated * (1.0 - squash))
+
+        steps = 3 if lax.axis_size("height") == 2 and (rows + 1) % 3 == 0 else 1
+
+        @pl.loop(0, (rows + 1) // 3 if steps == 3 else high - low)
+        def _(trip):
+            for step in range(steps):
+                conv_row(low + trip * steps + step)
 
         def gather(at, results):
             cache = {}

time: 47.8 us -> 47.8 us (level)
  no operation moved by 1% of the time
where the time goes in v8:
time: 47.8 us; the launch traced here: 47.4 us
  starting transfers between devices  23 us (48%)
  Pallas kernels  15.6 us (33%)
  waiting for transfers between devices  6.52 us (14%)
  local copies, waits for them, and re-layouts  1.28 us (3%)
  between operations  0.83 us (2%)
    ppermute x4, starting transfers between devices, along_frames(): sent = {hop: lax.ppermute(own, 'tm', moves[hop - 1]) for hop in hops}  8.86 us
    pallas_call x1, Pallas kernels, ffn(): pl.pallas_call(functools.partial(conv_kernel, len(halo_rows)), out_shape=...  6.24 us
    ppermute x4, waiting for transfers between devices, along_frames(): sent = {hop: lax.ppermute(own, 'tm', moves[hop - 1]) for hop in hops}  4.02 us
    ppermute x1, starting transfers between devices, paired(): came = lax.ppermute(state, 'width', SWAP)  2.98 us
    ppermute x1, starting transfers between devices, paired(): far_came = lax.ppermute(far, 'width', SWAP)  2.33 us
    pallas_call x1, Pallas kernels, paired(): vmem_call(state_kernel, (pair, pair), [pltpu.VMEM((2, 2, half, LANES), jn...  2.12 us
    ppermute x1, starting transfers between devices, convolve(): back_came = lax.ppermute(other, 'height', SWAP)  1.74 us
    pallas_call x1, Pallas kernels, paired(): vmem_call(query_kernel, (share, share, back, back), [pltpu.VMEM((2, half,...  1.73 us
  transfers between devices with their start and end apart: 16, of which 8 were waited for; matrix products, arithmetic and copies ran while one was open for 3% of the time, Pallas kernels for 25%

profile of v8, /device:TPU:9, one launch (start us, length us, event | category | flops | bytes accessed | tf_op | source)
XLA Modules:
  0.0 47.4 jit_solution(7983045270899954389)
XLA Ops:
  0.6 2.1 %shard_map.102 = (f32[2,280,128]{2,1,0:T(8,128)S(1)}, f32[2,280,128]{2,1,0:T(8,128)S(1)}) custom-call(bf16[128,1120]{1,0:T(8,128)(2,1)} %bitcast.22, bf16[128,1120]{1,0:T(8,128)(2,1)} %bitcast.25), custom_call_target="tpu_custom_call" | custom-call | flops 36700160 | bytes 1146880 | tf_op jit(solution)/shard_map/pallas_call | solution.py:515
  2.8 0.7 %collective-permute-start = (f32[2,280,128]{2,1,0:T(8,128)S(1)}, f32[2,280,128]{2,1,0:T(8,128)S(1)}, u32[]{:S(2)}, u32[]{:S(2)}) collective-permute-start(f32[2,280,128]{2,1,0:T(8,128)S(1)} %get-tuple-element.50), channel_id=1, source_target_pairs={{0,1},{1,0},{2,3},{3,2},{4,5},{5,4},{6,7},{7,6},{8,9},{9,8},{10,11... | collective-permute-start | bytes 860168 | tf_op jit(solution)/shard_map/ppermute | solution.py:521
  3.5 1.0 %dynamic-slice_bitcast_fusion = bf16[2,16,5632]{2,1,0:T(8,128)(2,1)S(1)} fusion(bf16[1,8,16,5632]{3,2,1,0:T(8,128)(2,1)} %param.12, s32[]{:T(128)S(6)} %select_n.11), kind=kLoop, calls=%fused_computation | loop fusion | bytes 720900 | tf_op jit(solution)/shard_map/dynamic_slice | solution.py:793
  4.7 0.2 shard_map.103
  4.9 1.3 %collective-permute-start.1 = (f32[248,128]{1,0:T(8,128)S(1)}, f32[248,128]{1,0:T(8,128)S(1)}, u32[]{:S(2)}, u32[]{:S(2)}) collective-permute-start(f32[248,128]{1,0:T(8,128)S(1)} %get-tuple-element.57), channel_id=1, source_target_pairs={{0,2},{2,0},{1,3},{3,1},{4,6},{6,4},{5,7},{7,5},{8,10},{10,8},{9,1... | collective-permute-start | bytes 380936 | tf_op jit(solution)/shard_map/ppermute | solution.py:524
  6.2 1.7 %shard_map.104 = (bf16[2,5,128,128]{3,2,1,0:T(8,128)(2,1)S(1)}, bf16[2,5,128,128]{3,2,1,0:T(8,128)(2,1)S(1)}, f32[8,128]{1,0:T(8,128)S(1)}) custom-call(bf16[128,1120]{1,0:T(8,128)(2,1)} %bitcast.29, bf16[128,1120]{1,0:T(8,128)(2,1)} %bitcast.30, s32[4]{0:T(128)} %clip_hbm.1), custom_call_target="tpu_custom_call" | custom-call | bytes 1720320 | tf_op jit(solution)/shard_map/pallas_call | solution.py:528
  7.9 0.3 collective-permute-start.4
  8.2 1.2 %collective-permute-start.7 = (bf16[2,16,5632]{2,1,0:T(8,128)(2,1)S(1)}, bf16[2,16,5632]{2,1,0:T(8,128)(2,1)S(1)}, u32[]{:S(2)}, u32[]{:S(2)}) collective-permute-start(bf16[2,16,5632]{2,1,0:T(8,128)(2,1)S(1)} %dynamic-slice_bitcast_fusion), channel_id=1, source_target_pairs={{0,2},{2,0},{1,3},{3,1},{4,6},{6,4},{5,7},{7,5},{8,10},{10,8},{9,1... | collective-permute-start | bytes 1081352 | tf_op jit(solution)/shard_map/ppermute | solution.py:813
  9.7 3.2 %collective-permute-start.2 = (f32[248,128]{1,0:T(8,128)S(1)}, f32[248,128]{1,0:T(8,128)S(1)}, u32[]{:S(2)}, u32[]{:S(2)}) collective-permute-start(f32[248,128]{1,0:T(8,128)S(1)} %add.21), channel_id=1, source_target_pairs={{0,4},{4,8},{8,12},{1,5},{5,9},{9,13},{2,6},{6,10},{10,14},{3,7},{... | collective-permute-start | bytes 380936 | tf_op jit(solution)/shard_map/ppermute | solution.py:544
  12.9 2.3 %collective-permute-start.3 = (f32[248,128]{1,0:T(8,128)S(1)}, f32[248,128]{1,0:T(8,128)S(1)}, u32[]{:S(2)}, u32[]{:S(2)}) collective-permute-start(f32[248,128]{1,0:T(8,128)S(1)} %add.21), channel_id=1, source_target_pairs={{0,8},{4,12},{1,9},{5,13},{2,10},{6,14},{3,11},{7,15},{16,24},{20,... | collective-permute-start | bytes 380936 | tf_op jit(solution)/shard_map/ppermute | solution.py:544
  15.2 0.5 %shard_map.105 = (f32[3,2,1920,128]{3,2,1,0:T(8,128)S(1)}, f32[432,128]{1,0:T(8,128)S(1)}) custom-call(bf16[8,16,5632]{2,1,0:T(8,128)(2,1)S(1)} %bitcast.21, f32[9,5632]{1,0:T(8,128)S(1)} %copy-done.3), custom_call_target="tpu_custom_call" | custom-call | flops 720896 | bytes 720896 | tf_op jit(solution)/shard_map/pallas_call | solution.py:823
  15.8 3.6 %collective-permute-done.3 = f32[248,128]{1,0:T(8,128)S(1)} collective-permute-done((f32[248,128]{1,0:T(8,128)S(1)}, f32[248,128]{1,0:T(8,128)S(1)}, u32[]{:S(2)}, u32[]{:S(2)}) %collective-permute-start.3) | collective-permute-done | bytes 127008 | tf_op jit(solution)/shard_map/ppermute | solution.py:544
  19.4 3.0 %collective-permute-start.5 = (f32[248,128]{1,0:T(8,128)S(1)}, f32[248,128]{1,0:T(8,128)S(1)}, u32[]{:S(2)}, u32[]{:S(2)}) collective-permute-start(f32[248,128]{1,0:T(8,128)S(1)} %multiply_add_fusion.1.state_ref), channel_id=1, source_target_pairs={{0,1},{1,0},{2,3},{3,2},{4,5},{5,4},{6,7},{7,6},{8,9},{9,8},{10,11... | collective-permute-start | bytes 380936 | tf_op jit(solution)/shard_map/ppermute | solution.py:556
  22.4 0.9 %collective-permute-done.5.came_ref = f32[248,128]{1,0:T(8,128)S(1)} collective-permute-done((f32[248,128]{1,0:T(8,128)S(1)}, f32[248,128]{1,0:T(8,128)S(1)}, u32[]{:S(2)}, u32[]{:S(2)}) %collective-permute-start.5) | collective-permute-done | bytes 127008 | tf_op jit(solution)/shard_map/ppermute | solution.py:556
  23.3 1.7 %shard_map.106 = (f32[248,128]{1,0:T(8,128)S(1)}, f32[248,128]{1,0:T(8,128)S(1)}, bf16[5,128,128]{2,1,0:T(8,128)(2,1)S(1)}, bf16[5,128,128]{2,1,0:T(8,128)(2,1)S(1)}) custom-call(f32[248,128]{1,0:T(8,128)S(1)} %multiply_add_fusion.1.state_ref, f32[248,128]{1,0:T(8,128)S(1)} %collective-permute-done.5.came_ref, ...), custom_call_target="tpu_custom_call" | custom-call | flops 256901120 | bytes 1146880 | tf_op jit(solution)/shard_map/pallas_call | solution.py:558
  25.1 0.4 collective-permute-start.6
  25.5 0.4 collective-permute-start.9
  25.9 0.5 %collective-permute-done.6 = f32[248,128]{1,0:T(8,128)S(1)} collective-permute-done((f32[248,128]{1,0:T(8,128)S(1)}, f32[248,128]{1,0:T(8,128)S(1)}, u32[]{:S(2)}, u32[]{:S(2)}) %collective-permute-start.6) | collective-permute-done | bytes 127008 | tf_op jit(solution)/shard_map/ppermute | solution.py:563
  26.5 0.3 collective-permute-done.9.refs_2_
  26.8 1.3 %collective-permute-start.10 = (f32[248,128]{1,0:T(8,128)S(1)}, f32[248,128]{1,0:T(8,128)S(1)}, u32[]{:S(2)}, u32[]{:S(2)}) collective-permute-start(f32[248,128]{1,0:T(8,128)S(1)} %add.24), channel_id=1, source_target_pairs={{8,0},{12,4},{9,1},{13,5},{10,2},{14,6},{11,3},{15,7},{24,16},{28,... | collective-permute-start | bytes 380936 | tf_op jit(solution)/shard_map/ppermute | solution.py:544
  28.1 2.1 %collective-permute-start.11 = (f32[248,128]{1,0:T(8,128)S(1)}, f32[248,128]{1,0:T(8,128)S(1)}, u32[]{:S(2)}, u32[]{:S(2)}) collective-permute-start(f32[248,128]{1,0:T(8,128)S(1)} %add.24), channel_id=1, source_target_pairs={{4,0},{8,4},{12,8},{5,1},{9,5},{13,9},{6,2},{10,6},{14,10},{7,3},{... | collective-permute-start | bytes 380936 | tf_op jit(solution)/shard_map/ppermute | solution.py:544
  30.2 1.7 %collective-permute-start.13 = (bf16[5,128,128]{2,1,0:T(8,128)(2,1)S(1)}, bf16[5,128,128]{2,1,0:T(8,128)(2,1)S(1)}, u32[]{:S(2)}, u32[]{:S(2)}) collective-permute-start(bf16[5,128,128]{2,1,0:T(8,128)(2,1)S(1)} %get-tuple-element.82), channel_id=1, source_target_pairs={{0,2},{2,0},{1,3},{3,1},{4,6},{6,4},{5,7},{7,5},{8,10},{10,8},{9,1... | collective-permute-start | bytes 491528 | tf_op jit(solution)/shard_map/ppermute | solution.py:568
  32.0 6.2 %shard_map.107 = (bf16[8,16,5632]{2,1,0:T(8,128)(2,1)}, f32[3,2,1920,128]{3,2,1,0:T(8,128)S(1)}) custom-call(bf16[2,16,5632]{2,1,0:T(8,128)(2,1)S(1)} %collective-permute-done.7.refs_0_, bf16[8,2,5632]{2,1,0:T(2,128)(2,1)S(1)} %collective-permute-done.8.refs_1_, ...), custom_call_target="tpu_custom_call", output_to_operand_aliasing={{1}: (3, {})} | custom-call | flops 1441792 | bytes 720896 | tf_op jit(solution)/shard_map/pallas_call | solution.py:839
  38.2 0.5 collective-permute-done.11
  38.7 1.4 %collective-permute-start.12 = (f32[248,128]{1,0:T(8,128)S(1)}, f32[248,128]{1,0:T(8,128)S(1)}, u32[]{:S(2)}, u32[]{:S(2)}) collective-permute-start(f32[248,128]{1,0:T(8,128)S(1)} %multiply_add_fusion.here_ref), channel_id=1, source_target_pairs={{0,2},{2,0},{1,3},{3,1},{4,6},{6,4},{5,7},{7,5},{8,10},{10,8},{9,1... | collective-permute-start | bytes 380936 | tf_op jit(solution)/shard_map/ppermute | solution.py:577
  40.1 1.3 %collective-permute-start.15 = (f32[248,128]{1,0:T(8,128)S(1)}, f32[248,128]{1,0:T(8,128)S(1)}, u32[]{:S(2)}, u32[]{:S(2)}) collective-permute-start(f32[248,128]{1,0:T(8,128)S(1)} %multiply_add_fusion.here_ref), channel_id=1, source_target_pairs={{0,1},{1,0},{2,3},{3,2},{4,5},{5,4},{6,7},{7,6},{8,9},{9,8},{10,11... | collective-permute-start | bytes 380936 | tf_op jit(solution)/shard_map/ppermute | solution.py:578
  41.4 0.9 %shard_map.108 = bf16[128,1120]{1,0:T(8,128)(2,1)} custom-call(bf16[5,128,128]{2,1,0:T(8,128)(2,1)S(1)} %get-tuple-element.80.mine_ref, bf16[5,128,128]{2,1,0:T(8,128)(2,1)S(1)} %collective-permute-done.13.came_ref), custom_call_target="tpu_custom_call" | custom-call | bytes 573440 | tf_op jit(solution)/shard_map/pallas_call | solution.py:570
  42.3 0.3 collective-permute-done.12.here_ref
  42.5 2.3 %collective-permute-start.14 = (f32[248,128]{1,0:T(8,128)S(1)}, f32[248,128]{1,0:T(8,128)S(1)}, u32[]{:S(2)}, u32[]{:S(2)}) collective-permute-start(f32[248,128]{1,0:T(8,128)S(1)} %collective-permute-done.12.here_ref), channel_id=1, source_target_pairs={{0,1},{1,0},{2,3},{3,2},{4,5},{5,4},{6,7},{7,6},{8,9},{9,8},{10,11... | collective-permute-start | bytes 380936 | tf_op jit(solution)/shard_map/ppermute | solution.py:585
  44.9 0.7 %shard_map.109 = (bf16[5,128,128]{2,1,0:T(8,128)(2,1)S(1)}, bf16[5,128,128]{2,1,0:T(8,128)(2,1)S(1)}) custom-call(bf16[128,1120]{1,0:T(8,128)(2,1)S(1)} %bitcast.23, bf16[128,1120]{1,0:T(8,128)(2,1)S(1)} %bitcast.26, f32[248,128]{1,0:T(8,128)S(1)} %multiply_add_fusion.here_ref, f32[248,128]{1,0:T(8,128)S(1)} %collective-permute-done.15.came_ref), custom_call_target="tpu_custom_call" | custom-call | flops 73400320 | bytes 573440 | tf_op jit(solution)/shard_map/pallas_call | solution.py:581
  45.6 0.3 collective-permute-done.14.came_ref
  45.9 1.5 %shard_map.110 = (bf16[128,1120]{1,0:T(8,128)(2,1)}, bf16[128,1120]{1,0:T(8,128)(2,1)}) custom-call(bf16[128,1120]{1,0:T(8,128)(2,1)S(1)} %bitcast.24, bf16[128,1120]{1,0:T(8,128)(2,1)S(1)} %bitcast.27, f32[248,128]{1,0:T(8,128)S(1)} %collective-permute-done.12.here_ref, f32[248,128]{1,0:T(8,128)S(1)} %collective-permute-done.14.came_ref, ...), custom_call_target="tpu_custom_call" | custom-call | flops 73400320 | bytes 573440 | tf_op jit(solution)/shard_map/pallas_call | solution.py:587
  (25 shorter events, 0.7 us)
Async XLA Ops:
  0.6 8.8 %copy-start = (bf16[1,8,16,5632]{3,2,1,0:T(8,128)(2,1)S(1)}, bf16[1,8,16,5632]{3,2,1,0:T(8,128)(2,1)}, u32[]{:S(2)}) copy-start(bf16[1,8,16,5632]{3,2,1,0:T(8,128)(2,1)} %param.12) | copy-start | bytes 4325380
  2.8 12.4 %copy-start.3 = (f32[9,5632]{1,0:T(8,128)S(1)}, f32[9,5632]{1,0:T(8,128)}, u32[]{:S(2)}) copy-start(f32[9,5632]{1,0:T(8,128)} %weight_ref.1) | copy-start | bytes 608260
  2.8 1.9 %collective-permute-start = (f32[2,280,128]{2,1,0:T(8,128)S(1)}, f32[2,280,128]{2,1,0:T(8,128)S(1)}, u32[]{:S(2)}, u32[]{:S(2)}) collective-permute-start(f32[2,280,128]{2,1,0:T(8,128)S(1)} %get-tuple-element.50), channel_id=1, source_target_pairs={{0,1},{1,0},{2,3},{3,2},{4,5},{5,4},{6,7},{7,6},{8,9},{9,8},{10,11... | collective-permute-start | bytes 860168 | tf_op jit(solution)/shard_map/ppermute | solution.py:521
  4.9 4.7 %collective-permute-start.1 = (f32[248,128]{1,0:T(8,128)S(1)}, f32[248,128]{1,0:T(8,128)S(1)}, u32[]{:S(2)}, u32[]{:S(2)}) collective-permute-start(f32[248,128]{1,0:T(8,128)S(1)} %get-tuple-element.57), channel_id=1, source_target_pairs={{0,2},{2,0},{1,3},{3,1},{4,6},{6,4},{5,7},{7,5},{8,10},{10,8},{9,1... | collective-permute-start | bytes 380936 | tf_op jit(solution)/shard_map/ppermute | solution.py:524
  7.9 11.4 %collective-permute-start.4 = (bf16[2,5,128,128]{3,2,1,0:T(8,128)(2,1)S(1)}, bf16[2,5,128,128]{3,2,1,0:T(8,128)(2,1)S(1)}, u32[]{:S(2)}, u32[]{:S(2)}) collective-permute-start(bf16[2,5,128,128]{3,2,1,0:T(8,128)(2,1)S(1)} %get-tuple-element.55), channel_id=1, source_target_pairs={{0,2},{2,0},{1,3},{3,1},{4,6},{6,4},{5,7},{7,5},{8,10},{10,8},{9,1... | collective-permute-start | bytes 983048 | tf_op jit(solution)/shard_map/ppermute | solution.py:539
  8.2 17.2 %collective-permute-start.7 = (bf16[2,16,5632]{2,1,0:T(8,128)(2,1)S(1)}, bf16[2,16,5632]{2,1,0:T(8,128)(2,1)S(1)}, u32[]{:S(2)}, u32[]{:S(2)}) collective-permute-start(bf16[2,16,5632]{2,1,0:T(8,128)(2,1)S(1)} %dynamic-slice_bitcast_fusion), channel_id=1, source_target_pairs={{0,2},{2,0},{1,3},{3,1},{4,6},{6,4},{5,7},{7,5},{8,10},{10,8},{9,1... | collective-permute-start | bytes 1081352 | tf_op jit(solution)/shard_map/ppermute | solution.py:813
  9.7 6.1 %collective-permute-start.2 = (f32[248,128]{1,0:T(8,128)S(1)}, f32[248,128]{1,0:T(8,128)S(1)}, u32[]{:S(2)}, u32[]{:S(2)}) collective-permute-start(f32[248,128]{1,0:T(8,128)S(1)} %add.21), channel_id=1, source_target_pairs={{0,4},{4,8},{8,12},{1,5},{5,9},{9,13},{2,6},{6,10},{10,14},{3,7},{... | collective-permute-start | bytes 380936 | tf_op jit(solution)/shard_map/ppermute | solution.py:544
  12.9 6.4 %collective-permute-start.3 = (f32[248,128]{1,0:T(8,128)S(1)}, f32[248,128]{1,0:T(8,128)S(1)}, u32[]{:S(2)}, u32[]{:S(2)}) collective-permute-start(f32[248,128]{1,0:T(8,128)S(1)} %add.21), channel_id=1, source_target_pairs={{0,8},{4,12},{1,9},{5,13},{2,10},{6,14},{3,11},{7,15},{16,24},{20,... | collective-permute-start | bytes 380936 | tf_op jit(solution)/shard_map/ppermute | solution.py:544
  19.4 4.0 %collective-permute-start.5 = (f32[248,128]{1,0:T(8,128)S(1)}, f32[248,128]{1,0:T(8,128)S(1)}, u32[]{:S(2)}, u32[]{:S(2)}) collective-permute-start(f32[248,128]{1,0:T(8,128)S(1)} %multiply_add_fusion.1.state_ref), channel_id=1, source_target_pairs={{0,1},{1,0},{2,3},{3,2},{4,5},{5,4},{6,7},{7,6},{8,9},{9,8},{10,11... | collective-permute-start | bytes 380936 | tf_op jit(solution)/shard_map/ppermute | solution.py:556
  22.3 4.1 %collective-permute-start.8 = (bf16[8,2,5632]{2,1,0:T(2,128)(2,1)S(1)}, bf16[8,2,5632]{2,1,0:T(2,128)(2,1)S(1)}, u32[]{:S(2)}, u32[]{:S(2)}) collective-permute-start(bf16[8,2,5632]{2,1,0:T(2,128)(2,1)S(1)} %dynamic-slice_bitcast_fusion.1), channel_id=1, source_target_pairs={{0,1},{1,0},{2,3},{3,2},{4,5},{5,4},{6,7},{7,6},{8,9},{9,8},{10,11... | collective-permute-start | bytes 540680 | tf_op jit(solution)/shard_map/ppermute | solution.py:814
  25.1 1.4 %collective-permute-start.6 = (f32[248,128]{1,0:T(8,128)S(1)}, f32[248,128]{1,0:T(8,128)S(1)}, u32[]{:S(2)}, u32[]{:S(2)}) collective-permute-start(f32[248,128]{1,0:T(8,128)S(1)} %get-tuple-element.68), channel_id=1, source_target_pairs={{0,1},{1,0},{2,3},{3,2},{4,5},{5,4},{6,7},{7,6},{8,9},{9,8},{10,11... | collective-permute-start | bytes 380936 | tf_op jit(solution)/shard_map/ppermute | solution.py:563
  25.5 1.3 %collective-permute-start.9 = (bf16[2,2,5632]{2,1,0:T(2,128)(2,1)S(1)}, bf16[2,2,5632]{2,1,0:T(2,128)(2,1)S(1)}, u32[]{:S(2)}, u32[]{:S(2)}) collective-permute-start(bf16[2,2,5632]{2,1,0:T(2,128)(2,1)S(1)} %constant_dynamic-slice_fusion), channel_id=1, source_target_pairs={{0,1},{1,0},{2,3},{3,2},{4,5},{5,4},{6,7},{7,6},{8,9},{9,8},{10,11... | collective-permute-start | bytes 135176 | tf_op jit(solution)/shard_map/ppermute | solution.py:815
  26.8 11.4 %collective-permute-start.10 = (f32[248,128]{1,0:T(8,128)S(1)}, f32[248,128]{1,0:T(8,128)S(1)}, u32[]{:S(2)}, u32[]{:S(2)}) collective-permute-start(f32[248,128]{1,0:T(8,128)S(1)} %add.24), channel_id=1, source_target_pairs={{8,0},{12,4},{9,1},{13,5},{10,2},{14,6},{11,3},{15,7},{24,16},{28,... | collective-permute-start | bytes 380936 | tf_op jit(solution)/shard_map/ppermute | solution.py:544
  28.1 10.6 %collective-permute-start.11 = (f32[248,128]{1,0:T(8,128)S(1)}, f32[248,128]{1,0:T(8,128)S(1)}, u32[]{:S(2)}, u32[]{:S(2)}) collective-permute-start(f32[248,128]{1,0:T(8,128)S(1)} %add.24), channel_id=1, source_target_pairs={{4,0},{8,4},{12,8},{5,1},{9,5},{13,9},{6,2},{10,6},{14,10},{7,3},{... | collective-permute-start | bytes 380936 | tf_op jit(solution)/shard_map/ppermute | solution.py:544
  30.2 14.7 %copy-start.1 = (bf16[1,8,16,1120]{3,2,1,0:T(8,128)(2,1)S(1)}, bf16[1,8,16,1120]{3,2,1,0:T(8,128)(2,1)}, u32[]{:S(2)}) copy-start(bf16[1,8,16,1120]{3,2,1,0:T(8,128)(2,1)} %param.8) | copy-start | bytes 860164
  30.2 14.7 %copy-start.2 = (bf16[1,8,16,1120]{3,2,1,0:T(8,128)(2,1)S(1)}, bf16[1,8,16,1120]{3,2,1,0:T(8,128)(2,1)}, u32[]{:S(2)}) copy-start(bf16[1,8,16,1120]{3,2,1,0:T(8,128)(2,1)} %param.9) | copy-start | bytes 860164
  30.2 11.1 %collective-permute-start.13 = (bf16[5,128,128]{2,1,0:T(8,128)(2,1)S(1)}, bf16[5,128,128]{2,1,0:T(8,128)(2,1)S(1)}, u32[]{:S(2)}, u32[]{:S(2)}) collective-permute-start(bf16[5,128,128]{2,1,0:T(8,128)(2,1)S(1)} %get-tuple-element.82), channel_id=1, source_target_pairs={{0,2},{2,0},{1,3},{3,1},{4,6},{6,4},{5,7},{7,5},{8,10},{10,8},{9,1... | collective-permute-start | bytes 491528 | tf_op jit(solution)/shard_map/ppermute | solution.py:568
  38.7 3.8 %collective-permute-start.12 = (f32[248,128]{1,0:T(8,128)S(1)}, f32[248,128]{1,0:T(8,128)S(1)}, u32[]{:S(2)}, u32[]{:S(2)}) collective-permute-start(f32[248,128]{1,0:T(8,128)S(1)} %multiply_add_fusion.here_ref), channel_id=1, source_target_pairs={{0,2},{2,0},{1,3},{3,1},{4,6},{6,4},{5,7},{7,5},{8,10},{10,8},{9,1... | collective-permute-start | bytes 380936 | tf_op jit(solution)/shard_map/ppermute | solution.py:577
  40.1 4.8 %collective-permute-start.15 = (f32[248,128]{1,0:T(8,128)S(1)}, f32[248,128]{1,0:T(8,128)S(1)}, u32[]{:S(2)}, u32[]{:S(2)}) collective-permute-start(f32[248,128]{1,0:T(8,128)S(1)} %multiply_add_fusion.here_ref), channel_id=1, source_target_pairs={{0,1},{1,0},{2,3},{3,2},{4,5},{5,4},{6,7},{7,6},{8,9},{9,8},{10,11... | collective-permute-start | bytes 380936 | tf_op jit(solution)/shard_map/ppermute | solution.py:578
  42.5 3.3 %collective-permute-start.14 = (f32[248,128]{1,0:T(8,128)S(1)}, f32[248,128]{1,0:T(8,128)S(1)}, u32[]{:S(2)}, u32[]{:S(2)}) collective-permute-start(f32[248,128]{1,0:T(8,128)S(1)} %collective-permute-done.12.here_ref), channel_id=1, source_target_pairs={{0,1},{1,0},{2,3},{3,2},{4,5},{5,4},{6,7},{7,6},{8,9},{9,8},{10,11... | collective-permute-start | bytes 380936 | tf_op jit(solution)/shard_map/ppermute | solution.py:585
